TPU v7x, 32 devices: a whole 2x2x4 slice. The times are simulated.
32 devices in a mesh: dp: 16 (over z, y, core), tensor: 2 (over x).
Axes of the slice: x: 2, y: 2, z: 4, core: 2. Of those that a mesh axis runs over, the one named last changes fastest.
Arguments:
- tokens: bfloat16 [16384, 1024], P('dp'), may hold values from -6 to 6
- lengths: int32 [16], P('dp'), may hold values from 256 to 1024, as said below
- w_query: bfloat16 [1024, 1024], P(None, 'tensor'), may hold values from -0.1875 to 0.1875
- w_key: bfloat16 [1024, 1024], P(None, 'tensor'), may hold values from -0.1875 to 0.1875
- w_value: bfloat16 [1024, 1024], P(None, 'tensor'), may hold values from -0.1875 to 0.1875
- w_out: bfloat16 [1024, 1024], P('tensor'), may hold values from -0.1875 to 0.1875
- w_up: bfloat16 [1024, 4096], P(None, 'tensor'), may hold values from -0.1875 to 0.1875
- w_down: bfloat16 [4096, 1024], P('tensor'), may hold values from -0.09375 to 0.09375
- norm_gain: float32 [4, 1024], replicated, may hold values from 0.1 to 1.9
- norm_bias: float32 [4, 1024], replicated, may hold values from -1.5 to 1.5
- cotangent: bfloat16 [16384, 1024], P('dp'), may hold values from -6 to 6
Outputs:
- result: bfloat16 [16384, 1024], P('dp')
- input_grad: bfloat16 [16384, 1024], P('dp')
- grad_query: float32 [1024, 1024], P('dp', 'tensor')
- grad_key: float32 [1024, 1024], P('dp', 'tensor')
- grad_value: float32 [1024, 1024], P('dp', 'tensor')
- grad_out: float32 [1024, 1024], P('tensor', 'dp')
- grad_up: float32 [1024, 4096], P('dp', 'tensor')
- grad_down: float32 [4096, 1024], P('tensor', 'dp')
- grad_gain: float32 [4, 1024], P(None, 'dp')
- grad_bias: float32 [4, 1024], P(None, 'dp')
Inputs may be any that keep to these rules, and one draw needn't show every extreme that they name: Each sequence's real tokens fill its first lengths[s] slots of 1024; some sequence is full and some has 256.
All inputs are finite; a program needn't handle non-finite values.
Results may differ from a plain program's by a relative error of at most 0.018.
Values may be sent and summed in bfloat16 or wider, within the bound.
A program may use at most 192 MiB of HBM per device.

v0:
```python
import jax
import jax.numpy as jnp
from jax import lax
from jax.sharding import PartitionSpec as P

HD = 64


epsilon = 1e-05
relax_scale = 0.125


def layer_norm(values, gain_vec, bias_vec):
    average = jnp.mean(values, axis=-1, keepdims=True)
    centered = values - average
    variance = jnp.mean(centered * centered, axis=-1, keepdims=True)
    return centered * lax.rsqrt(variance + epsilon) * gain_vec + bias_vec


def norm_back(values, gain_vec, bias_vec, grad_output):
    unused, pull = jax.vjp(layer_norm, values, gain_vec, bias_vec)
    return pull(grad_output)


def split_heads(matrix):
    return matrix.reshape(matrix.shape[0], -1, HD)


def masked_scores(query_block, key_heads, key_valid):
    scores = (
        jnp.einsum("qhd,khd->hqk", query_block, key_heads, preferred_element_type=jnp.float32)
        * relax_scale
    )
    return jnp.where(key_valid[None, None, :], scores, -1000000000.0)


def block_size():
    return 512


def attention_forward(queries, key_rows, value_rows, valid_mask):
    seq_count, seq_len = valid_mask.shape
    block_rows = block_size()
    outputs = []
    log_totals = []
    key_heads = split_heads(key_rows)
    value_heads = split_heads(value_rows)
    for block_index in range(seq_len // block_rows):
        row_start = block_index * block_rows
        query_block = split_heads(queries[row_start : row_start + block_rows])
        scores = masked_scores(query_block, key_heads, valid_mask[0])
        maxima = jnp.max(scores, axis=-1, keepdims=True)
        exponent = jnp.exp(scores - maxima)
        sums_soft = jnp.sum(exponent, axis=-1, keepdims=True)
        soft_weights = (exponent / sums_soft).astype(jnp.bfloat16)
        mixture = jnp.einsum(
            "hqk,khd->qhd", soft_weights, value_heads, preferred_element_type=jnp.float32
        )
        outputs.append(mixture.reshape(block_rows, -1).astype(jnp.bfloat16))
        log_totals.append(maxima + jnp.log(sums_soft))
    return (jnp.concatenate(outputs, axis=0), log_totals)


def attention_backward(queries, key_rows, value_rows, grad_attended, log_totals, valid_mask):
    seq_count, seq_len = valid_mask.shape
    block_rows = block_size()
    query_grads = []
    counter = 0
    key_heads = split_heads(key_rows)
    value_heads = split_heads(value_rows)
    key_sum = jnp.zeros(key_heads.shape, jnp.float32)
    value_sum = jnp.zeros(value_heads.shape, jnp.float32)
    for block_index in range(seq_len // block_rows):
        row_start = block_index * block_rows
        query_block = split_heads(queries[row_start : row_start + block_rows])
        grad_block = split_heads(grad_attended[row_start : row_start + block_rows])
        scores = masked_scores(query_block, key_heads, valid_mask[0])
        soft_weights = jnp.exp(scores - log_totals[counter])
        counter += 1
        grad_soft = jnp.einsum(
            "qhd,khd->hqk", grad_block, value_heads, preferred_element_type=jnp.float32
        )
        row_dots = jnp.sum(soft_weights * grad_soft, axis=-1, keepdims=True)
        grad_scores = (soft_weights * (grad_soft - row_dots)).astype(jnp.bfloat16)
        query_grad = (
            jnp.einsum("hqk,khd->qhd", grad_scores, key_heads, preferred_element_type=jnp.float32)
            * relax_scale
        )
        query_grads.append(query_grad.reshape(block_rows, -1).astype(jnp.bfloat16))
        key_sum = (
            key_sum
            + jnp.einsum(
                "hqk,qhd->khd", grad_scores, query_block, preferred_element_type=jnp.float32
            )
            * relax_scale
        )
        value_sum = value_sum + jnp.einsum(
            "hqk,qhd->khd",
            soft_weights.astype(jnp.bfloat16),
            grad_block,
            preferred_element_type=jnp.float32,
        )
    key_grads = key_sum.reshape(seq_len, -1).astype(jnp.bfloat16)
    value_grads = value_sum.reshape(seq_len, -1).astype(jnp.bfloat16)
    return (jnp.concatenate(query_grads, axis=0), key_grads, value_grads)


def on_device(
    tokens, lengths, w_query, w_key, w_value, w_out, w_up, w_down, norm_gain, norm_bias, cotangent
):
    row_count = tokens.shape[0]
    seq_count = lengths.shape[0]
    seq_len = row_count // seq_count
    inputs = tokens.astype(jnp.float32)
    positions = jnp.arange(seq_len, dtype=jnp.int32)
    valid_mask = positions[None, :] < lengths[:, None]
    row_valid = valid_mask.reshape(row_count, 1).astype(jnp.float32)
    normed_in = layer_norm(inputs, norm_gain[0], norm_bias[0]).astype(jnp.bfloat16)
    queries = jnp.dot(normed_in, w_query, preferred_element_type=jnp.float32).astype(jnp.bfloat16)
    key_rows = jnp.dot(normed_in, w_key, preferred_element_type=jnp.float32).astype(jnp.bfloat16)
    value_rows = jnp.dot(normed_in, w_value, preferred_element_type=jnp.float32).astype(
        jnp.bfloat16
    )
    attended, log_totals = attention_forward(queries, key_rows, value_rows, valid_mask)
    attn_total = lax.psum(
        jnp.dot(attended, w_out, preferred_element_type=jnp.float32).astype(jnp.bfloat16), "tensor"
    ).astype(jnp.float32)
    middle = inputs + layer_norm(attn_total, norm_gain[1], norm_bias[1])
    normed_mid = layer_norm(middle, norm_gain[2], norm_bias[2]).astype(jnp.bfloat16)
    up_proj = jnp.dot(normed_mid, w_up, preferred_element_type=jnp.float32)
    hidden = jax.nn.gelu(up_proj).astype(jnp.bfloat16)
    ffn_total = lax.psum(
        jnp.dot(hidden, w_down, preferred_element_type=jnp.float32).astype(jnp.bfloat16), "tensor"
    ).astype(jnp.float32)
    result = (middle + layer_norm(ffn_total, norm_gain[3], norm_bias[3])).astype(jnp.bfloat16)
    grad_output = cotangent.astype(jnp.float32) * row_valid
    grad_last = norm_back(ffn_total, norm_gain[3], norm_bias[3], grad_output)
    grad_ffn_low = grad_last[0].astype(jnp.bfloat16)
    grad_w_down = jnp.einsum("rf,rd->fd", hidden, grad_ffn_low, preferred_element_type=jnp.float32)
    grad_hidden = jnp.einsum("rd,fd->rf", grad_ffn_low, w_down, preferred_element_type=jnp.float32)
    unused, gelu_pull = jax.vjp(jax.nn.gelu, up_proj)
    grad_upper = gelu_pull(grad_hidden)[0].astype(jnp.bfloat16)
    grad_w_up = jnp.einsum("rd,rf->df", normed_mid, grad_upper, preferred_element_type=jnp.float32)
    mid_part = jnp.einsum("rf,df->rd", grad_upper, w_up, preferred_element_type=jnp.float32)
    grad_normed_mid = lax.psum(mid_part.astype(jnp.bfloat16), "tensor").astype(jnp.float32)
    grad_mid, gain_mid, bias_mid = norm_back(middle, norm_gain[2], norm_bias[2], grad_normed_mid)
    grad_middle = grad_output + grad_mid
    grad_attn, gain_post, bias_post = norm_back(attn_total, norm_gain[1], norm_bias[1], grad_middle)
    grad_attn_low = grad_attn.astype(jnp.bfloat16)
    gain_last = grad_last[1]
    bias_last = grad_last[2]
    grad_w_out = jnp.einsum(
        "rk,rd->kd", attended, grad_attn_low, preferred_element_type=jnp.float32
    )
    grad_attended = jnp.einsum(
        "rd,kd->rk", grad_attn_low, w_out, preferred_element_type=jnp.float32
    ).astype(jnp.bfloat16)
    grad_queries, grad_keys, grad_values = attention_backward(
        queries, key_rows, value_rows, grad_attended, log_totals, valid_mask
    )
    grad_w_query = jnp.einsum(
        "rd,re->de", normed_in, grad_queries, preferred_element_type=jnp.float32
    )
    grad_w_key = jnp.einsum("rd,re->de", normed_in, grad_keys, preferred_element_type=jnp.float32)
    grad_w_value = jnp.einsum(
        "rd,re->de", normed_in, grad_values, preferred_element_type=jnp.float32
    )
    in_part = jnp.einsum("re,de->rd", grad_queries, w_query, preferred_element_type=jnp.float32)
    in_part = in_part + jnp.einsum(
        "re,de->rd", grad_keys, w_key, preferred_element_type=jnp.float32
    )
    in_part = in_part + jnp.einsum(
        "re,de->rd", grad_values, w_value, preferred_element_type=jnp.float32
    )
    grad_normed_in = lax.psum(in_part.astype(jnp.bfloat16), "tensor").astype(jnp.float32)
    grad_in, gain_in, bias_in = norm_back(inputs, norm_gain[0], norm_bias[0], grad_normed_in)
    input_grad = (grad_middle + grad_in).astype(jnp.bfloat16)
    gain_grads = jnp.stack([gain_in, gain_post, gain_mid, gain_last])
    bias_grads = jnp.stack([bias_in, bias_post, bias_mid, bias_last])
    summed = (
        lax.psum_scatter(grad_w_query, "dp", scatter_dimension=0, tiled=True),
        lax.psum_scatter(grad_w_key, "dp", scatter_dimension=0, tiled=True),
        lax.psum_scatter(grad_w_value, "dp", scatter_dimension=0, tiled=True),
        lax.psum_scatter(grad_w_out, "dp", scatter_dimension=1, tiled=True),
        lax.psum_scatter(grad_w_up, "dp", scatter_dimension=0, tiled=True),
        lax.psum_scatter(grad_w_down, "dp", scatter_dimension=1, tiled=True),
        lax.psum_scatter(gain_grads, "dp", scatter_dimension=1, tiled=True),
        lax.psum_scatter(bias_grads, "dp", scatter_dimension=1, tiled=True),
    )
    return (
        result,
        input_grad,
        summed[0],
        summed[1],
        summed[2],
        summed[3],
        summed[4],
        summed[5],
        summed[6],
        summed[7],
    )


def solution(mesh):
    in_specs = (
        P("dp", None),
        P("dp"),
        P(None, "tensor"),
        P(None, "tensor"),
        P(None, "tensor"),
        P("tensor", None),
        P(None, "tensor"),
        P("tensor", None),
        P(),
        P(),
        P("dp", None),
    )
    out_specs = (
        P("dp", None),
        P("dp", None),
        P("dp", "tensor"),
        P("dp", "tensor"),
        P("dp", "tensor"),
        P("tensor", "dp"),
        P("dp", "tensor"),
        P("tensor", "dp"),
        P(None, "dp"),
        P(None, "dp"),
    )
    return jax.shard_map(
        on_device, mesh=mesh, in_specs=in_specs, out_specs=out_specs, check_vma=False
    )
```

profile of v0, /device:TPU:0, one launch (start us, length us, event | category | flops | bytes accessed | tf_op | source)
XLA Modules:
  0.0 1082.1 jit_solution(6936342399880564148)
XLA Ops:
  21.6 8.7 fusion.90
  37.9 8.0 fusion
  56.0 65.7 %all-reduce.5.cloned.1.call-done = bf16[1024,1024]{1,0:T(8,128)(2,1)} async-done(((bf16[1024,1024]{1,0:T(8,128)(2,1)}), bf16[1024,1024]{1,0:T(8,128)(2,1)}) %all-reduce.5.cloned.1.call-update) | async-done | bytes 2097168 | tf_op jit(solution)/shard_map/psum | solution.py:125
  145.0 63.0 %all-reduce.7.cloned.1.call-done = bf16[1024,1024]{1,0:T(8,128)(2,1)} async-done(((bf16[1024,1024]{1,0:T(8,128)(2,1)}), bf16[1024,1024]{1,0:T(8,128)(2,1)}) %all-reduce.7.cloned.1.call-update) | async-done | bytes 2097168 | tf_op jit(solution)/shard_map/psum | solution.py:132
  218.2 12.4 %fusion.10 = bf16[1024,2048]{1,0:T(8,128)(2,1)S(1)} fusion(f32[1024,2048]{1,0:T(8,128)} %copy-done.87, bf16[2048,1024]{1,0:T(8,128)(2,1)S(1)} %copy-done.77, bf16[1024,1024]{1,0:T(8,128)(2,1)S(1)} %copy-done.10, bf16[1024,1024]{1,0:T(8,128)(2,1)S(1)} %copy-done.13, f32[1024]{0:T(1024)S(1)} %negate_multiply_fusion.3, f32[1024]{0:T(1024)S(1)} %get-tuple-element.42, ...), kind=kOutput, calls=%fused_computation.24 | convolution fusion | flops 4348444672 | bytes 20996096 | tf_op jit(solution)/shard_map/rd,fd->rf/dot_general | solution.py:140
  238.4 63.0 %all-reduce.9.cloned.1.call-done = bf16[1024,1024]{1,0:T(8,128)(2,1)} async-done(((bf16[1024,1024]{1,0:T(8,128)(2,1)}), bf16[1024,1024]{1,0:T(8,128)(2,1)}) %all-reduce.9.cloned.1.call-update) | async-done | bytes 2097168 | tf_op jit(solution)/shard_map/psum | solution.py:145
  306.7 6.7 fusion.54
  325.1 9.3 multiply_reduce_fusion.1
  334.4 15.7 %multiply_convert_fusion.1 = bf16[8,512,1024]{2,1,0:T(8,128)(2,1)} fusion(f32[8,512,1024]{2,1,0:T(8,128)} %get-tuple-element.51, f32[8,512,1024]{2,1,0:T(8,128)} %get-tuple-element.47, f32[8,512]{1,0:T(8,128)S(1)} %get-tuple-element.50, f32[8,512]{1,0:T(8,128)S(1)} %log_add_fusion.1), kind=kLoop, calls=%fused_computation.3 | loop fusion | flops 16777216 | bytes 41975808 | tf_op jit(solution)/shard_map/convert_element_type | solution.py:84
  350.1 6.9 fusion.62
  357.1 6.5 fusion.91
  368.0 9.9 multiply_reduce_fusion
  377.9 9.0 add_convert_fusion.5
  386.9 10.2 multiply_convert_fusion
  412.7 63.0 %all-reduce.11.cloned.1.call-done = bf16[1024,1024]{1,0:T(8,128)(2,1)} async-done(((bf16[1024,1024]{1,0:T(8,128)(2,1)}), bf16[1024,1024]{1,0:T(8,128)(2,1)}) %all-reduce.11.cloned.1.call-update) | async-done | bytes 2097168 | tf_op jit(solution)/shard_map/psum | solution.py:175
  502.9 13.9 %fusion.81 = f32[2048,1024]{0,1:T(8,128)} fusion(f32[1024,2048]{1,0:T(8,128)} %copy-done.87, bf16[1024,1024]{1,0:T(8,128)(2,1)} %all-reduce.7.cloned.1.call-done, bf16[1024,1024]{1,0:T(8,128)(2,1)} %param.21, f32[1024]{0:T(1024)S(1)} %copy-done.71, f32[1024]{0:T(1024)S(1)} %copy-done.61, f32[1024]{0:T(1024)S(1)} %copy-done.47, f32[1024]{0:T(1024)S(1)} %bitcast.149, ...), kind=kOutput, calls=%fused_computation.151 | convolution fusion | flops 4325376000 | bytes 20996096 | tf_op jit(solution)/shard_map/rf,rd->fd/dot_general | solution.py:139
  517.5 11.4 %fusion.79 = f32[1024,2048]{1,0:T(8,128)} fusion(bf16[1024,2048]{1,0:T(8,128)(2,1)} %copy-done.86, f32[1024]{0:T(1024)S(1)} %bitcast.163, f32[1024]{0:T(1024)S(1)} %bitcast.144, f32[1024]{0:T(1024)S(1)} %copy-done.55, f32[1024]{0:T(1024)S(1)} %copy-done.40, bf16[1024,1024]{1,0:T(8,128)(2,1)S(1)} %copy-done.5, ...), kind=kOutput, calls=%fused_computation.149 | convolution fusion | flops 4307550208 | bytes 16809984 | tf_op jit(solution)/shard_map/rd,rf->df/dot_general | solution.py:143
  540.0 57.3 %reduce-scatter.27.cloned.1.call-done = f32[64,4]{1,0:T(8,128)} async-done(((f32[1024,4]{1,0:T(8,128)}), f32[64,4]{1,0:T(8,128)}) %reduce-scatter.27.cloned.1.call-update) | async-done | bytes 1040
  598.7 63.6 %reduce-scatter.19.cloned.1.call-done = f32[512,64]{0,1:T(8,128)} async-done(((f32[512,1024]{0,1:T(8,128)}), f32[512,64]{0,1:T(8,128)}) %reduce-scatter.19.cloned.1.call-update) | async-done | bytes 131088 | tf_op jit(solution)/shard_map/reduce_scatter | solution.py:184
  662.3 65.3 %reduce-scatter.17.cloned.1.call-done = f32[64,512]{1,0:T(8,128)} async-done(((f32[1024,512]{1,0:T(8,128)}), f32[64,512]{1,0:T(8,128)}) %reduce-scatter.17.cloned.1.call-update) | async-done | bytes 131088 | tf_op jit(solution)/shard_map/reduce_scatter | solution.py:183
  727.6 65.0 %reduce-scatter.13.cloned.1.call-done = f32[64,512]{1,0:T(8,128)} async-done(((f32[1024,512]{1,0:T(8,128)}), f32[64,512]{1,0:T(8,128)}) %reduce-scatter.13.cloned.1.call-update) | async-done | bytes 131088 | tf_op jit(solution)/shard_map/reduce_scatter | solution.py:181
  792.6 65.2 %reduce-scatter.15.cloned.1.call-done = f32[64,512]{1,0:T(8,128)} async-done(((f32[1024,512]{1,0:T(8,128)}), f32[64,512]{1,0:T(8,128)}) %reduce-scatter.15.cloned.1.call-update) | async-done | bytes 131088 | tf_op jit(solution)/shard_map/reduce_scatter | solution.py:182
  857.8 108.3 %reduce-scatter.23.cloned.1.call-done = f32[2048,64]{0,1:T(8,128)} async-done(((f32[2048,1024]{0,1:T(8,128)}), f32[2048,64]{0,1:T(8,128)}) %reduce-scatter.23.cloned.1.call-update) | async-done | bytes 524304 | tf_op jit(solution)/shard_map/reduce_scatter | solution.py:186
  966.1 108.9 %reduce-scatter.21.cloned.1.call-done = f32[64,2048]{1,0:T(8,128)} async-done(((f32[1024,2048]{1,0:T(8,128)}), f32[64,2048]{1,0:T(8,128)}) %reduce-scatter.21.cloned.1.call-update) | async-done | bytes 524304 | tf_op jit(solution)/shard_map/reduce_scatter | solution.py:185
  (286 shorter events, 148.7 us)
Async XLA Ops:
  7.2 114.5 %all-reduce.5.cloned.1.call-start = ((), (), s32[]{:S(2)}) async-start(), calls=%async_computation.8 | async-start | bytes 4194304 | tf_op jit(solution)/shard_map/psum | solution.py:125
  13.1 293.6 %copy-start.50 = (f32[1,1024]{1,0:T(1,128)}, f32[1,1024]{1,0:T(1,128)S(1)}, u32[]{:S(2)}) copy-start(f32[1,1024]{1,0:T(1,128)S(1)} %get-tuple-element.34) | copy-start | bytes 12292
  13.1 300.3 %copy-start.44 = (f32[1,1024]{1,0:T(1,128)}, f32[1,1024]{1,0:T(1,128)S(1)}, u32[]{:S(2)}) copy-start(f32[1,1024]{1,0:T(1,128)S(1)} %get-tuple-element.37) | copy-start | bytes 12292
  13.1 305.6 %copy-start.33 = (f32[1,1024]{1,0:T(1,128)}, f32[1,1024]{1,0:T(1,128)S(1)}, u32[]{:S(2)}) copy-start(f32[1,1024]{1,0:T(1,128)S(1)} %get-tuple-element.35) | copy-start | bytes 12292
  13.1 116.7 %copy-start.74 = (f32[1,1024]{1,0:T(1,128)}, f32[1,1024]{1,0:T(1,128)S(1)}, u32[]{:S(2)}) copy-start(f32[1,1024]{1,0:T(1,128)S(1)} %get-tuple-element.41) | copy-start | bytes 12292
  13.1 300.3 %copy-start.35 = (f32[1,1024]{1,0:T(1,128)}, f32[1,1024]{1,0:T(1,128)S(1)}, u32[]{:S(2)}) copy-start(f32[1,1024]{1,0:T(1,128)S(1)} %get-tuple-element.39) | copy-start | bytes 12292
  55.9 152.1 %all-reduce.7.cloned.1.call-start = ((), (), s32[]{:S(2)}) async-start(), calls=%async_computation.9 | async-start | bytes 4194304 | tf_op jit(solution)/shard_map/psum | solution.py:132
  127.6 185.9 %copy-start.39 = (f32[1024]{0:T(1024)}, f32[1024]{0:T(1024)S(1)}, u32[]{:S(2)}) copy-start(f32[1024]{0:T(1024)S(1)} %broadcast_multiply_fusion.1) | copy-start | bytes 12292
  129.8 183.6 %copy-start.54 = (f32[1024]{0:T(1024)}, f32[1024]{0:T(1024)S(1)}, u32[]{:S(2)}) copy-start(f32[1024]{0:T(1024)S(1)} %fusion.71) | copy-start | bytes 12292
  144.9 156.5 %all-reduce.9.cloned.1.call-start = ((), (), s32[]{:S(2)}) async-start(), calls=%async_computation.10 | async-start | bytes 4194304 | tf_op jit(solution)/shard_map/psum | solution.py:145
  145.0 168.5 %copy-start.46 = (f32[1024]{0:T(1024)}, f32[1024]{0:T(1024)S(1)}, u32[]{:S(2)}) copy-start(f32[1024]{0:T(1024)S(1)} %fusion.73) | copy-start | bytes 12292
  210.1 96.6 %copy-start.48 = (f32[1024]{0:T(1024)}, f32[1024]{0:T(1024)S(1)}, u32[]{:S(2)}) copy-start(f32[1024]{0:T(1024)S(1)} %broadcast_multiply_fusion) | copy-start | bytes 12292
  214.8 91.9 %copy-start.56 = (f32[1024]{0:T(1024)}, f32[1024]{0:T(1024)S(1)}, u32[]{:S(2)}) copy-start(f32[1024]{0:T(1024)S(1)} %get-tuple-element.43) | copy-start | bytes 12292
  238.3 237.4 %all-reduce.11.cloned.1.call-start = ((), (), s32[]{:S(2)}) async-start(), calls=%async_computation.11 | async-start | bytes 4194304 | tf_op jit(solution)/shard_map/psum | solution.py:175
  238.4 96.0 %copy-start.32 = (f32[8,512]{1,0:T(8,128)}, f32[8,512]{1,0:T(8,128)S(1)}, u32[]{:S(2)}) copy-start(f32[8,512]{1,0:T(8,128)S(1)} %log_add_fusion.1) | copy-start | bytes 49156
  412.7 125.9 %reduce-scatter.25.cloned.1.call-start = ((), (), s32[]{:S(2)}) async-start(), calls=%async_computation.18 | async-start | bytes 557056
  482.7 114.6 %reduce-scatter.27.cloned.1.call-start = ((), (), s32[]{:S(2)}) async-start(), calls=%async_computation.19 | async-start | bytes 557056
  483.9 178.4 %reduce-scatter.19.cloned.1.call-start = ((), (), s32[]{:S(2)}) async-start(), calls=%async_computation.15 | async-start | bytes 2228224 | tf_op jit(solution)/shard_map/reduce_scatter | solution.py:184
  489.3 238.4 %reduce-scatter.17.cloned.1.call-start = ((), (), s32[]{:S(2)}) async-start(), calls=%async_computation.14 | async-start | bytes 2228224 | tf_op jit(solution)/shard_map/reduce_scatter | solution.py:183
  493.8 298.8 %reduce-scatter.13.cloned.1.call-start = ((), (), s32[]{:S(2)}) async-start(), calls=%async_computation.12 | async-start | bytes 2228224 | tf_op jit(solution)/shard_map/reduce_scatter | solution.py:181
  498.5 359.3 %reduce-scatter.15.cloned.1.call-start = ((), (), s32[]{:S(2)}) async-start(), calls=%async_computation.13 | async-start | bytes 2228224 | tf_op jit(solution)/shard_map/reduce_scatter | solution.py:182
  502.8 463.3 %reduce-scatter.23.cloned.1.call-start = ((), (), s32[]{:S(2)}) async-start(), calls=%async_computation.17 | async-start | bytes 8912896 | tf_op jit(solution)/shard_map/reduce_scatter | solution.py:186
  516.9 558.1 %reduce-scatter.21.cloned.1.call-start = ((), (), s32[]{:S(2)}) async-start(), calls=%async_computation.16 | async-start | bytes 8912896 | tf_op jit(solution)/shard_map/reduce_scatter | solution.py:185
  529.0 546.1 %copy-start.1 = (bf16[512,1024]{1,0:T(8,128)(2,1)S(1)}, bf16[512,1024]{1,0:T(8,128)(2,1)}, u32[]{:S(2)}) copy-start(bf16[512,1024]{1,0:T(8,128)(2,1)} %param.16) | copy-start | bytes 3145732
  (84 other events, 1310.9 us)
Sparse Core Ops, SparseCore 0:
  56.1 65.6 all-reduce.4
  145.0 62.9 all-reduce.6
  238.4 62.8 all-reduce.8
  412.8 62.9 all-reduce.10
  482.8 55.7 reduce-scatter.24
  542.5 54.8 reduce-scatter.26
  601.6 60.6 reduce-scatter.18
  667.1 60.5 reduce-scatter.16
  732.0 60.6 reduce-scatter.12
  797.2 60.5 reduce-scatter.14
  862.5 103.6 reduce-scatter.22
  970.6 104.3 reduce-scatter.20
where the time goes:
time: 1100 us; the launch traced here: 1080 us
  waiting for transfers between devices  793 us (72%)
  matrix products  161 us (15%)
  other arithmetic  90.5 us (8%)
  local copies, waits for them, and re-layouts  19.6 us (2%)
  between operations  16.5 us (2%)
    reduce_scatter x1, waiting for transfers between devices, on_device(): lax.psum_scatter(grad_w_up, 'dp', scatter_dimension=0, tiled=True)  109 us
    reduce_scatter x1, waiting for transfers between devices, on_device(): lax.psum_scatter(grad_w_down, 'dp', scatter_dimension=1, tiled=True)  108 us
    psum x1, waiting for transfers between devices, on_device(): lax.psum(jnp.dot(attended, w_out, preferred_element_type=jnp.float32).ast...  65.7 us
    reduce_scatter x1, waiting for transfers between devices, on_device(): lax.psum_scatter(grad_w_value, 'dp', scatter_dimension=0, tiled=True)  65.3 us
    reduce_scatter x1, waiting for transfers between devices, on_device(): lax.psum_scatter(grad_w_key, 'dp', scatter_dimension=0, tiled=True)  65.2 us
    reduce_scatter x1, waiting for transfers between devices, on_device(): lax.psum_scatter(grad_w_query, 'dp', scatter_dimension=0, tiled=True)  65 us
    reduce_scatter x1, waiting for transfers between devices, on_device(): lax.psum_scatter(grad_w_out, 'dp', scatter_dimension=1, tiled=True)  63.6 us
    psum x1, waiting for transfers between devices, on_device(): lax.psum(jnp.dot(hidden, w_down, preferred_element_type=jnp.float32).asty...  63 us
  transfers between devices with their start and end apart: 12, of which 12 were waited for; matrix products, arithmetic and copies ran while one was open for 5% of the time, Pallas kernels for 0%

commit v1 on v0

--- a/solution.py
+++ b/solution.py
@@ -20,6 +20,30 @@
 def norm_back(values, gain_vec, bias_vec, grad_output):
     unused, pull = jax.vjp(layer_norm, values, gain_vec, bias_vec)
     return pull(grad_output)
+
+
+def pair_sum(part):
+    other = lax.ppermute(part, "tensor", [(0, 1), (1, 0)])
+    return part.astype(jnp.float32) + other.astype(jnp.float32)
+
+
+def scatter_sum(grad, dp_size):
+    index = lax.axis_index("dp")
+    width = grad.shape[1]
+    rows = grad.shape[0] // dp_size
+    held = grad
+    bit = 1
+    while bit < dp_size:
+        blocks = held.reshape(-1, 2, rows, width)
+        side = (index // bit) % 2
+        keep = lax.dynamic_index_in_dim(blocks, side, 1, keepdims=False)
+        give = lax.dynamic_index_in_dim(blocks, 1 - side, 1, keepdims=False)
+        come = lax.ppermute(
+            give.astype(jnp.bfloat16), "dp", [(i, i ^ bit) for i in range(dp_size)]
+        )
+        held = (keep.astype(jnp.float32) + come.astype(jnp.float32)).reshape(-1, width)
+        bit *= 2
+    return held
 
 
 def split_heads(matrix):
@@ -122,27 +146,27 @@
         jnp.bfloat16
     )
     attended, log_totals = attention_forward(queries, key_rows, value_rows, valid_mask)
-    attn_total = lax.psum(
-        jnp.dot(attended, w_out, preferred_element_type=jnp.float32).astype(jnp.bfloat16), "tensor"
-    ).astype(jnp.float32)
+    attn_total = pair_sum(
+        jnp.dot(attended, w_out, preferred_element_type=jnp.float32).astype(jnp.bfloat16)
+    )
     middle = inputs + layer_norm(attn_total, norm_gain[1], norm_bias[1])
     normed_mid = layer_norm(middle, norm_gain[2], norm_bias[2]).astype(jnp.bfloat16)
     up_proj = jnp.dot(normed_mid, w_up, preferred_element_type=jnp.float32)
     hidden = jax.nn.gelu(up_proj).astype(jnp.bfloat16)
-    ffn_total = lax.psum(
-        jnp.dot(hidden, w_down, preferred_element_type=jnp.float32).astype(jnp.bfloat16), "tensor"
-    ).astype(jnp.float32)
+    ffn_total = pair_sum(
+        jnp.dot(hidden, w_down, preferred_element_type=jnp.float32).astype(jnp.bfloat16)
+    )
     result = (middle + layer_norm(ffn_total, norm_gain[3], norm_bias[3])).astype(jnp.bfloat16)
     grad_output = cotangent.astype(jnp.float32) * row_valid
     grad_last = norm_back(ffn_total, norm_gain[3], norm_bias[3], grad_output)
     grad_ffn_low = grad_last[0].astype(jnp.bfloat16)
-    grad_w_down = jnp.einsum("rf,rd->fd", hidden, grad_ffn_low, preferred_element_type=jnp.float32)
+    grad_w_down = jnp.einsum("rd,rf->df", grad_ffn_low, hidden, preferred_element_type=jnp.float32)
     grad_hidden = jnp.einsum("rd,fd->rf", grad_ffn_low, w_down, preferred_element_type=jnp.float32)
     unused, gelu_pull = jax.vjp(jax.nn.gelu, up_proj)
     grad_upper = gelu_pull(grad_hidden)[0].astype(jnp.bfloat16)
     grad_w_up = jnp.einsum("rd,rf->df", normed_mid, grad_upper, preferred_element_type=jnp.float32)
     mid_part = jnp.einsum("rf,df->rd", grad_upper, w_up, preferred_element_type=jnp.float32)
-    grad_normed_mid = lax.psum(mid_part.astype(jnp.bfloat16), "tensor").astype(jnp.float32)
+    grad_normed_mid = pair_sum(mid_part.astype(jnp.bfloat16))
     grad_mid, gain_mid, bias_mid = norm_back(middle, norm_gain[2], norm_bias[2], grad_normed_mid)
     grad_middle = grad_output + grad_mid
     grad_attn, gain_post, bias_post = norm_back(attn_total, norm_gain[1], norm_bias[1], grad_middle)
@@ -150,7 +174,7 @@
     gain_last = grad_last[1]
     bias_last = grad_last[2]
     grad_w_out = jnp.einsum(
-        "rk,rd->kd", attended, grad_attn_low, preferred_element_type=jnp.float32
+        "rd,rk->dk", grad_attn_low, attended, preferred_element_type=jnp.float32
     )
     grad_attended = jnp.einsum(
         "rd,kd->rk", grad_attn_low, w_out, preferred_element_type=jnp.float32
@@ -172,20 +196,24 @@
     in_part = in_part + jnp.einsum(
         "re,de->rd", grad_values, w_value, preferred_element_type=jnp.float32
     )
-    grad_normed_in = lax.psum(in_part.astype(jnp.bfloat16), "tensor").astype(jnp.float32)
+    grad_normed_in = pair_sum(in_part.astype(jnp.bfloat16))
     grad_in, gain_in, bias_in = norm_back(inputs, norm_gain[0], norm_bias[0], grad_normed_in)
     input_grad = (grad_middle + grad_in).astype(jnp.bfloat16)
     gain_grads = jnp.stack([gain_in, gain_post, gain_mid, gain_last])
     bias_grads = jnp.stack([bias_in, bias_post, bias_mid, bias_last])
+    dp_size = lax.axis_size("dp")
+    up_sum = scatter_sum(grad_w_up, dp_size)
+    down_sum = scatter_sum(grad_w_down, dp_size).T
+    norm_sum = scatter_sum(jnp.concatenate([gain_grads, bias_grads]).T, dp_size).T
     summed = (
-        lax.psum_scatter(grad_w_query, "dp", scatter_dimension=0, tiled=True),
-        lax.psum_scatter(grad_w_key, "dp", scatter_dimension=0, tiled=True),
-        lax.psum_scatter(grad_w_value, "dp", scatter_dimension=0, tiled=True),
-        lax.psum_scatter(grad_w_out, "dp", scatter_dimension=1, tiled=True),
-        lax.psum_scatter(grad_w_up, "dp", scatter_dimension=0, tiled=True),
-        lax.psum_scatter(grad_w_down, "dp", scatter_dimension=1, tiled=True),
-        lax.psum_scatter(gain_grads, "dp", scatter_dimension=1, tiled=True),
-        lax.psum_scatter(bias_grads, "dp", scatter_dimension=1, tiled=True),
+        scatter_sum(grad_w_query, dp_size),
+        scatter_sum(grad_w_key, dp_size),
+        scatter_sum(grad_w_value, dp_size),
+        scatter_sum(grad_w_out, dp_size).T,
+        up_sum,
+        down_sum,
+        norm_sum[:4],
+        norm_sum[4:],
     )
     return (
         result,

time: 1100 us -> 495 us (0.45)
  waiting for transfers between devices: 793 us -> 163 us
  starting transfers between devices: 0.88 us -> 37 us
  local copies, waits for them, and re-layouts: 19.6 us -> 43.4 us
  matrix products: 161 us -> 139 us
  between operations: 16.5 us -> 3.39 us
    reduce_scatter x6 -> x0, waiting for transfers between devices: 476 us -> none  [the longest x1 109 us: on_device(): lax.psum_scatter(grad_w_up, 'dp', scatter_dimension=0, tiled=True)]
    psum x4 -> x0, waiting for transfers between devices: 255 us -> none  [the longest x1 65.7 us: on_device(): lax.psum(jnp.dot(attended, w_out, preferred_element_type=jnp.float32).ast...]
    ppermute x0 -> x32, waiting for transfers between devices: none -> 163 us  [the longest x4 102 us: pair_sum(): other = lax.ppermute(part, 'tensor', [(0, 1), (1, 0)])]
    unnamed x14 -> x0, waiting for transfers between devices: 62.4 us -> none
    ppermute x0 -> x32, starting transfers between devices: none -> 37 us  [the longest x28 29.6 us: scatter_sum(): lax.ppermute(give.astype(jnp.bfloat16), 'dp', [(i, i ^ bit) for i in rang...]
    add x0 -> x21, other arithmetic: none -> 14.1 us  [scatter_sum(): keep.astype(jnp.float32) + come.astype(jnp.float32)]
    unnamed x196 -> x152, local copies, waits for them, and re-layouts: 19.4 us -> 30.3 us
  transfers between devices with their start and end apart: 12 -> 32, of which waited for: 12 -> 19; matrix products, arithmetic and copies ran while one was open for 5% -> 36% of each run, Pallas kernels for 0% -> 0%
where the time goes in v1:
time: 495 us; the launch traced here: 486 us
  waiting for transfers between devices  163 us (33%)
  matrix products  139 us (28%)
  other arithmetic  99.7 us (20%)
  local copies, waits for them, and re-layouts  43.4 us (9%)
  starting transfers between devices  37 us (7%)
    ppermute x4, waiting for transfers between devices, pair_sum(): other = lax.ppermute(part, 'tensor', [(0, 1), (1, 0)])  102 us
    ppermute x28, waiting for transfers between devices, scatter_sum(): lax.ppermute(give.astype(jnp.bfloat16), 'dp', [(i, i ^ bit) for i in rang...  60.9 us
    unnamed x152, local copies, waits for them, and re-layouts  30.3 us
    reduce_sum x7, other arithmetic, layer_norm(): return centered * lax.rsqrt(variance + epsilon) * gain_vec + bias_vec  29.7 us
    ppermute x28, starting transfers between devices, scatter_sum(): lax.ppermute(give.astype(jnp.bfloat16), 'dp', [(i, i ^ bit) for i in rang...  29.6 us
    convert_element_type x2, other arithmetic, attention_backward(): grad_scores = (soft_weights * (grad_soft - row_dots)).astype(jnp.bfloat16)  22.2 us
    dot_general x2, matrix products, attention_backward(): jnp.einsum('qhd,khd->hqk', grad_block, value_heads, preferred_element_typ...  21.4 us
    add x21, other arithmetic, scatter_sum(): keep.astype(jnp.float32) + come.astype(jnp.float32)  14.1 us
  transfers between devices with their start and end apart: 32, of which 19 were waited for; matrix products, arithmetic and copies ran while one was open for 36% of the time, Pallas kernels for 0%

profile of v1, /device:TPU:0, one launch (start us, length us, event | category | flops | bytes accessed | tf_op | source)
XLA Modules:
  0.0 486.0 jit_solution(6869486342009922972)
XLA Ops:
  15.6 8.8 %fusion.97 = (f32[8,512]{1,0:T(8,128)S(1)}, f32[8,512,1024]{2,1,0:T(8,128)}) fusion(bf16[512,8,64]{0,2,1:T(8,128)(2,1)S(1)} %bitcast.262, bf16[1024,8,64]{0,2,1:T(8,128)(2,1)S(1)} %bitcast.249, pred[1024]{0:T(1024)(128)(4,1)S(1)} %iota_compare_fusion), kind=kOutput, calls=%fused_computation.226 | convolution fusion | flops 549449728 | bytes 18367488 | tf_op jit(solution)/shard_map/qhd,khd->hqk/dot_general | solution.py:55
  32.2 8.0 %fusion = f32[8,512]{1,0:T(8,128)S(1)} fusion(f32[8,512,1024]{2,1,0:T(8,128)} %get-tuple-element.89, f32[8,512]{1,0:T(8,128)S(1)} %get-tuple-element.88), kind=kLoop, calls=%fused_computation.12 | loop fusion | flops 8384512 | bytes 16809984 | tf_op jit(solution)/shard_map/reduce_sum | solution.py:78
  51.2 45.6 %collective-permute-done = bf16[1024,1024]{0,1:T(8,128)(2,1)S(1)} collective-permute-done((bf16[1024,1024]{0,1:T(8,128)(2,1)S(1)}, bf16[1024,1024]{0,1:T(8,128)(2,1)S(1)}, u32[]{:S(2)}, u32[]{:S(2)}) %collective-permute-start) | collective-permute-done | bytes 2097184 | tf_op jit(solution)/shard_map/ppermute | solution.py:26
  109.3 6.1 %convolution_convert_fusion.1 = bf16[1024,1024]{0,1:T(8,128)(2,1)} fusion(bf16[2048,1024]{1,0:T(8,128)(2,1)S(1)} %copy-done.58, f32[1024,2048]{1,0:T(8,128)S(1)} %fusion.87), kind=kOutput, calls=%fused_computation.92 | convolution fusion | flops 4314890240 | bytes 14680064 | tf_op jit(solution)/shard_map/dot_general | solution.py:157
  120.7 41.8 %collective-permute-done.1 = bf16[1024,1024]{0,1:T(8,128)(2,1)} collective-permute-done((bf16[1024,1024]{0,1:T(8,128)(2,1)}, bf16[1024,1024]{0,1:T(8,128)(2,1)}, u32[]{:S(2)}, u32[]{:S(2)}) %collective-permute-start.1) | collective-permute-done | bytes 2097184 | tf_op jit(solution)/shard_map/ppermute | solution.py:26
  170.1 6.4 %multiply_reduce_fusion.2 = (f32[1024]{0:T(1024)}, f32[1024]{0:T(1024)S(1)}, bf16[1024,1024]{0,1:T(8,128)(2,1)}) fusion(bf16[1024,1024]{0,1:T(8,128)(2,1)S(1)} %copy.61, bf16[1024,1024]{0,1:T(8,128)(2,1)} %collective-permute-done.1, bf16[1024,1024]{0,1:T(8,128)(2,1)} %convolution_convert_fusion.1, f32[1024]{0:T(1024)S(1)} %fusion.80, ...), kind=kLoop, calls=%fused_computation.54 | loop fusion | flops 19920896 | bytes 12615680 | tf_op jit(solution)/shard_map/transpose(jvp())/reduce_sum | solution.py:17
  176.5 13.9 %fusion.10 = bf16[1024,2048]{1,0:T(8,128)(2,1)S(1)} fusion(f32[1024,2048]{1,0:T(8,128)} %copy-done.68, bf16[2048,1024]{1,0:T(8,128)(2,1)S(1)} %copy-done.59, f32[1024]{0:T(1024)S(1)} %negate_multiply_fusion.3, bf16[1024,1024]{0,1:T(8,128)(2,1)S(1)} %copy.61, bf16[1024,1024]{0,1:T(8,128)(2,1)} %collective-permute-done.1, ...), kind=kOutput, calls=%fused_computation.24 | convolution fusion | flops 4350541824 | bytes 23093248 | tf_op jit(solution)/shard_map/rd,fd->rf/dot_general | solution.py:164
  190.4 6.0 %convolution_convert_fusion = bf16[1024,1024]{0,1:T(8,128)(2,1)} fusion(bf16[1024,2048]{1,0:T(8,128)(2,1)S(1)} %fusion.10, bf16[1024,2048]{1,0:T(8,128)(2,1)S(1)} %copy-done.61), kind=kOutput, calls=%fused_computation.91 | convolution fusion | flops 4296015872 | bytes 10485760 | tf_op jit(solution)/shard_map/rf,df->rd/dot_general | solution.py:168
  197.8 13.9 %fusion.48 = f32[1024,2048]{1,0:T(8,128)} fusion(f32[1024]{0:T(1024)S(1)} %negate_multiply_fusion.3, f32[1024,2048]{1,0:T(8,128)} %copy-done.68, bf16[1024,1024]{0,1:T(8,128)(2,1)S(1)} %copy.61, bf16[1024,1024]{0,1:T(8,128)(2,1)} %collective-permute-done.1, bf16[1024,1024]{0,1:T(8,128)(2,1)} %convolution_convert_fusion.1, f32[1024]{0:T(1024)S(1)} %get-tuple-element.84, ...), kind=kOutput, calls=%fused_computation.120 | convolution fusion | flops 4327473152 | bytes 23093248 | tf_op jit(solution)/shard_map/rd,rf->df/dot_general | solution.py:163
  219.1 6.5 %fusion.86 = f32[1024,2048]{1,0:T(8,128)S(1)} fusion(bf16[1024,2048]{1,0:T(8,128)(2,1)} %copy-done.69, f32[1024,1024]{0,1:T(8,128)S(1)} %copy-done.5, f32[1024]{0:T(1024)S(1)} %bitcast.340, f32[1024]{0:T(1024)S(1)} %bitcast.317, f32[1024]{0:T(1024)S(1)} %fusion.78, f32[1024]{0:T(1024)S(1)} %broadcast_multiply_fusion.1), kind=kOutput, calls=%fused_computation.215 | convolution fusion | flops 4300210176 | bytes 16793600 | tf_op jit(solution)/shard_map/rd,rf->df/dot_general | solution.py:167
  227.5 15.0 %collective-permute-done.2 = bf16[1024,1024]{0,1:T(8,128)(2,1)} collective-permute-done((bf16[1024,1024]{0,1:T(8,128)(2,1)}, bf16[1024,1024]{0,1:T(8,128)(2,1)}, u32[]{:S(2)}, u32[]{:S(2)}) %collective-permute-start.2) | collective-permute-done | bytes 2097184 | tf_op jit(solution)/shard_map/ppermute | solution.py:26
  250.8 6.8 %multiply_reduce_fusion.4 = (f32[1024]{0:T(1024)}, f32[1024]{0:T(1024)S(1)}, f32[1024]{0:T(1024)}, f32[1024,1024]{0,1:T(8,128)S(1)}) fusion(bf16[1024,1024]{0,1:T(8,128)(2,1)S(1)} %copy-done.13, bf16[1024,1024]{0,1:T(8,128)(2,1)S(1)} %copy-done.11, f32[1024]{0:T(1024)S(1)} %fusion.77, f32[1024]{0:T(1024)S(1)} %broadcast_multiply_fusion.2, ...), kind=kLoop, calls=%fused_computation.56 | loop fusion | flops 25162752 | bytes 18923520 | tf_op jit(solution)/shard_map/transpose(jvp())/reduce_sum | solution.py:17
  275.8 11.5 %multiply_reduce_fusion.1 = (f32[8,512]{1,0:T(8,128)S(1)}, f32[8,512,1024]{2,1,0:T(8,128)}) fusion(f32[8,512,1024]{2,1,0:T(8,128)} %get-tuple-element.89, f32[8,512]{1,0:T(8,128)S(1)} %copy-done.44, bf16[512,8,64]{0,2,1:T(8,128)(2,1)S(1)} %bitcast.266, bf16[1024,8,64]{0,2,1:T(8,128)(2,1)} %bitcast.274), kind=kOutput, calls=%fused_computation.4 | convolution fusion | flops 549449728 | bytes 35160064 | tf_op jit(solution)/shard_map/qhd,khd->hqk/dot_general | solution.py:104
  287.3 8.4 %add_convert_fusion.6 = bf16[8,64,1024]{2,1,0:T(8,128)(2,1)S(1)} fusion(f32[8,64,1024]{2,1,0:T(8,128)} %fusion.11, bf16[512,8,64]{0,2,1:T(8,128)(2,1)S(1)} %bitcast.267, f32[8,512,1024]{2,1,0:T(8,128)} %get-tuple-element.89, f32[8,512]{1,0:T(8,128)S(1)} %copy-done.44), kind=kOutput, calls=%fused_computation.89 | convolution fusion | flops 546308096 | bytes 20463616 | tf_op jit(solution)/shard_map/hqk,qhd->khd/dot_general | solution.py:121
  298.5 11.8 %multiply_convert_fusion.1 = bf16[8,512,1024]{2,1,0:T(8,128)(2,1)S(1)} fusion(f32[8,512,1024]{2,1,0:T(8,128)} %get-tuple-element.93, f32[8,512,1024]{2,1,0:T(8,128)} %get-tuple-element.89, f32[8,512]{1,0:T(8,128)S(1)} %get-tuple-element.92, f32[8,512]{1,0:T(8,128)S(1)} %copy-done.44), kind=kLoop, calls=%fused_computation.3 | loop fusion | flops 16777216 | bytes 41975808 | tf_op jit(solution)/shard_map/convert_element_type | solution.py:108
  316.5 6.8 %fusion.42 = bf16[8,64,512]{2,1,0:T(8,128)(2,1)} fusion(bf16[1024,8,64]{0,2,1:T(8,128)(2,1)S(1)} %bitcast.250, bf16[8,512,1024]{2,1,0:T(8,128)(2,1)} %copy-done.9), kind=kOutput, calls=%fused_computation.100 | convolution fusion | flops 537395200 | bytes 9961472 | tf_op jit(solution)/shard_map/hqk,khd->qhd/dot_general | solution.py:110
  323.3 9.9 %multiply_reduce_fusion = (f32[8,512]{1,0:T(8,128)}, f32[8,512,1024]{2,1,0:T(8,128)}) fusion(f32[8,512,1024]{2,1,0:T(8,128)S(1)} %bitcast.247, f32[8,512]{1,0:T(8,128)S(1)} %log_add_fusion, bf16[512,8,64]{0,2,1:T(8,128)(2,1)S(1)} %bitcast.265, bf16[1024,8,64]{0,2,1:T(8,128)(2,1)} %bitcast.275), kind=kOutput, calls=%fused_computation.1 | convolution fusion | flops 549449728 | bytes 35160064 | tf_op jit(solution)/shard_map/qhd,khd->hqk/dot_general | solution.py:104
  340.6 10.4 %multiply_convert_fusion = bf16[8,512,1024]{2,1,0:T(8,128)(2,1)} fusion(f32[8,512,1024]{2,1,0:T(8,128)} %get-tuple-element.91, f32[8,512,1024]{2,1,0:T(8,128)S(1)} %bitcast.247, f32[8,512]{1,0:T(8,128)S(1)} %copy-done.49, f32[8,512]{1,0:T(8,128)S(1)} %log_add_fusion), kind=kLoop, calls=%fused_computation | loop fusion | flops 16777216 | bytes 41975808 | tf_op jit(solution)/shard_map/convert_element_type | solution.py:108
  351.1 6.2 %fusion.43 = bf16[8,64,512]{2,1,0:T(8,128)(2,1)S(1)} fusion(bf16[1024,8,64]{0,2,1:T(8,128)(2,1)S(1)} %bitcast.251, bf16[8,512,1024]{2,1,0:T(8,128)(2,1)} %multiply_convert_fusion), kind=kOutput, calls=%fused_computation.101 | convolution fusion | flops 537395200 | bytes 9961472 | tf_op jit(solution)/shard_map/hqk,khd->qhd/dot_general | solution.py:110
  375.1 6.6 %collective-permute-done.17 = bf16[4,64,512]{2,1,0:T(8,128)(2,1)S(1)} collective-permute-done((bf16[4,64,512]{2,1,0:T(8,128)(2,1)S(1)}, bf16[4,64,512]{2,1,0:T(8,128)(2,1)S(1)}, u32[]{:S(2)}, u32[]{:S(2)}) %collective-permute-start.17) | collective-permute-done | bytes 262176 | tf_op jit(solution)/shard_map/ppermute | solution.py:41
  429.2 12.5 %collective-permute-done.26 = bf16[2,64,2048]{2,1,0:T(8,128)(2,1)S(1)} collective-permute-done((bf16[2,64,2048]{2,1,0:T(8,128)(2,1)S(1)}, bf16[2,64,2048]{2,1,0:T(8,128)(2,1)S(1)}, u32[]{:S(2)}, u32[]{:S(2)}) %collective-permute-start.26) | collective-permute-done | bytes 524320 | tf_op jit(solution)/shard_map/ppermute | solution.py:41
  443.7 5.6 %collective-permute-done.22 = bf16[2,64,2048]{2,1,0:T(8,128)(2,1)S(1)} collective-permute-done((bf16[2,64,2048]{2,1,0:T(8,128)(2,1)S(1)}, bf16[2,64,2048]{2,1,0:T(8,128)(2,1)S(1)}, u32[]{:S(2)}, u32[]{:S(2)}) %collective-permute-start.22) | collective-permute-done | bytes 524320 | tf_op jit(solution)/shard_map/ppermute | solution.py:41
  452.4 8.6 %collective-permute-done.27 = bf16[1,64,2048]{2,1,0:T(8,128)(2,1)S(1)} collective-permute-done((bf16[1,64,2048]{2,1,0:T(8,128)(2,1)S(1)}, bf16[1,64,2048]{2,1,0:T(8,128)(2,1)S(1)}, u32[]{:S(2)}, u32[]{:S(2)}) %collective-permute-start.27) | collective-permute-done | bytes 262176 | tf_op jit(solution)/shard_map/ppermute | solution.py:41
  475.5 5.5 %add_convert_fusion = bf16[1024,1024]{0,1:T(8,128)(2,1)} fusion(f32[1024,1024]{0,1:T(8,128)} %copy-done.14, f32[1024]{0:T(1024)S(1)} %negate_multiply_fusion, f32[1024]{0:T(1024)S(1)} %multiply_multiply_fusion.2, f32[1024]{0:T(1024)S(1)} %copy-done.46, bf16[1024,1024]{0,1:T(8,128)(2,1)S(1)} %copy-done.7, f32[1024]{0:T(1024)S(1)} %copy-done.51, ...), kind=kLoop, calls=%fused_computation.57 | loop fusion | flops 13631488 | bytes 12603392 | tf_op jit(solution)/shard_map/convert_element_type | solution.py:201
  (328 shorter events, 199.9 us)
Async XLA Ops:
  48.2 48.6 %collective-permute-start = (bf16[1024,1024]{0,1:T(8,128)(2,1)S(1)}, bf16[1024,1024]{0,1:T(8,128)(2,1)S(1)}, u32[]{:S(2)}, u32[]{:S(2)}) collective-permute-start(bf16[1024,1024]{0,1:T(8,128)(2,1)S(1)} %convolution_convert_fusion.2), channel_id=1, source_target_pairs={{0,1},{1,0},{2,3},{3,2},{4,5},{5,4},{6,7},{7,6},{8,9},{9,8},{10,11... | collective-permute-start | bytes 6291464 | tf_op jit(solution)/shard_map/ppermute | solution.py:26
  115.4 47.1 %collective-permute-start.1 = (bf16[1024,1024]{0,1:T(8,128)(2,1)}, bf16[1024,1024]{0,1:T(8,128)(2,1)}, u32[]{:S(2)}, u32[]{:S(2)}) collective-permute-start(bf16[1024,1024]{0,1:T(8,128)(2,1)} %convolution_convert_fusion.1), channel_id=1, source_target_pairs={{0,1},{1,0},{2,3},{3,2},{4,5},{5,4},{6,7},{7,6},{8,9},{9,8},{10,11... | collective-permute-start | bytes 6291464 | tf_op jit(solution)/shard_map/ppermute | solution.py:26
  196.3 46.2 %collective-permute-start.2 = (bf16[1024,1024]{0,1:T(8,128)(2,1)}, bf16[1024,1024]{0,1:T(8,128)(2,1)}, u32[]{:S(2)}, u32[]{:S(2)}) collective-permute-start(bf16[1024,1024]{0,1:T(8,128)(2,1)} %convolution_convert_fusion), channel_id=1, source_target_pairs={{0,1},{1,0},{2,3},{3,2},{4,5},{5,4},{6,7},{7,6},{8,9},{9,8},{10,11... | collective-permute-start | bytes 6291464 | tf_op jit(solution)/shard_map/ppermute | solution.py:26
  218.3 44.0 %collective-permute-start.24 = (bf16[8,64,2048]{2,1,0:T(8,128)(2,1)S(1)}, bf16[8,64,2048]{2,1,0:T(8,128)(2,1)}, u32[]{:S(2)}, u32[]{:S(2)}) collective-permute-start(bf16[8,64,2048]{2,1,0:T(8,128)(2,1)S(1)} %fusion.39), channel_id=1, source_target_pairs={{0,2},{2,0},{4,6},{6,4},{8,10},{10,8},{12,14},{14,12},{16,18},{18,... | collective-permute-start | bytes 6291464 | tf_op jit(solution)/shard_map/ppermute | solution.py:41
  227.5 105.8 %collective-permute-start.20 = (bf16[8,64,2048]{2,1,0:T(8,128)(2,1)}, bf16[8,64,2048]{2,1,0:T(8,128)(2,1)}, u32[]{:S(2)}, u32[]{:S(2)}) collective-permute-start(bf16[8,64,2048]{2,1,0:T(8,128)(2,1)} %fusion.38), channel_id=1, source_target_pairs={{0,2},{2,0},{4,6},{6,4},{8,10},{10,8},{12,14},{14,12},{16,18},{18,... | collective-permute-start | bytes 6291464 | tf_op jit(solution)/shard_map/ppermute | solution.py:41
  269.7 152.6 %collective-permute-start.25 = (bf16[4,64,2048]{2,1,0:T(8,128)(2,1)}, bf16[4,64,2048]{2,1,0:T(8,128)(2,1)}, u32[]{:S(2)}, u32[]{:S(2)}) collective-permute-start(bf16[4,64,2048]{2,1,0:T(8,128)(2,1)} %fusion.47), channel_id=1, source_target_pairs={{0,4},{2,6},{4,0},{6,2},{8,12},{10,14},{12,8},{14,10},{16,20},{18,... | collective-permute-start | bytes 3145736 | tf_op jit(solution)/shard_map/ppermute | solution.py:41
  271.8 96.0 %collective-permute-start.16 = (bf16[8,64,512]{2,1,0:T(8,128)(2,1)}, bf16[8,64,512]{2,1,0:T(8,128)(2,1)}, u32[]{:S(2)}, u32[]{:S(2)}) collective-permute-start(bf16[8,64,512]{2,1,0:T(8,128)(2,1)} %fusion.58), channel_id=1, source_target_pairs={{0,2},{2,0},{4,6},{6,4},{8,10},{10,8},{12,14},{14,12},{16,18},{18,... | collective-permute-start | bytes 1572872 | tf_op jit(solution)/shard_map/ppermute | solution.py:41
  298.0 72.0 %collective-permute-start.12 = (bf16[8,64,512]{2,1,0:T(8,128)(2,1)}, bf16[8,64,512]{2,1,0:T(8,128)(2,1)}, u32[]{:S(2)}, u32[]{:S(2)}) collective-permute-start(bf16[8,64,512]{2,1,0:T(8,128)(2,1)} %fusion.54), channel_id=1, source_target_pairs={{0,2},{2,0},{4,6},{6,4},{8,10},{10,8},{12,14},{14,12},{16,18},{18,... | collective-permute-start | bytes 1572872 | tf_op jit(solution)/shard_map/ppermute | solution.py:41
  339.8 87.7 %collective-permute-start.21 = (bf16[4,64,2048]{2,1,0:T(8,128)(2,1)}, bf16[4,64,2048]{2,1,0:T(8,128)(2,1)}, u32[]{:S(2)}, u32[]{:S(2)}) collective-permute-start(bf16[4,64,2048]{2,1,0:T(8,128)(2,1)} %fusion.46), channel_id=1, source_target_pairs={{0,4},{2,6},{4,0},{6,2},{8,12},{10,14},{12,8},{14,10},{16,20},{18,... | collective-permute-start | bytes 3145736 | tf_op jit(solution)/shard_map/ppermute | solution.py:41
  362.0 10.5 %collective-permute-start.8 = (bf16[8,64,512]{2,1,0:T(8,128)(2,1)S(1)}, bf16[8,64,512]{2,1,0:T(8,128)(2,1)S(1)}, u32[]{:S(2)}, u32[]{:S(2)}) collective-permute-start(bf16[8,64,512]{2,1,0:T(8,128)(2,1)S(1)} %fusion.53), channel_id=1, source_target_pairs={{0,2},{2,0},{4,6},{6,4},{8,10},{10,8},{12,14},{14,12},{16,18},{18,... | collective-permute-start | bytes 1572872 | tf_op jit(solution)/shard_map/ppermute | solution.py:41
  367.8 6.5 %collective-permute-start.4 = (bf16[8,64,512]{2,1,0:T(8,128)(2,1)S(1)}, bf16[8,64,512]{2,1,0:T(8,128)(2,1)S(1)}, u32[]{:S(2)}, u32[]{:S(2)}) collective-permute-start(bf16[8,64,512]{2,1,0:T(8,128)(2,1)S(1)} %fusion.57), channel_id=1, source_target_pairs={{0,2},{2,0},{4,6},{6,4},{8,10},{10,8},{12,14},{14,12},{16,18},{18,... | collective-permute-start | bytes 1572872 | tf_op jit(solution)/shard_map/ppermute | solution.py:41
  370.0 91.9 %collective-permute-start.3 = (bf16[1024,1024]{0,1:T(8,128)(2,1)S(1)}, bf16[1024,1024]{0,1:T(8,128)(2,1)S(1)}, u32[]{:S(2)}, u32[]{:S(2)}) collective-permute-start(bf16[1024,1024]{0,1:T(8,128)(2,1)S(1)} %add_convert_fusion.1), channel_id=1, source_target_pairs={{0,1},{1,0},{2,3},{3,2},{4,5},{5,4},{6,7},{7,6},{8,9},{9,8},{10,11... | collective-permute-start | bytes 6291464 | tf_op jit(solution)/shard_map/ppermute | solution.py:26
  372.5 9.2 %collective-permute-start.17 = (bf16[4,64,512]{2,1,0:T(8,128)(2,1)S(1)}, bf16[4,64,512]{2,1,0:T(8,128)(2,1)S(1)}, u32[]{:S(2)}, u32[]{:S(2)}) collective-permute-start(bf16[4,64,512]{2,1,0:T(8,128)(2,1)S(1)} %fusion.61), channel_id=1, source_target_pairs={{0,4},{2,6},{4,0},{6,2},{8,12},{10,14},{12,8},{14,10},{16,20},{18,... | collective-permute-start | bytes 786440 | tf_op jit(solution)/shard_map/ppermute | solution.py:41
  374.2 13.1 %collective-permute-start.13 = (bf16[4,64,512]{2,1,0:T(8,128)(2,1)S(1)}, bf16[4,64,512]{2,1,0:T(8,128)(2,1)S(1)}, u32[]{:S(2)}, u32[]{:S(2)}) collective-permute-start(bf16[4,64,512]{2,1,0:T(8,128)(2,1)S(1)} %fusion.63), channel_id=1, source_target_pairs={{0,4},{2,6},{4,0},{6,2},{8,12},{10,14},{12,8},{14,10},{16,20},{18,... | collective-permute-start | bytes 786440 | tf_op jit(solution)/shard_map/ppermute | solution.py:41
  381.7 11.2 %collective-permute-start.9 = (bf16[4,64,512]{2,1,0:T(8,128)(2,1)S(1)}, bf16[4,64,512]{2,1,0:T(8,128)(2,1)S(1)}, u32[]{:S(2)}, u32[]{:S(2)}) collective-permute-start(bf16[4,64,512]{2,1,0:T(8,128)(2,1)S(1)} %fusion.62), channel_id=1, source_target_pairs={{0,4},{2,6},{4,0},{6,2},{8,12},{10,14},{12,8},{14,10},{16,20},{18,... | collective-permute-start | bytes 786440 | tf_op jit(solution)/shard_map/ppermute | solution.py:41
  387.3 10.3 %collective-permute-start.5 = (bf16[4,64,512]{2,1,0:T(8,128)(2,1)S(1)}, bf16[4,64,512]{2,1,0:T(8,128)(2,1)S(1)}, u32[]{:S(2)}, u32[]{:S(2)}) collective-permute-start(bf16[4,64,512]{2,1,0:T(8,128)(2,1)S(1)} %fusion.60), channel_id=1, source_target_pairs={{0,4},{2,6},{4,0},{6,2},{8,12},{10,14},{12,8},{14,10},{16,20},{18,... | collective-permute-start | bytes 786440 | tf_op jit(solution)/shard_map/ppermute | solution.py:41
  399.4 7.2 %collective-permute-start.10 = (bf16[2,64,512]{2,1,0:T(8,128)(2,1)S(1)}, bf16[2,64,512]{2,1,0:T(8,128)(2,1)S(1)}, u32[]{:S(2)}, u32[]{:S(2)}) collective-permute-start(bf16[2,64,512]{2,1,0:T(8,128)(2,1)S(1)} %fusion.65), channel_id=1, source_target_pairs={{0,8},{2,10},{4,12},{6,14},{8,0},{10,2},{12,4},{14,6},{16,24},{18,... | collective-permute-start | bytes 393224 | tf_op jit(solution)/shard_map/ppermute | solution.py:41
  406.6 7.8 %collective-permute-start.19 = (bf16[1,64,512]{2,1,0:T(8,128)(2,1)S(1)}, bf16[1,64,512]{2,1,0:T(8,128)(2,1)S(1)}, u32[]{:S(2)}, u32[]{:S(2)}) collective-permute-start(bf16[1,64,512]{2,1,0:T(8,128)(2,1)S(1)} %dynamic-slice_convert_fusion.14), channel_id=1, source_target_pairs={{0,16},{2,18},{4,20},{6,22},{8,24},{10,26},{12,28},{14,30},{16,0},... | collective-permute-start | bytes 196616 | tf_op jit(solution)/shard_map/ppermute | solution.py:41
  409.3 7.2 %collective-permute-start.15 = (bf16[1,64,512]{2,1,0:T(8,128)(2,1)S(1)}, bf16[1,64,512]{2,1,0:T(8,128)(2,1)S(1)}, u32[]{:S(2)}, u32[]{:S(2)}) collective-permute-start(bf16[1,64,512]{2,1,0:T(8,128)(2,1)S(1)} %dynamic-slice_convert_fusion.15), channel_id=1, source_target_pairs={{0,16},{2,18},{4,20},{6,22},{8,24},{10,26},{12,28},{14,30},{16,0},... | collective-permute-start | bytes 196616 | tf_op jit(solution)/shard_map/ppermute | solution.py:41
  424.0 17.8 %collective-permute-start.26 = (bf16[2,64,2048]{2,1,0:T(8,128)(2,1)S(1)}, bf16[2,64,2048]{2,1,0:T(8,128)(2,1)S(1)}, u32[]{:S(2)}, u32[]{:S(2)}) collective-permute-start(bf16[2,64,2048]{2,1,0:T(8,128)(2,1)S(1)} %fusion.56), channel_id=1, source_target_pairs={{0,8},{2,10},{4,12},{6,14},{8,0},{10,2},{12,4},{14,6},{16,24},{18,... | collective-permute-start | bytes 1572872 | tf_op jit(solution)/shard_map/ppermute | solution.py:41
  429.1 20.1 %collective-permute-start.22 = (bf16[2,64,2048]{2,1,0:T(8,128)(2,1)S(1)}, bf16[2,64,2048]{2,1,0:T(8,128)(2,1)S(1)}, u32[]{:S(2)}, u32[]{:S(2)}) collective-permute-start(bf16[2,64,2048]{2,1,0:T(8,128)(2,1)S(1)} %fusion.55), channel_id=1, source_target_pairs={{0,8},{2,10},{4,12},{6,14},{8,0},{10,2},{12,4},{14,6},{16,24},{18,... | collective-permute-start | bytes 1572872 | tf_op jit(solution)/shard_map/ppermute | solution.py:41
  441.9 19.1 %collective-permute-start.27 = (bf16[1,64,2048]{2,1,0:T(8,128)(2,1)S(1)}, bf16[1,64,2048]{2,1,0:T(8,128)(2,1)S(1)}, u32[]{:S(2)}, u32[]{:S(2)}) collective-permute-start(bf16[1,64,2048]{2,1,0:T(8,128)(2,1)S(1)} %dynamic-slice_convert_fusion.6), channel_id=1, source_target_pairs={{0,16},{2,18},{4,20},{6,22},{8,24},{10,26},{12,28},{14,30},{16,0},... | collective-permute-start | bytes 786440 | tf_op jit(solution)/shard_map/ppermute | solution.py:41
  450.4 18.7 %collective-permute-start.23 = (bf16[1,64,2048]{2,1,0:T(8,128)(2,1)}, bf16[1,64,2048]{2,1,0:T(8,128)(2,1)S(1)}, u32[]{:S(2)}, u32[]{:S(2)}) collective-permute-start(bf16[1,64,2048]{2,1,0:T(8,128)(2,1)} %dynamic-slice_convert_fusion.7), channel_id=1, source_target_pairs={{0,16},{2,18},{4,20},{6,22},{8,24},{10,26},{12,28},{14,30},{16,0},... | collective-permute-start | bytes 786440 | tf_op jit(solution)/shard_map/ppermute | solution.py:41
  474.9 10.1 %collective-permute-start.31 = (bf16[1,64,8]{1,2,0:T(8,128)(2,1)S(1)}, bf16[1,64,8]{1,2,0:T(8,128)(2,1)S(1)}, u32[]{:S(2)}, u32[]{:S(2)}) collective-permute-start(bf16[1,64,8]{1,2,0:T(8,128)(2,1)S(1)} %fusion.75), channel_id=1, source_target_pairs={{0,16},{2,18},{4,20},{6,22},{8,24},{10,26},{12,28},{14,30},{16,0},... | collective-permute-start | bytes 3080 | tf_op jit(solution)/shard_map/ppermute | solution.py:41
  (82 other events, 850.1 us)

commit v2 on v1

v2 whole, which is shorter than its diff:
```python
import functools

import jax
import jax.numpy as jnp
from jax import lax
from jax.experimental import pallas as pl
from jax.experimental.pallas import tpu as pltpu
from jax.sharding import PartitionSpec as P

HD = 64
LANES = 128
EPS = 1e-05
CHUNK = 256
BLOCK = 32
NEG = -1000000000.0
F32 = jnp.float32
BF16 = jnp.bfloat16
MESH = pl.DeviceIdType.MESH
NN = (((1,), (0,)), ((), ()))
NT = (((1,), (1,)), ((), ()))
TN = (((0,), (0,)), ((), ()))
ROOT = 0.7978845608028654
CUBE = 0.044715


def dot(left, right, dims):
    return lax.dot_general(left, right, dims, preferred_element_type=F32)


def row_mean(values):
    return jnp.sum(values, axis=-1, keepdims=True) * (1.0 / values.shape[-1])


def normalize(values):
    centered = values - row_mean(values)
    scale = lax.rsqrt(row_mean(centered * centered) + EPS)
    return centered * scale, scale


def norm_pull(hat, scale, gain, grad):
    weighed = grad * gain
    return scale * (weighed - row_mean(weighed) - hat * row_mean(weighed * hat))


def gelu_both(v):
    square = v * v
    tanh = jnp.tanh(v * (ROOT + (ROOT * CUBE) * square))
    half = 0.5 + 0.5 * tanh
    slope = half + (0.5 * v) * (1.0 - tanh * tanh) * (ROOT + (3.0 * ROOT * CUBE) * square)
    return v * half, slope


def lane_index(shape):
    return lax.broadcasted_iota(jnp.int32, shape, 1)


def head_of_pair(values, side):
    low = lane_index(values.shape) < HD
    return jnp.where(low if side == 0 else jnp.logical_not(low), values, jnp.zeros_like(values))


def join_pair(first, second):
    return jnp.where(lane_index(first.shape) < HD, first, second)


def fold_rows(values):
    return jnp.sum(values.reshape(-1, 8, values.shape[-1]), axis=0)


def layer_kernel(
    length_ref, tokens_hbm, wq_hbm, wk_hbm, wv_hbm, wo_hbm, wu_hbm, wd_hbm, gain_ref, bias_ref, cot_hbm,
    result_hbm, gmid_hbm, nin_hbm, att_hbm, nmid_hbm, hid_hbm, gffn_hbm, gup_hbm, gattn_hbm,
    gq_hbm, gk_hbm, gv_hbm, ngrad_ref,
    tokens, wq, wk, wv, wo, wu, wd, cot,
    nin, q, k, v, att, lse, own1, got1, own2, got2, got3, middle, hid, slope, gffn, gattn, gatt, gk, gv,
    stage, acc, load_sem, save_sem, stage_sem, send_sem, recv_sem,
):
    rows = tokens.shape[0]
    chunks = rows // CHUNK
    pairs = q.shape[1] // LANES
    inner = hid.shape[1]
    peer = {"tensor": 1 - lax.axis_index("tensor")}

    def load(index, source, target):
        return pltpu.make_async_copy(source, target, load_sem.at[index])

    def save(index, source, target):
        return pltpu.make_async_copy(source, target, save_sem.at[index])

    loads = [
        load(0, tokens_hbm, tokens), load(1, wq_hbm, wq), load(2, wk_hbm, wk), load(3, wv_hbm, wv),
        load(4, wo_hbm, wo), load(5, wu_hbm, wu), load(6, wd_hbm, wd), load(7, cot_hbm, cot),
    ]
    for copy in loads:
        copy.start()

    barrier = pltpu.get_barrier_semaphore()
    pl.semaphore_signal(barrier, inc=1, device_id=peer, device_id_type=MESH)
    pl.semaphore_wait(barrier, 1)

    def rows_of(c):
        return pl.ds(pl.multiple_of(c * CHUNK, CHUNK), CHUNK)

    def exchange(step, c, source, target):
        index = step * chunks + c
        return pltpu.make_async_remote_copy(
            src_ref=source.at[rows_of(c)],
            dst_ref=target.at[rows_of(c)],
            send_sem=send_sem.at[index],
            recv_sem=recv_sem.at[index],
            device_id=peer,
            device_id_type=MESH,
        )

    length = length_ref[0]

    def gain(j):
        return gain_ref[j : j + 1, :]

    def bias(j):
        return bias_ref[j : j + 1, :]

    def blocks(c, body):
        def step(b, carry):
            start = pl.multiple_of(c * CHUNK + b * BLOCK, BLOCK)
            body(start, pl.ds(start, BLOCK))
            return carry

        lax.fori_loop(0, CHUNK // BLOCK, step, 0)

    def real_rows(start):
        index = start + lax.broadcasted_iota(jnp.int32, (BLOCK, 1), 0)
        return jnp.where(index < length, 1.0, 0.0)

    acc[...] = jnp.zeros_like(acc)
    gk[...] = jnp.zeros_like(gk)
    gv[...] = jnp.zeros_like(gv)

    loads[0].wait()

    def project(c, carry):
        def norm_in(start, at):
            hat, _ = normalize(tokens[at, :].astype(F32))
            nin[at, :] = (hat * gain(0) + bias(0)).astype(BF16)

        blocks(c, norm_in)

        @pl.when(c == 0)
        def _():
            loads[1].wait()
            loads[2].wait()
            loads[3].wait()

        at = rows_of(c)
        normed = nin[at, :]
        q[at, :] = (dot(normed, wq[...], NN) * 0.125).astype(BF16)
        k[at, :] = dot(normed, wk[...], NN).astype(BF16)
        v[at, :] = dot(normed, wv[...], NN).astype(BF16)
        return carry

    lax.fori_loop(0, chunks, project, 0)
    save(0, nin, nin_hbm).start()
    loads[4].wait()

    key_bias = jnp.where(lane_index((1, rows)) < length, 0.0, NEG)

    def attend(c, carry):
        at = rows_of(c)

        def pair(p, carry):
            cols = pl.ds(pl.multiple_of(p * LANES, LANES), LANES)
            query, keys, values = q[at, cols], k[:, cols], v[:, cols]
            mixed = []
            logs = lse[at, :]
            for side in range(2):
                scores = dot(head_of_pair(query, side), keys, NT) + key_bias
                top = jnp.max(scores, axis=1, keepdims=True)
                weights = jnp.exp(scores - top)
                total = jnp.sum(weights, axis=1, keepdims=True)
                mixed.append(dot(weights.astype(BF16), values, NN) / total)
                logs = jnp.where(lane_index(logs.shape) == 2 * p + side, top + jnp.log(total), logs)
            lse[at, :] = logs
            att[at, cols] = join_pair(*mixed).astype(BF16)
            return carry

        lax.fori_loop(0, pairs, pair, 0)
        own1[at, :] = dot(att[at, :], wo[...], NN).astype(BF16)
        exchange(0, c, own1, got1).start()
        return carry

    lax.fori_loop(0, chunks, attend, 0)
    save(1, att, att_hbm).start()
    loads[5].wait()
    loads[6].wait()
    save(0, nin, nin_hbm).wait()
    nmid = nin

    def feed(c, carry):
        at = rows_of(c)
        exchange(0, c, own1, got1).wait_recv()

        def norms(start, at):
            hat, _ = normalize(own1[at, :].astype(F32) + got1[at, :].astype(F32))
            mid = tokens[at, :].astype(F32) + (hat * gain(1) + bias(1))
            middle[at, :] = mid
            hat, _ = normalize(mid)
            nmid[at, :] = (hat * gain(2) + bias(2)).astype(BF16)

        blocks(c, norms)
        normed = nmid[at, :]
        width = 512
        for n in range(inner // width):
            cols = pl.ds(n * width, width)
            value, grade = gelu_both(dot(normed, wu[:, cols], NN))
            hid[at, cols] = value.astype(BF16)
            slope[at, cols] = grade.astype(BF16)
        own2[at, :] = dot(hid[at, :], wd[...], NN).astype(BF16)
        exchange(1, c, own2, got2).start()
        return carry

    lax.fori_loop(0, chunks, feed, 0)
    save(2, nmid, nmid_hbm).start()
    save(3, hid, hid_hbm).start()
    loads[7].wait()

    def result_copy(c):
        slot = lax.rem(c, 2)
        return pltpu.make_async_copy(stage.at[slot], result_hbm.at[rows_of(c)], stage_sem.at[slot])

    def feed_back(c, carry):
        at = rows_of(c)
        slot = lax.rem(c, 2)
        exchange(1, c, own2, got2).wait_recv()

        @pl.when(c >= 2)
        def _():
            result_copy(c - 2).wait()

        def norms(start, at):
            hat, scale = normalize(own2[at, :].astype(F32) + got2[at, :].astype(F32))
            out = middle[at, :] + (hat * gain(3) + bias(3))
            stage[slot, pl.ds(pl.multiple_of(start - c * CHUNK, BLOCK), BLOCK), :] = out.astype(BF16)
            grad = cot[at, :].astype(F32) * real_rows(start)
            gffn[at, :] = norm_pull(hat, scale, gain(3), grad).astype(BF16)
            acc[2] += fold_rows(grad * hat)
            acc[5] += fold_rows(grad)

        blocks(c, norms)
        result_copy(c).start()
        grad = gffn[at, :]
        width = 512
        for n in range(inner // width):
            cols = pl.ds(n * width, width)
            wide = dot(grad, wd[cols, :], NT)
            slope[at, cols] = (wide * slope[at, cols].astype(F32)).astype(BF16)
        exchange(1, c, own2, got2).wait_send()
        own2[at, :] = dot(slope[at, :], wu[...], NT).astype(BF16)
        exchange(2, c, own2, got3).start()
        return carry

    lax.fori_loop(0, chunks, feed_back, 0)
    save(4, gffn, gffn_hbm).start()
    save(5, slope, gup_hbm).start()

    def attend_back(c, carry):
        at = rows_of(c)
        exchange(2, c, own2, got3).wait_recv()

        def norms(start, at):
            grad = own2[at, :].astype(F32) + got3[at, :].astype(F32)
            hat, scale = normalize(middle[at, :])
            out = cot[at, :].astype(F32) * real_rows(start)
            mid = out + norm_pull(hat, scale, gain(2), grad)
            acc[1] += fold_rows(grad * hat)
            acc[4] += fold_rows(grad)
            middle[at, :] = mid
            hat, scale = normalize(own1[at, :].astype(F32) + got1[at, :].astype(F32))
            gattn[at, :] = norm_pull(hat, scale, gain(1), mid).astype(BF16)
            acc[0] += fold_rows(mid * hat)
            acc[3] += fold_rows(mid)

        blocks(c, norms)
        gatt[...] = dot(gattn[at, :], wo[...], NT).astype(BF16)

        def pair(p, carry):
            cols = pl.ds(pl.multiple_of(p * LANES, LANES), LANES)
            query, keys, values, grad = q[at, cols], k[:, cols], v[:, cols], gatt[:, cols]
            through = grad.astype(F32) * att[at, cols].astype(F32)
            logs = lse[at, :]
            parts = []
            key_part = value_part = 0.0
            for side in range(2):
                one_query, one_grad = head_of_pair(query, side), head_of_pair(grad, side)
                log = jnp.sum(
                    jnp.where(lane_index(logs.shape) == 2 * p + side, logs, 0.0), axis=1, keepdims=True
                )
                weights = jnp.exp(dot(one_query, keys, NT) + key_bias - log)
                shift = jnp.sum(head_of_pair(through, side), axis=1, keepdims=True)
                slopes = (weights * (dot(one_grad, values, NT) - shift)).astype(BF16)
                parts.append(dot(slopes, keys, NN))
                key_part = key_part + dot(slopes, one_query, TN)
                value_part = value_part + dot(weights.astype(BF16), one_grad, TN)
            q[at, cols] = (join_pair(*parts) * 0.125).astype(BF16)
            gk[:, cols] += key_part
            gv[:, cols] += value_part
            return carry

        lax.fori_loop(0, pairs, pair, 0)
        return carry

    lax.fori_loop(0, chunks, attend_back, 0)
    k[...] = gk[...].astype(BF16)
    v[...] = gv[...].astype(BF16)
    tail = [
        save(6, middle, gmid_hbm), save(7, gattn, gattn_hbm), save(8, q, gq_hbm), save(9, k, gk_hbm), save(10, v, gv_hbm),
    ]
    for copy in tail:
        copy.start()
    ngrad_ref[...] = jnp.zeros_like(ngrad_ref)
    for j in range(6):
        ngrad_ref[j : j + 1, :] = jnp.sum(acc[j], axis=0, keepdims=True)
    save(1, att, att_hbm).wait()
    save(2, nmid, nmid_hbm).wait()
    save(3, hid, hid_hbm).wait()
    save(4, gffn, gffn_hbm).wait()
    save(5, slope, gup_hbm).wait()
    for copy in tail:
        copy.wait()
    for c in range(max(chunks - 2, 0), chunks):
        result_copy(c).wait()

    def drain(c, carry):
        exchange(0, c, own1, got1).wait_send()
        exchange(2, c, own2, got3).wait_send()
        return carry

    lax.fori_loop(0, chunks, drain, 0)


def run_layer(lengths, tokens, wq, wk, wv, wo, wu, wd, gains, biases, cot):
    rows, width = tokens.shape
    local, inner = wq.shape[1], wu.shape[1]
    chunks = rows // CHUNK
    shape = jax.ShapeDtypeStruct
    anywhere = pl.BlockSpec(memory_space=pl.ANY)
    vmem = pl.BlockSpec(memory_space=pltpu.VMEM)
    wide = (rows, width)
    thin = (rows, local)
    outs = [
        shape(wide, BF16), shape(wide, F32), shape(wide, BF16), shape(thin, BF16), shape(wide, BF16),
        shape((rows, inner), BF16), shape(wide, BF16), shape((rows, inner), BF16), shape(wide, BF16),
        shape(thin, BF16), shape(thin, BF16), shape(thin, BF16), shape((8, width), F32),
    ]
    scratch = [
        pltpu.VMEM(wide, BF16), pltpu.VMEM(wq.shape, BF16), pltpu.VMEM(wk.shape, BF16), pltpu.VMEM(wv.shape, BF16),
        pltpu.VMEM(wo.shape, BF16), pltpu.VMEM(wu.shape, BF16), pltpu.VMEM(wd.shape, BF16), pltpu.VMEM(wide, BF16),
        pltpu.VMEM(wide, BF16), pltpu.VMEM(thin, BF16), pltpu.VMEM(thin, BF16), pltpu.VMEM(thin, BF16),
        pltpu.VMEM(thin, BF16), pltpu.VMEM((rows, LANES), F32),
        pltpu.VMEM(wide, BF16), pltpu.VMEM(wide, BF16), pltpu.VMEM(wide, BF16), pltpu.VMEM(wide, BF16),
        pltpu.VMEM(wide, BF16), pltpu.VMEM(wide, F32), pltpu.VMEM((rows, inner), BF16), pltpu.VMEM((rows, inner), BF16),
        pltpu.VMEM(wide, BF16), pltpu.VMEM(wide, BF16), pltpu.VMEM((CHUNK, local), BF16),
        pltpu.VMEM(thin, F32), pltpu.VMEM(thin, F32),
        pltpu.VMEM((2, CHUNK, width), BF16), pltpu.VMEM((6, 8, width), F32),
        pltpu.SemaphoreType.DMA((8,)), pltpu.SemaphoreType.DMA((11,)), pltpu.SemaphoreType.DMA((2,)),
        pltpu.SemaphoreType.DMA((3 * chunks,)), pltpu.SemaphoreType.DMA((3 * chunks,)),
    ]
    return pl.pallas_call(
        layer_kernel,
        out_shape=outs,
        in_specs=[pl.BlockSpec(memory_space=pltpu.SMEM)] + [anywhere] * 7 + [vmem, vmem, anywhere],
        out_specs=[anywhere] * 12 + [vmem],
        scratch_shapes=scratch,
        compiler_params=pltpu.CompilerParams(
            collective_id=0, has_side_effects=True, vmem_limit_bytes=61 * 1024 * 1024
        ),
        name="layer",
    )(lengths, tokens, wq, wk, wv, wo, wu, wd, gains, biases, cot)


def pair_sum(part):
    other = lax.ppermute(part, "tensor", [(0, 1), (1, 0)])
    return part.astype(F32) + other.astype(F32)


def scatter_sum(grad, dp_size):
    index = lax.axis_index("dp")
    width = grad.shape[1]
    rows = grad.shape[0] // dp_size
    held = grad
    bit = 1
    while bit < dp_size:
        blocks = held.reshape(-1, 2, rows, width)
        side = (index // bit) % 2
        keep = lax.dynamic_index_in_dim(blocks, side, 1, keepdims=False)
        give = lax.dynamic_index_in_dim(blocks, 1 - side, 1, keepdims=False)
        come = lax.ppermute(give.astype(BF16), "dp", [(i, i ^ bit) for i in range(dp_size)])
        held = (keep.astype(F32) + come.astype(F32)).reshape(-1, width)
        bit *= 2
    return held


def on_device(tokens, lengths, wq, wk, wv, wo, wu, wd, gains, biases, cot):
    result, gmid, nin, att, nmid, hid, gffn, gup, gattn, gq, gk, gv, ngrad = run_layer(
        lengths, tokens, wq, wk, wv, wo, wu, wd, gains, biases, cot
    )
    part = dot(gq, wq, NT) + dot(gk, wk, NT) + dot(gv, wv, NT)
    grad = pair_sum(part.astype(BF16))
    hat, scale = normalize(tokens.astype(F32))
    input_grad = (gmid + norm_pull(hat, scale, gains[0:1], grad)).astype(BF16)
    gain_in, bias_in = jnp.sum(grad * hat, axis=0, keepdims=True), jnp.sum(grad, axis=0, keepdims=True)
    norms = jnp.concatenate([gain_in, ngrad[:3], bias_in, ngrad[3:6]])
    dp_size = lax.axis_size("dp")
    up = scatter_sum(dot(nmid, gup, TN), dp_size)
    down = scatter_sum(dot(gffn, hid, TN), dp_size).T
    out = scatter_sum(dot(gattn, att, TN), dp_size).T
    query = scatter_sum(dot(nin, gq, TN), dp_size)
    key = scatter_sum(dot(nin, gk, TN), dp_size)
    value = scatter_sum(dot(nin, gv, TN), dp_size)
    norm_sum = scatter_sum(norms.T, dp_size).T
    return result, input_grad, query, key, value, out, up, down, norm_sum[:4], norm_sum[4:]


def solution(mesh):
    in_specs = (
        P("dp", None), P("dp"), P(None, "tensor"), P(None, "tensor"), P(None, "tensor"), P("tensor", None),
        P(None, "tensor"), P("tensor", None), P(), P(), P("dp", None),
    )
    out_specs = (
        P("dp", None), P("dp", None), P("dp", "tensor"), P("dp", "tensor"), P("dp", "tensor"), P("tensor", "dp"),
        P("dp", "tensor"), P("tensor", "dp"), P(None, "dp"), P(None, "dp"),
    )
    return jax.shard_map(on_device, mesh=mesh, in_specs=in_specs, out_specs=out_specs, check_vma=False)
```

time: 495 us -> 361 us (0.73); the launches traced: 486 us -> 360 us
  Pallas kernels: 0 us -> 171 us
  matrix products: 139 us -> 24.3 us
  waiting for transfers between devices: 163 us -> 83.6 us
  other arithmetic: 99.7 us -> 27 us
  local copies, waits for them, and re-layouts: 43.4 us -> 18.2 us
    pallas_call x0 -> x1, Pallas kernels: none -> 171 us  [run_layer(): pl.pallas_call(layer_kernel, out_shape=outs, in_specs=[pl.BlockSpec(memor...]
    dot_general x30 -> x9, matrix products: 139 us -> 24.3 us  [dot(): return lax.dot_general(left, right, dims, preferred_element_type=F32)]
    ppermute x4 -> x1, waiting for transfers between devices: 102 us -> 0.01 us  [pair_sum(): other = lax.ppermute(part, 'tensor', [(0, 1), (1, 0)])]
    reduce_sum x17 -> x3, other arithmetic: 50.9 us -> 5.08 us  [the longest x1 4.05 us: on_device(): jnp.sum(grad * hat, axis=0, keepdims=True)]
    convert_element_type x5 -> x1, other arithmetic: 28.5 us -> 4.42 us  [on_device(): input_grad = (gmid + norm_pull(hat, scale, gains[0:1], grad)).astype(BF16)]
    ppermute x28, waiting for transfers between devices: 60.9 us -> 83.6 us  [scatter_sum(): lax.ppermute(give.astype(BF16), 'dp', [(i, i ^ bit) for i in range(dp_siz...]
    unnamed x152 -> x50, local copies, waits for them, and re-layouts: 30.3 us -> 8.06 us
    ppermute x4 -> x1, starting transfers between devices: 7.32 us -> 0.74 us  [pair_sum(): other = lax.ppermute(part, 'tensor', [(0, 1), (1, 0)])]
  transfers between devices with their start and end apart: 32 -> 29, of which waited for: 19 -> 15; matrix products, arithmetic and copies ran while one was open for 36% -> 16% of each run, Pallas kernels for 0% -> 0%
where the time goes in v2:
time: 361 us; the launch traced here: 360 us
  Pallas kernels  171 us (47%)
  waiting for transfers between devices  83.6 us (23%)
  starting transfers between devices  34.1 us (9%)
  other arithmetic  27 us (7%)
  matrix products  24.3 us (7%)
  local copies, waits for them, and re-layouts  18.2 us (5%)
    pallas_call x1, Pallas kernels, run_layer(): pl.pallas_call(layer_kernel, out_shape=outs, in_specs=[pl.BlockSpec(memor...  171 us
    ppermute x28, waiting for transfers between devices, scatter_sum(): lax.ppermute(give.astype(BF16), 'dp', [(i, i ^ bit) for i in range(dp_siz...  83.6 us
    ppermute x28, starting transfers between devices, scatter_sum(): lax.ppermute(give.astype(BF16), 'dp', [(i, i ^ bit) for i in range(dp_siz...  33.3 us
    dot_general x9, matrix products, dot(): return lax.dot_general(left, right, dims, preferred_element_type=F32)  24.3 us
    add x21, other arithmetic, scatter_sum(): held = (keep.astype(F32) + come.astype(F32)).reshape(-1, width)  13.1 us
    convert_element_type x27, local copies, waits for them, and re-layouts, scatter_sum(): give.astype(BF16)  8.67 us
    unnamed x50, local copies, waits for them, and re-layouts  8.06 us
  transfers between devices with their start and end apart: 29, of which 15 were waited for; matrix products, arithmetic and copies ran while one was open for 16% of the time, Pallas kernels for 0%

profile of v2, /device:TPU:0, one launch (start us, length us, event | category | flops | bytes accessed | tf_op | source)
XLA Modules:
  0.0 360.3 jit_solution(6368704974878213259)
XLA Ops:
  1.3 171.2 %layer.1 = (bf16[1024,1024]{1,0:T(8,128)(2,1)}, f32[1024,1024]{1,0:T(8,128)}, bf16[1024,1024]{1,0:T(8,128)(2,1)}, bf16[1024,512]{1,0:T(8,128)(2,1)}, bf16[1024,1...) custom-call(s32[1]{0:T(128)S(6)} %copy.44.length_ref, ...), custom_call_target="tpu_custom_call" | custom-call | tf_op jit(solution)/shard_map/layer/pallas_call | solution.py:367
  172.5 3.3 fusion.49
  187.3 2.6 add_convert_fusion
  192.1 5.0 %fusion.50 = f32[1024,2048]{1,0:T(8,128)S(1)} fusion(bf16[1024,1024]{1,0:T(8,128)(2,1)S(1)} %copy-done.20, bf16[1024,2048]{1,0:T(8,128)(2,1)S(1)} %copy-done.18), kind=kOutput, calls=%fused_computation.117 | convolution fusion | flops 4294967296 | bytes 14680064 | tf_op jit(solution)/shard_map/dot_general | solution.py:27
  198.8 3.6 %copy-done.17 = bf16[1024,2048]{1,0:T(8,128)(2,1)S(1)} copy-done((bf16[1024,2048]{1,0:T(8,128)(2,1)S(1)}, bf16[1024,2048]{1,0:T(8,128)(2,1)}, u32[]{:S(2)}) %copy-start.17) | copy-done | bytes 4194328
  202.4 7.0 %fusion.51 = f32[1024,2048]{1,0:T(8,128)} fusion(bf16[1024,1024]{1,0:T(8,128)(2,1)S(1)} %copy-done.19, bf16[1024,2048]{1,0:T(8,128)(2,1)S(1)} %copy-done.17), kind=kOutput, calls=%fused_computation.118 | convolution fusion | flops 4294967296 | bytes 14680064 | tf_op jit(solution)/shard_map/dot_general | solution.py:27
  210.2 4.0 %fusion.16 = bf16[8,64,2048]{2,1,0:T(8,128)(2,1)} fusion(f32[8,2,64,2048]{3,2,1,0:T(8,128)} %bitcast.184, s32[]{:T(128)S(6)} %select_n.188), kind=kLoop, calls=%fused_computation.24 | loop fusion | bytes 4194308 | tf_op jit(solution)/shard_map/convert_element_type | solution.py:396
  222.4 4.5 %collective-permute-done.14 = bf16[4,64,512]{2,1,0:T(8,128)(2,1)S(1)} collective-permute-done((bf16[4,64,512]{2,1,0:T(8,128)(2,1)S(1)}, bf16[4,64,512]{2,1,0:T(8,128)(2,1)S(1)}, u32[]{:S(2)}, u32[]{:S(2)}) %collective-permute-start.14) | collective-permute-done | bytes 262176 | tf_op jit(solution)/shard_map/ppermute | solution.py:396
  228.5 4.0 %collective-permute-done.2 = bf16[4,64,512]{2,1,0:T(8,128)(2,1)S(1)} collective-permute-done((bf16[4,64,512]{2,1,0:T(8,128)(2,1)S(1)}, bf16[4,64,512]{2,1,0:T(8,128)(2,1)S(1)}, u32[]{:S(2)}, u32[]{:S(2)}) %collective-permute-start.2) | collective-permute-done | bytes 262176 | tf_op jit(solution)/shard_map/ppermute | solution.py:396
  234.2 4.0 %collective-permute-done.6 = bf16[4,64,512]{2,1,0:T(8,128)(2,1)S(1)} collective-permute-done((bf16[4,64,512]{2,1,0:T(8,128)(2,1)S(1)}, bf16[4,64,512]{2,1,0:T(8,128)(2,1)S(1)}, u32[]{:S(2)}, u32[]{:S(2)}) %collective-permute-start.6) | collective-permute-done | bytes 262176 | tf_op jit(solution)/shard_map/ppermute | solution.py:396
  239.8 3.0 collective-permute-done.10
  245.1 4.1 %collective-permute-done.3 = bf16[2,64,512]{2,1,0:T(8,128)(2,1)S(1)} collective-permute-done((bf16[2,64,512]{2,1,0:T(8,128)(2,1)S(1)}, bf16[2,64,512]{2,1,0:T(8,128)(2,1)S(1)}, u32[]{:S(2)}, u32[]{:S(2)}) %collective-permute-start.3) | collective-permute-done | bytes 131104 | tf_op jit(solution)/shard_map/ppermute | solution.py:396
  251.8 2.9 collective-permute-start.16
  254.7 2.3 collective-permute-start.4
  267.6 4.0 %fusion.10 = (f32[1024]{0:T(1024)S(1)}, f32[1024]{0:T(1024)S(1)}, f32[1024]{0:T(1024)S(1)}, f32[1024]{0:T(1024)S(1)}) fusion(bf16[1024,1024]{1,0:T(8,128)(2,1)S(1)} %copy-done, bf16[1024,1024]{1,0:T(8,128)(2,1)} %collective-permute-done, bf16[1024,1024]{1,0:T(8,128)(2,1)} %add_convert_fusion, f32[1024]{0:T(1024)S(1)} %add_rsqrt_fusion, ...), kind=kLoop, calls=%fused_computation.12 | loop fusion | flops 13627392 | bytes 6320128 | tf_op jit(solution)/shard_map/reduce_sum | solution.py:410
  271.9 3.4 bitcast_add_fusion.1
  277.1 3.4 bitcast_add_fusion
  282.9 18.8 %collective-permute-done.26 = bf16[4,64,8]{1,2,0:T(8,128)(2,1)S(1)} collective-permute-done((bf16[4,64,8]{1,2,0:T(8,128)(2,1)S(1)}, bf16[4,64,8]{1,2,0:T(8,128)(2,1)S(1)}, u32[]{:S(2)}, u32[]{:S(2)}) %collective-permute-start.26) | collective-permute-done | bytes 4128 | tf_op jit(solution)/shard_map/ppermute | solution.py:396
  301.7 3.5 collective-permute-start.27
  307.4 4.4 %fusion.9 = bf16[1024,1024]{1,0:T(8,128)(2,1)} fusion(f32[1024,1024]{1,0:T(8,128)S(1)} %copy-done.2, bf16[1024,1024]{1,0:T(8,128)(2,1)S(1)} %copy-done, bf16[1024,1024]{1,0:T(8,128)(2,1)} %collective-permute-done, bf16[1024,1024]{1,0:T(8,128)(2,1)} %add_convert_fusion, f32[1024]{0:T(1024)S(1)} %get-tuple-element.44, f32[1024]{0:T(1024)S(1)} %get-tuple-element.45, ...), kind=kLoop, calls=%fused_computation.11 | loop fusion | flops 13631488 | bytes 12603392 | tf_op jit(solution)/shard_map/convert_element_type | solution.py:409
  314.8 8.9 %collective-permute-done.22 = bf16[4,64,2048]{2,1,0:T(8,128)(2,1)S(1)} collective-permute-done((bf16[4,64,2048]{2,1,0:T(8,128)(2,1)S(1)}, bf16[4,64,2048]{2,1,0:T(8,128)(2,1)S(1)}, u32[]{:S(2)}, u32[]{:S(2)}) %collective-permute-start.22) | collective-permute-done | bytes 1048608 | tf_op jit(solution)/shard_map/ppermute | solution.py:396
  324.1 3.5 collective-permute-start.23
  328.5 16.6 %collective-permute-done.23 = bf16[2,64,2048]{2,1,0:T(8,128)(2,1)S(1)} collective-permute-done((bf16[2,64,2048]{2,1,0:T(8,128)(2,1)S(1)}, bf16[2,64,2048]{2,1,0:T(8,128)(2,1)S(1)}, u32[]{:S(2)}, u32[]{:S(2)}) %collective-permute-start.23) | collective-permute-done | bytes 524320 | tf_op jit(solution)/shard_map/ppermute | solution.py:396
  346.2 12.0 %collective-permute-done.24 = bf16[1,64,2048]{2,1,0:T(8,128)(2,1)S(1)} collective-permute-done((bf16[1,64,2048]{2,1,0:T(8,128)(2,1)S(1)}, bf16[1,64,2048]{2,1,0:T(8,128)(2,1)S(1)}, u32[]{:S(2)}, u32[]{:S(2)}) %collective-permute-start.24) | collective-permute-done | bytes 262176 | tf_op jit(solution)/shard_map/ppermute | solution.py:396
  (163 shorter events, 58.3 us)
Async XLA Ops:
  176.8 37.5 %collective-permute-start.13 = (bf16[8,64,512]{2,1,0:T(8,128)(2,1)}, bf16[8,64,512]{2,1,0:T(8,128)(2,1)}, u32[]{:S(2)}, u32[]{:S(2)}) collective-permute-start(bf16[8,64,512]{2,1,0:T(8,128)(2,1)} %fusion.24), channel_id=1, source_target_pairs={{0,2},{2,0},{4,6},{6,4},{8,10},{10,8},{12,14},{14,12},{16,18},{18,... | collective-permute-start | bytes 1572872 | tf_op jit(solution)/shard_map/ppermute | solution.py:396
  179.6 36.1 %collective-permute-start.1 = (bf16[8,64,512]{2,1,0:T(8,128)(2,1)}, bf16[8,64,512]{2,1,0:T(8,128)(2,1)}, u32[]{:S(2)}, u32[]{:S(2)}) collective-permute-start(bf16[8,64,512]{2,1,0:T(8,128)(2,1)} %fusion.21), channel_id=1, source_target_pairs={{0,2},{2,0},{4,6},{6,4},{8,10},{10,8},{12,14},{14,12},{16,18},{18,... | collective-permute-start | bytes 1572872 | tf_op jit(solution)/shard_map/ppermute | solution.py:396
  181.5 36.2 %collective-permute-start.5 = (bf16[8,64,512]{2,1,0:T(8,128)(2,1)S(1)}, bf16[8,64,512]{2,1,0:T(8,128)(2,1)}, u32[]{:S(2)}, u32[]{:S(2)}) collective-permute-start(bf16[8,64,512]{2,1,0:T(8,128)(2,1)S(1)} %fusion.22), channel_id=1, source_target_pairs={{0,2},{2,0},{4,6},{6,4},{8,10},{10,8},{12,14},{14,12},{16,18},{18,... | collective-permute-start | bytes 1572872 | tf_op jit(solution)/shard_map/ppermute | solution.py:396
  184.1 36.4 %collective-permute-start.9 = (bf16[8,64,512]{2,1,0:T(8,128)(2,1)S(1)}, bf16[8,64,512]{2,1,0:T(8,128)(2,1)}, u32[]{:S(2)}, u32[]{:S(2)}) collective-permute-start(bf16[8,64,512]{2,1,0:T(8,128)(2,1)S(1)} %fusion.23), channel_id=1, source_target_pairs={{0,2},{2,0},{4,6},{6,4},{8,10},{10,8},{12,14},{14,12},{16,18},{18,... | collective-permute-start | bytes 1572872 | tf_op jit(solution)/shard_map/ppermute | solution.py:396
  190.0 77.6 %collective-permute-start = (bf16[1024,1024]{1,0:T(8,128)(2,1)}, bf16[1024,1024]{1,0:T(8,128)(2,1)}, u32[]{:S(2)}, u32[]{:S(2)}) collective-permute-start(bf16[1024,1024]{1,0:T(8,128)(2,1)} %add_convert_fusion), channel_id=1, source_target_pairs={{0,1},{1,0},{2,3},{3,2},{4,5},{5,4},{6,7},{7,6},{8,9},{9,8},{10,11... | collective-permute-start | bytes 6291464 | tf_op jit(solution)/shard_map/ppermute | solution.py:381
  214.2 57.7 %collective-permute-start.17 = (bf16[8,64,2048]{2,1,0:T(8,128)(2,1)}, bf16[8,64,2048]{2,1,0:T(8,128)(2,1)}, u32[]{:S(2)}, u32[]{:S(2)}) collective-permute-start(bf16[8,64,2048]{2,1,0:T(8,128)(2,1)} %fusion.15), channel_id=1, source_target_pairs={{0,2},{2,0},{4,6},{6,4},{8,10},{10,8},{12,14},{14,12},{16,18},{18,... | collective-permute-start | bytes 6291464 | tf_op jit(solution)/shard_map/ppermute | solution.py:396
  215.7 61.4 %collective-permute-start.21 = (bf16[8,64,2048]{2,1,0:T(8,128)(2,1)}, bf16[8,64,2048]{2,1,0:T(8,128)(2,1)}, u32[]{:S(2)}, u32[]{:S(2)}) collective-permute-start(bf16[8,64,2048]{2,1,0:T(8,128)(2,1)} %fusion.16), channel_id=1, source_target_pairs={{0,2},{2,0},{4,6},{6,4},{8,10},{10,8},{12,14},{14,12},{16,18},{18,... | collective-permute-start | bytes 6291464 | tf_op jit(solution)/shard_map/ppermute | solution.py:396
  217.7 9.2 %collective-permute-start.14 = (bf16[4,64,512]{2,1,0:T(8,128)(2,1)S(1)}, bf16[4,64,512]{2,1,0:T(8,128)(2,1)S(1)}, u32[]{:S(2)}, u32[]{:S(2)}) collective-permute-start(bf16[4,64,512]{2,1,0:T(8,128)(2,1)S(1)} %fusion.28), channel_id=1, source_target_pairs={{0,4},{2,6},{4,0},{6,2},{8,12},{10,14},{12,8},{14,10},{16,20},{18,... | collective-permute-start | bytes 786440 | tf_op jit(solution)/shard_map/ppermute | solution.py:396
  220.5 12.0 %collective-permute-start.2 = (bf16[4,64,512]{2,1,0:T(8,128)(2,1)S(1)}, bf16[4,64,512]{2,1,0:T(8,128)(2,1)S(1)}, u32[]{:S(2)}, u32[]{:S(2)}) collective-permute-start(bf16[4,64,512]{2,1,0:T(8,128)(2,1)S(1)} %fusion.25), channel_id=1, source_target_pairs={{0,4},{2,6},{4,0},{6,2},{8,12},{10,14},{12,8},{14,10},{16,20},{18,... | collective-permute-start | bytes 786440 | tf_op jit(solution)/shard_map/ppermute | solution.py:396
  226.9 11.2 %collective-permute-start.6 = (bf16[4,64,512]{2,1,0:T(8,128)(2,1)S(1)}, bf16[4,64,512]{2,1,0:T(8,128)(2,1)S(1)}, u32[]{:S(2)}, u32[]{:S(2)}) collective-permute-start(bf16[4,64,512]{2,1,0:T(8,128)(2,1)S(1)} %fusion.26), channel_id=1, source_target_pairs={{0,4},{2,6},{4,0},{6,2},{8,12},{10,14},{12,8},{14,10},{16,20},{18,... | collective-permute-start | bytes 786440 | tf_op jit(solution)/shard_map/ppermute | solution.py:396
  232.6 10.3 %collective-permute-start.10 = (bf16[4,64,512]{2,1,0:T(8,128)(2,1)S(1)}, bf16[4,64,512]{2,1,0:T(8,128)(2,1)S(1)}, u32[]{:S(2)}, u32[]{:S(2)}) collective-permute-start(bf16[4,64,512]{2,1,0:T(8,128)(2,1)S(1)} %fusion.27), channel_id=1, source_target_pairs={{0,4},{2,6},{4,0},{6,2},{8,12},{10,14},{12,8},{14,10},{16,20},{18,... | collective-permute-start | bytes 786440 | tf_op jit(solution)/shard_map/ppermute | solution.py:396
  238.2 6.4 %collective-permute-start.15 = (bf16[2,64,512]{2,1,0:T(8,128)(2,1)S(1)}, bf16[2,64,512]{2,1,0:T(8,128)(2,1)S(1)}, u32[]{:S(2)}, u32[]{:S(2)}) collective-permute-start(bf16[2,64,512]{2,1,0:T(8,128)(2,1)S(1)} %fusion.32), channel_id=1, source_target_pairs={{0,8},{2,10},{4,12},{6,14},{8,0},{10,2},{12,4},{14,6},{16,24},{18,... | collective-permute-start | bytes 393224 | tf_op jit(solution)/shard_map/ppermute | solution.py:396
  242.9 6.4 %collective-permute-start.3 = (bf16[2,64,512]{2,1,0:T(8,128)(2,1)S(1)}, bf16[2,64,512]{2,1,0:T(8,128)(2,1)S(1)}, u32[]{:S(2)}, u32[]{:S(2)}) collective-permute-start(bf16[2,64,512]{2,1,0:T(8,128)(2,1)S(1)} %fusion.29), channel_id=1, source_target_pairs={{0,8},{2,10},{4,12},{6,14},{8,0},{10,2},{12,4},{14,6},{16,24},{18,... | collective-permute-start | bytes 393224 | tf_op jit(solution)/shard_map/ppermute | solution.py:396
  244.6 7.2 %collective-permute-start.7 = (bf16[2,64,512]{2,1,0:T(8,128)(2,1)S(1)}, bf16[2,64,512]{2,1,0:T(8,128)(2,1)S(1)}, u32[]{:S(2)}, u32[]{:S(2)}) collective-permute-start(bf16[2,64,512]{2,1,0:T(8,128)(2,1)S(1)} %fusion.30), channel_id=1, source_target_pairs={{0,8},{2,10},{4,12},{6,14},{8,0},{10,2},{12,4},{14,6},{16,24},{18,... | collective-permute-start | bytes 393224 | tf_op jit(solution)/shard_map/ppermute | solution.py:396
  251.8 7.5 %collective-permute-start.16 = (bf16[1,64,512]{2,1,0:T(8,128)(2,1)S(1)}, bf16[1,64,512]{2,1,0:T(8,128)(2,1)S(1)}, u32[]{:S(2)}, u32[]{:S(2)}) collective-permute-start(bf16[1,64,512]{2,1,0:T(8,128)(2,1)S(1)} %dynamic-slice_convert_fusion.14), channel_id=1, source_target_pairs={{0,16},{2,18},{4,20},{6,22},{8,24},{10,26},{12,28},{14,30},{16,0},... | collective-permute-start | bytes 196616 | tf_op jit(solution)/shard_map/ppermute | solution.py:396
  254.7 6.7 %collective-permute-start.4 = (bf16[1,64,512]{2,1,0:T(8,128)(2,1)S(1)}, bf16[1,64,512]{2,1,0:T(8,128)(2,1)S(1)}, u32[]{:S(2)}, u32[]{:S(2)}) collective-permute-start(bf16[1,64,512]{2,1,0:T(8,128)(2,1)S(1)} %dynamic-slice_convert_fusion.17), channel_id=1, source_target_pairs={{0,16},{2,18},{4,20},{6,22},{8,24},{10,26},{12,28},{14,30},{16,0},... | collective-permute-start | bytes 196616 | tf_op jit(solution)/shard_map/ppermute | solution.py:396
  271.8 8.8 %collective-permute-start.25 = (bf16[8,64,8]{1,2,0:T(8,128)(2,1)S(1)}, bf16[8,64,8]{1,2,0:T(8,128)(2,1)S(1)}, u32[]{:S(2)}, u32[]{:S(2)}) collective-permute-start(bf16[8,64,8]{1,2,0:T(8,128)(2,1)S(1)} %bitcast.218), channel_id=1, source_target_pairs={{0,2},{2,0},{4,6},{6,4},{8,10},{10,8},{12,14},{14,12},{16,18},{18,... | collective-permute-start | bytes 24584 | tf_op jit(solution)/shard_map/ppermute | solution.py:396
  275.5 36.9 %collective-permute-start.18 = (bf16[4,64,2048]{2,1,0:T(8,128)(2,1)S(1)}, bf16[4,64,2048]{2,1,0:T(8,128)(2,1)S(1)}, u32[]{:S(2)}, u32[]{:S(2)}) collective-permute-start(bf16[4,64,2048]{2,1,0:T(8,128)(2,1)S(1)} %fusion.17), channel_id=1, source_target_pairs={{0,4},{2,6},{4,0},{6,2},{8,12},{10,14},{12,8},{14,10},{16,20},{18,... | collective-permute-start | bytes 3145736 | tf_op jit(solution)/shard_map/ppermute | solution.py:396
  280.6 21.1 %collective-permute-start.26 = (bf16[4,64,8]{1,2,0:T(8,128)(2,1)S(1)}, bf16[4,64,8]{1,2,0:T(8,128)(2,1)S(1)}, u32[]{:S(2)}, u32[]{:S(2)}) collective-permute-start(bf16[4,64,8]{1,2,0:T(8,128)(2,1)S(1)} %fusion.37), channel_id=1, source_target_pairs={{0,4},{2,6},{4,0},{6,2},{8,12},{10,14},{12,8},{14,10},{16,20},{18,... | collective-permute-start | bytes 12296 | tf_op jit(solution)/shard_map/ppermute | solution.py:396
  281.6 42.2 %collective-permute-start.22 = (bf16[4,64,2048]{2,1,0:T(8,128)(2,1)S(1)}, bf16[4,64,2048]{2,1,0:T(8,128)(2,1)S(1)}, u32[]{:S(2)}, u32[]{:S(2)}) collective-permute-start(bf16[4,64,2048]{2,1,0:T(8,128)(2,1)S(1)} %fusion.18), channel_id=1, source_target_pairs={{0,4},{2,6},{4,0},{6,2},{8,12},{10,14},{12,8},{14,10},{16,20},{18,... | collective-permute-start | bytes 3145736 | tf_op jit(solution)/shard_map/ppermute | solution.py:396
  312.8 14.9 %collective-permute-start.19 = (bf16[2,64,2048]{2,1,0:T(8,128)(2,1)S(1)}, bf16[2,64,2048]{2,1,0:T(8,128)(2,1)S(1)}, u32[]{:S(2)}, u32[]{:S(2)}) collective-permute-start(bf16[2,64,2048]{2,1,0:T(8,128)(2,1)S(1)} %fusion.19), channel_id=1, source_target_pairs={{0,8},{2,10},{4,12},{6,14},{8,0},{10,2},{12,4},{14,6},{16,24},{18,... | collective-permute-start | bytes 1572872 | tf_op jit(solution)/shard_map/ppermute | solution.py:396
  324.1 20.9 %collective-permute-start.23 = (bf16[2,64,2048]{2,1,0:T(8,128)(2,1)S(1)}, bf16[2,64,2048]{2,1,0:T(8,128)(2,1)S(1)}, u32[]{:S(2)}, u32[]{:S(2)}) collective-permute-start(bf16[2,64,2048]{2,1,0:T(8,128)(2,1)S(1)} %fusion.20), channel_id=1, source_target_pairs={{0,8},{2,10},{4,12},{6,14},{8,0},{10,2},{12,4},{14,6},{16,24},{18,... | collective-permute-start | bytes 1572872 | tf_op jit(solution)/shard_map/ppermute | solution.py:396
  327.8 17.5 %collective-permute-start.20 = (bf16[1,64,2048]{2,1,0:T(8,128)(2,1)S(1)}, bf16[1,64,2048]{2,1,0:T(8,128)(2,1)S(1)}, u32[]{:S(2)}, u32[]{:S(2)}) collective-permute-start(bf16[1,64,2048]{2,1,0:T(8,128)(2,1)S(1)} %dynamic-slice_convert_fusion.5), channel_id=1, source_target_pairs={{0,16},{2,18},{4,20},{6,22},{8,24},{10,26},{12,28},{14,30},{16,0},... | collective-permute-start | bytes 786440 | tf_op jit(solution)/shard_map/ppermute | solution.py:396
  345.3 12.9 %collective-permute-start.24 = (bf16[1,64,2048]{2,1,0:T(8,128)(2,1)S(1)}, bf16[1,64,2048]{2,1,0:T(8,128)(2,1)S(1)}, u32[]{:S(2)}, u32[]{:S(2)}) collective-permute-start(bf16[1,64,2048]{2,1,0:T(8,128)(2,1)S(1)} %dynamic-slice_convert_fusion.4), channel_id=1, source_target_pairs={{0,16},{2,18},{4,20},{6,22},{8,24},{10,26},{12,28},{14,30},{16,0},... | collective-permute-start | bytes 786440 | tf_op jit(solution)/shard_map/ppermute | solution.py:396
  (29 other events, 185.2 us)

commit v3 on v2

--- a/solution.py
+++ b/solution.py
@@ -21,6 +21,10 @@
 TN = (((0,), (0,)), ((), ()))
 ROOT = 0.7978845608028654
 CUBE = 0.044715
+VMEM_BYTES = 61 * 1024 * 1024
+SLOTS = {
+    (2, 0): 0, (3, 0): 1, (0, 1): 4, (0, 2): 7, (0, 3): 10, (1, 1): 9, (1, 2): 12, (1, 3): 15, (2, 1): 14,
+}
 
 
 def dot(left, right, dims):
@@ -68,16 +72,18 @@
 
 
 def layer_kernel(
+    dp_size,
     length_ref, tokens_hbm, wq_hbm, wk_hbm, wv_hbm, wo_hbm, wu_hbm, wd_hbm, gain_ref, bias_ref, cot_hbm,
-    result_hbm, gmid_hbm, nin_hbm, att_hbm, nmid_hbm, hid_hbm, gffn_hbm, gup_hbm, gattn_hbm,
-    gq_hbm, gk_hbm, gv_hbm, ngrad_ref,
+    result_hbm, ingrad_hbm, nin_hbm, up_ref, down_ref, attn_ref, norm_ref,
     tokens, wq, wk, wv, wo, wu, wd, cot,
     nin, q, k, v, att, lse, own1, got1, own2, got2, got3, middle, hid, slope, gffn, gattn, gatt, gk, gv,
-    stage, acc, load_sem, save_sem, stage_sem, send_sem, recv_sem,
+    stage, acc, norm_held, norm_box, norm_peer,
+    load_sem, save_sem, stage_sem, send_sem, recv_sem, give_sem, take_sem, free_sem,
 ):
     rows = tokens.shape[0]
     chunks = rows // CHUNK
-    pairs = q.shape[1] // LANES
+    local = q.shape[1]
+    pairs = local // LANES
     inner = hid.shape[1]
     peer = {"tensor": 1 - lax.axis_index("tensor")}
 
@@ -94,9 +100,135 @@
     for copy in loads:
         copy.start()
 
+    levels = dp_size.bit_length() - 1
+    me = lax.axis_index("dp")
+    partner, keep, give, half = [], [], [], []
+    base, size = 0, dp_size
+    for level in range(levels):
+        bit = lax.rem(me // (1 << level), 2)
+        partner.append({"dp": me + (1 << level) * (1 - 2 * bit)})
+        size //= 2
+        keep.append(base + bit * size)
+        give.append(base + (1 - bit) * size)
+        half.append(size)
+        base = keep[-1]
+
+    def position(index):
+        return sum(lax.rem(index // (1 << b), 2) * (1 << (levels - 1 - b)) for b in range(levels))
+
     barrier = pltpu.get_barrier_semaphore()
-    pl.semaphore_signal(barrier, inc=1, device_id=peer, device_id_type=MESH)
-    pl.semaphore_wait(barrier, 1)
+    for other in [peer] + partner:
+        pl.semaphore_signal(barrier, inc=1, device_id=other, device_id_type=MESH)
+    pl.semaphore_wait(barrier, levels + 1)
+
+    width = tokens.shape[1]
+    blk = width // dp_size
+    wide = 1024
+    down_units = inner // wide
+    units = 2 * down_units + 2
+    norm_unit = units
+
+    def held(unit):
+        if unit < down_units:
+            return wd.at[pl.ds(unit * width, width), :]
+        if unit < 2 * down_units:
+            return wu.at[:, pl.ds((unit - down_units) * wide, wide)]
+        if unit < units:
+            return hid.at[:, pl.ds((unit - 2 * down_units) * wide, wide)]
+        return norm_held
+
+    def inbox(unit, level):
+        if unit == norm_unit:
+            return norm_box.at[pl.ds(8 * (dp_size - 2 * half[level]), 8 * half[level]), :]
+        count = half[level] * blk
+        if unit >= 2 * down_units:
+            start = width - 2 * count
+            return slope.at[pl.ds(start, count), pl.ds((unit - 2 * down_units) * wide, wide)]
+        if level == 0:
+            room = got2 if unit < down_units else tokens
+            return room.at[pl.ds((unit % down_units) * count, count), :]
+        if level == 1:
+            return gffn.at[pl.ds(unit * count, count), :]
+        start = width // 4 - 2 * count
+        return tokens.at[pl.ds(2 * down_units * start + unit * count, count), :]
+
+    def block_of(unit):
+        return 8 if unit == norm_unit else blk
+
+    def hop(unit, level):
+        rows_each = block_of(unit)
+        index = unit * levels + level
+        start = pl.multiple_of(give[level] * rows_each, 8)
+        return pltpu.make_async_remote_copy(
+            src_ref=held(unit).at[pl.ds(start, half[level] * rows_each), :],
+            dst_ref=inbox(unit, level),
+            send_sem=give_sem.at[index],
+            recv_sem=take_sem.at[index],
+            device_id=partner[level],
+            device_id_type=MESH,
+        )
+
+    def release(level, phase):
+        pl.semaphore_signal(
+            free_sem.at[2 * level + phase], inc=1, device_id=partner[level], device_id_type=MESH
+        )
+
+    def send(unit, level):
+        if unit == 0 or unit == 2 * down_units:
+            pl.semaphore_wait(free_sem.at[2 * level + (0 if unit == 0 else 1)], 1)
+        hop(unit, level).start()
+
+    def final(unit):
+        if unit < down_units:
+            return down_ref.at[:, pl.ds(unit * wide, wide)]
+        if unit < 2 * down_units:
+            return up_ref.at[:, pl.ds((unit - down_units) * wide, wide)]
+        if unit < units:
+            return attn_ref.at[:, pl.ds((unit - 2 * down_units) * wide, wide)]
+        return norm_ref
+
+    def take(unit, level):
+        hop(unit, level).wait_recv()
+        rows_each = block_of(unit)
+        count = half[level] * rows_each
+        step_rows = min(count, 32)
+        mine, came = held(unit), inbox(unit, level)
+        last = level == levels - 1
+        target = final(unit)
+
+        def add(b, carry):
+            here = pl.multiple_of(b * step_rows, step_rows)
+            there = pl.multiple_of(keep[level] * rows_each + b * step_rows, 8)
+            total = mine[pl.ds(there, step_rows), :].astype(F32) + came[pl.ds(here, step_rows), :].astype(F32)
+            if last:
+                target[pl.ds(here, step_rows), :] = total
+            else:
+                mine[pl.ds(there, step_rows), :] = total.astype(mine.dtype)
+            return carry
+
+        lax.fori_loop(0, count // step_rows, add, 0)
+        if unit == 2 * down_units - 1 and level == 0:
+            for other in range(2, levels):
+                release(other, 0)
+        if not last:
+            send(unit, level + 1)
+
+    def weight_grad(left, right, targets):
+        span = 256
+
+        def part(j, carry):
+            cols = pl.ds(pl.multiple_of(j * span, span), span)
+            grad = dot(left[:, cols], right[...], TN)
+            for i in range(span // blk):
+                start = pl.multiple_of(position(j * (span // blk) + i) * blk, 8)
+                piece = grad[i * blk : (i + 1) * blk].astype(BF16)
+                done = 0
+                for ref, count in targets:
+                    ref[pl.ds(start, blk), :] = piece[:, done : done + count]
+                    done += count
+            return carry
+
+        lax.fori_loop(0, width // span, part, 0)
 
     def rows_of(c):
         return pl.ds(pl.multiple_of(c * CHUNK, CHUNK), CHUNK)
@@ -189,7 +321,6 @@
         return carry
 
     lax.fori_loop(0, chunks, attend, 0)
-    save(1, att, att_hbm).start()
     loads[5].wait()
     loads[6].wait()
     save(0, nin, nin_hbm).wait()
@@ -208,9 +339,9 @@
 
         blocks(c, norms)
         normed = nmid[at, :]
-        width = 512
-        for n in range(inner // width):
-            cols = pl.ds(n * width, width)
+        span = 512
+        for n in range(inner // span):
+            cols = pl.ds(n * span, span)
             value, grade = gelu_both(dot(normed, wu[:, cols], NN))
             hid[at, cols] = value.astype(BF16)
             slope[at, cols] = grade.astype(BF16)
@@ -219,8 +350,6 @@
         return carry
 
     lax.fori_loop(0, chunks, feed, 0)
-    save(2, nmid, nmid_hbm).start()
-    save(3, hid, hid_hbm).start()
     loads[7].wait()
 
     def result_copy(c):
@@ -248,19 +377,43 @@
         blocks(c, norms)
         result_copy(c).start()
         grad = gffn[at, :]
-        width = 512
-        for n in range(inner // width):
-            cols = pl.ds(n * width, width)
-            wide = dot(grad, wd[cols, :], NT)
-            slope[at, cols] = (wide * slope[at, cols].astype(F32)).astype(BF16)
+        span = 512
+        for n in range(inner // span):
+            cols = pl.ds(n * span, span)
+            grown = dot(grad, wd[cols, :], NT)
+            slope[at, cols] = (grown * slope[at, cols].astype(F32)).astype(BF16)
         exchange(1, c, own2, got2).wait_send()
         own2[at, :] = dot(slope[at, :], wu[...], NT).astype(BF16)
         exchange(2, c, own2, got3).start()
         return carry
 
     lax.fori_loop(0, chunks, feed_back, 0)
-    save(4, gffn, gffn_hbm).start()
-    save(5, slope, gup_hbm).start()
+    release(0, 0)
+
+    weight_grad(gffn, hid, [(held(u), wide) for u in range(down_units)])
+    release(1, 0)
+    for u in range(down_units):
+        send(u, 0)
+    weight_grad(nmid, slope, [(held(u), wide) for u in range(down_units, 2 * down_units)])
+    for level in range(levels):
+        release(level, 1)
+    for u in range(down_units, 2 * down_units):
+        send(u, 0)
+    nin_back = pltpu.make_async_copy(nin_hbm, nin, save_sem.at[1])
+    nin_back.start()
+    for u in range(down_units):
+        take(u, 0)
+
+    agenda, later = {}, []
+    for u in range(2 * down_units):
+        for level in range(0 if u >= down_units else 1, levels):
+            slot = SLOTS.get((u, level), chunks * pairs)
+            if slot < chunks * pairs:
+                agenda.setdefault(slot, []).append((u, level))
+            else:
+                later.append((u, level))
+
+    tokens_back = pltpu.make_async_copy(tokens_hbm, own1, save_sem.at[2])
 
     def attend_back(c, carry):
         at = rows_of(c)
@@ -280,9 +433,24 @@
             acc[3] += fold_rows(mid)
 
         blocks(c, norms)
+
+        @pl.when(c == chunks - 1)
+        def _():
+            pl.semaphore_signal(free_sem.at[2 * levels], inc=1, device_id=peer, device_id_type=MESH)
+            for done in range(chunks):
+                exchange(0, done, own1, got1).wait_send()
+            tokens_back.start()
+
         gatt[...] = dot(gattn[at, :], wo[...], NT).astype(BF16)
 
         def pair(p, carry):
+            for slot, work in agenda.items():
+
+                @pl.when(c * pairs + p == slot)
+                def _(work=work):
+                    for unit, level in work:
+                        take(unit, level)
+
             cols = pl.ds(pl.multiple_of(p * LANES, LANES), LANES)
             query, keys, values, grad = q[at, cols], k[:, cols], v[:, cols], gatt[:, cols]
             through = grad.astype(F32) * att[at, cols].astype(F32)
@@ -311,45 +479,131 @@
     lax.fori_loop(0, chunks, attend_back, 0)
     k[...] = gk[...].astype(BF16)
     v[...] = gv[...].astype(BF16)
-    tail = [
-        save(6, middle, gmid_hbm), save(7, gattn, gattn_hbm), save(8, q, gq_hbm), save(9, k, gk_hbm), save(10, v, gv_hbm),
-    ]
-    for copy in tail:
-        copy.start()
-    ngrad_ref[...] = jnp.zeros_like(ngrad_ref)
-    for j in range(6):
-        ngrad_ref[j : j + 1, :] = jnp.sum(acc[j], axis=0, keepdims=True)
-    save(1, att, att_hbm).wait()
-    save(2, nmid, nmid_hbm).wait()
-    save(3, hid, hid_hbm).wait()
-    save(4, gffn, gffn_hbm).wait()
-    save(5, slope, gup_hbm).wait()
-    for copy in tail:
-        copy.wait()
+
+    pl.semaphore_wait(free_sem.at[2 * levels], 1)
+
+    def input_part(c, carry):
+        at = rows_of(c)
+        exchange(2, c, own2, got3).wait_send()
+        part = dot(q[at, :], wq[...], NT) + dot(k[at, :], wk[...], NT) + dot(v[at, :], wv[...], NT)
+        own2[at, :] = part.astype(BF16)
+        exchange(3, c, own2, got3).start()
+        return carry
+
+    lax.fori_loop(0, chunks, input_part, 0)
+
+    nin_back.wait()
+    first = hid.at[:, pl.ds(0, local)]
+    second = hid.at[:, pl.ds(local, local)]
+    third = hid.at[:, pl.ds(2 * local, local)]
+    fourth = hid.at[:, pl.ds(3 * local, local)]
+    weight_grad(nin, q, [(first, local)])
+    weight_grad(nin, k, [(second, local)])
+    send(2 * down_units, 0)
+    weight_grad(nin, v, [(third, local)])
+    weight_grad(gattn, att, [(fourth, local)])
+    send(2 * down_units + 1, 0)
+
+    tokens_back.wait()
+    back = own1
+
+    def first_norm(c, carry):
+        def sums(start, at):
+            hat, _ = normalize(back[at, :].astype(F32))
+            grad = own2[at, :].astype(F32)
+            acc[6] += fold_rows(grad * hat)
+            acc[7] += fold_rows(grad)
+
+        blocks(c, sums)
+        return carry
+
+    lax.fori_loop(0, chunks, first_norm, 0)
+    table = jnp.concatenate([jnp.sum(acc[j], axis=0, keepdims=True) for j in (6, 0, 1, 2, 7, 3, 4, 5)])
+    for index in range(dp_size):
+        tile, shift = divmod(index * blk, LANES)
+        piece = table[:, tile * LANES : (tile + 1) * LANES]
+        if shift:
+            piece = pltpu.roll(piece, LANES - shift, 1)
+        spot = int(format(index, "b").zfill(levels)[::-1], 2)
+        norm_held[8 * spot : 8 * spot + 8, :] = piece
+    send(norm_unit, 0)
+
+    def grad_copy(c):
+        slot = lax.rem(c, 2)
+        return pltpu.make_async_copy(stage.at[slot], ingrad_hbm.at[rows_of(c)], stage_sem.at[slot])
+
+    def input_grad(c):
+        at = rows_of(c)
+        slot = c % 2
+        exchange(3, c, own2, got3).wait_recv()
+        (result_copy if c < 2 else grad_copy)(chunks - 2 + c if c < 2 else c - 2).wait()
+
+        def norms(start, at):
+            grad = own2[at, :].astype(F32) + got3[at, :].astype(F32)
+            hat, scale = normalize(back[at, :].astype(F32))
+            total = middle[at, :] + norm_pull(hat, scale, gain(0), grad)
+            stage[slot, pl.ds(pl.multiple_of(start - c * CHUNK, BLOCK), BLOCK), :] = total.astype(BF16)
+
+        blocks(c, norms)
+        grad_copy(c).start()
+
+    late = [2 * down_units, 2 * down_units + 1]
+    plan = [("take", u, l) for u, l in later if l <= 1] + [("take", u, 0) for u in late + [norm_unit]]
+    plan += [("take", u, l) for u, l in later if l > 1]
+    plan += [("take", norm_unit, l) for l in range(1, levels)]
+    plan += [("grad", 0, 0), ("grad", 1, 0), ("take", late[0], 1)]
+    plan += [("take", late[0], 2), ("grad", 2, 0), ("take", late[1], 1), ("take", late[0], 3)]
+    plan += [("take", late[1], l) for l in range(2, levels)]
+    plan += [("take", late[0], l) for l in range(4, levels)]
+    plan += [("grad", c, 0) for c in range(3, chunks)]
+    for kind, which, level in plan:
+        if kind == "take":
+            take(which, level)
+            if which == norm_unit and level == levels - 1:
+                tell = pltpu.make_async_remote_copy(
+                    src_ref=norm_ref,
+                    dst_ref=norm_peer,
+                    send_sem=send_sem.at[4 * chunks],
+                    recv_sem=recv_sem.at[4 * chunks],
+                    device_id=peer,
+                    device_id_type=MESH,
+                )
+                tell.start()
+        else:
+            input_grad(which)
+    tell.wait()
+    row = lax.broadcasted_iota(jnp.int32, norm_ref.shape, 0)
+    norm_ref[...] += jnp.where(lax.rem(row, 4) == 0, norm_peer[...], 0.0)
+
     for c in range(max(chunks - 2, 0), chunks):
-        result_copy(c).wait()
+        grad_copy(c).wait()
 
     def drain(c, carry):
-        exchange(0, c, own1, got1).wait_send()
-        exchange(2, c, own2, got3).wait_send()
+        exchange(3, c, own2, got3).wait_send()
         return carry
 
     lax.fori_loop(0, chunks, drain, 0)
+    for unit in range(units + 1):
+        for level in range(levels):
+            hop(unit, level).wait_send()
 
 
 def run_layer(lengths, tokens, wq, wk, wv, wo, wu, wd, gains, biases, cot):
+    dp_size = lax.axis_size("dp")
     rows, width = tokens.shape
     local, inner = wq.shape[1], wu.shape[1]
     chunks = rows // CHUNK
+    levels = dp_size.bit_length() - 1
+    units = 2 * (inner // 1024) + 2
     shape = jax.ShapeDtypeStruct
     anywhere = pl.BlockSpec(memory_space=pl.ANY)
     vmem = pl.BlockSpec(memory_space=pltpu.VMEM)
     wide = (rows, width)
     thin = (rows, local)
+    blk = width // dp_size
     outs = [
-        shape(wide, BF16), shape(wide, F32), shape(wide, BF16), shape(thin, BF16), shape(wide, BF16),
-        shape((rows, inner), BF16), shape(wide, BF16), shape((rows, inner), BF16), shape(wide, BF16),
-        shape(thin, BF16), shape(thin, BF16), shape(thin, BF16), shape((8, width), F32),
+        shape(wide, BF16), shape(wide, BF16), shape(wide, BF16),
+        shape((blk, inner), F32), shape((blk, inner), F32), shape((blk, 4 * local), F32), shape((8, LANES), F32),
     ]
     scratch = [
         pltpu.VMEM(wide, BF16), pltpu.VMEM(wq.shape, BF16), pltpu.VMEM(wk.shape, BF16), pltpu.VMEM(wv.shape, BF16),
@@ -360,64 +614,34 @@
         pltpu.VMEM(wide, BF16), pltpu.VMEM(wide, F32), pltpu.VMEM((rows, inner), BF16), pltpu.VMEM((rows, inner), BF16),
         pltpu.VMEM(wide, BF16), pltpu.VMEM(wide, BF16), pltpu.VMEM((CHUNK, local), BF16),
         pltpu.VMEM(thin, F32), pltpu.VMEM(thin, F32),
-        pltpu.VMEM((2, CHUNK, width), BF16), pltpu.VMEM((6, 8, width), F32),
-        pltpu.SemaphoreType.DMA((8,)), pltpu.SemaphoreType.DMA((11,)), pltpu.SemaphoreType.DMA((2,)),
-        pltpu.SemaphoreType.DMA((3 * chunks,)), pltpu.SemaphoreType.DMA((3 * chunks,)),
+        pltpu.VMEM((2, CHUNK, width), BF16), pltpu.VMEM((8, 8, width), F32),
+        pltpu.VMEM((8 * dp_size, LANES), F32), pltpu.VMEM((8 * dp_size, LANES), F32), pltpu.VMEM((8, LANES), F32),
+        pltpu.SemaphoreType.DMA((8,)), pltpu.SemaphoreType.DMA((3,)), pltpu.SemaphoreType.DMA((2,)),
+        pltpu.SemaphoreType.DMA((4 * chunks + 1,)), pltpu.SemaphoreType.DMA((4 * chunks + 1,)),
+        pltpu.SemaphoreType.DMA(((units + 1) * levels,)), pltpu.SemaphoreType.DMA(((units + 1) * levels,)),
+        pltpu.SemaphoreType.REGULAR((2 * levels + 1,)),
     ]
     return pl.pallas_call(
-        layer_kernel,
+        functools.partial(layer_kernel, dp_size),
         out_shape=outs,
         in_specs=[pl.BlockSpec(memory_space=pltpu.SMEM)] + [anywhere] * 7 + [vmem, vmem, anywhere],
-        out_specs=[anywhere] * 12 + [vmem],
+        out_specs=[anywhere] * 3 + [vmem] * 4,
         scratch_shapes=scratch,
         compiler_params=pltpu.CompilerParams(
-            collective_id=0, has_side_effects=True, vmem_limit_bytes=61 * 1024 * 1024
+            collective_id=0, has_side_effects=True, vmem_limit_bytes=VMEM_BYTES
         ),
         name="layer",
     )(lengths, tokens, wq, wk, wv, wo, wu, wd, gains, biases, cot)
 
 
-def pair_sum(part):
-    other = lax.ppermute(part, "tensor", [(0, 1), (1, 0)])
-    return part.astype(F32) + other.astype(F32)
-
-
-def scatter_sum(grad, dp_size):
-    index = lax.axis_index("dp")
-    width = grad.shape[1]
-    rows = grad.shape[0] // dp_size
-    held = grad
-    bit = 1
-    while bit < dp_size:
-        blocks = held.reshape(-1, 2, rows, width)
-        side = (index // bit) % 2
-        keep = lax.dynamic_index_in_dim(blocks, side, 1, keepdims=False)
-        give = lax.dynamic_index_in_dim(blocks, 1 - side, 1, keepdims=False)
-        come = lax.ppermute(give.astype(BF16), "dp", [(i, i ^ bit) for i in range(dp_size)])
-        held = (keep.astype(F32) + come.astype(F32)).reshape(-1, width)
-        bit *= 2
-    return held
-
-
 def on_device(tokens, lengths, wq, wk, wv, wo, wu, wd, gains, biases, cot):
-    result, gmid, nin, att, nmid, hid, gffn, gup, gattn, gq, gk, gv, ngrad = run_layer(
+    local = wq.shape[1]
+    result, input_grad, _, up, down, attn, norms = run_layer(
         lengths, tokens, wq, wk, wv, wo, wu, wd, gains, biases, cot
     )
-    part = dot(gq, wq, NT) + dot(gk, wk, NT) + dot(gv, wv, NT)
-    grad = pair_sum(part.astype(BF16))
-    hat, scale = normalize(tokens.astype(F32))
-    input_grad = (gmid + norm_pull(hat, scale, gains[0:1], grad)).astype(BF16)
-    gain_in, bias_in = jnp.sum(grad * hat, axis=0, keepdims=True), jnp.sum(grad, axis=0, keepdims=True)
-    norms = jnp.concatenate([gain_in, ngrad[:3], bias_in, ngrad[3:6]])
-    dp_size = lax.axis_size("dp")
-    up = scatter_sum(dot(nmid, gup, TN), dp_size)
-    down = scatter_sum(dot(gffn, hid, TN), dp_size).T
-    out = scatter_sum(dot(gattn, att, TN), dp_size).T
-    query = scatter_sum(dot(nin, gq, TN), dp_size)
-    key = scatter_sum(dot(nin, gk, TN), dp_size)
-    value = scatter_sum(dot(nin, gv, TN), dp_size)
-    norm_sum = scatter_sum(norms.T, dp_size).T
-    return result, input_grad, query, key, value, out, up, down, norm_sum[:4], norm_sum[4:]
+    blk = up.shape[0]
+    query, key, value, out = (attn[:, i * local : (i + 1) * local] for i in range(4))
+    return result, input_grad, query, key, value, out.T, up, down.T, norms[:4, :blk], norms[4:, :blk]
 
 
 def solution(mesh):

time: 361 us -> 265 us (0.73)
  waiting for transfers between devices: 83.6 us -> 0 us
  Pallas kernels: 171 us -> 253 us
  starting transfers between devices: 34.1 us -> 0 us
  other arithmetic: 27 us -> 0 us
  matrix products: 24.3 us -> 0 us
  local copies, waits for them, and re-layouts: 18.2 us -> 9.42 us
    ppermute x29 -> x0, waiting for transfers between devices: 83.6 us -> none  [the longest x28 83.6 us: scatter_sum(): lax.ppermute(give.astype(BF16), 'dp', [(i, i ^ bit) for i in range(dp_siz...]
    pallas_call x1, Pallas kernels: 171 us -> 253 us  [run_layer(): pl.pallas_call(functools.partial(layer_kernel, dp_size), out_shape=outs,...]
    ppermute x29 -> x0, starting transfers between devices: 34.1 us -> none  [the longest x28 33.3 us: scatter_sum(): lax.ppermute(give.astype(BF16), 'dp', [(i, i ^ bit) for i in range(dp_siz...]
    dot_general x9 -> x0, matrix products: 24.3 us -> none  [dot(): return lax.dot_general(left, right, dims, preferred_element_type=F32)]
    add x21 -> x0, other arithmetic: 13.1 us -> none  [scatter_sum(): held = (keep.astype(F32) + come.astype(F32)).reshape(-1, width)]
    convert_element_type x27 -> x0, local copies, waits for them, and re-layouts: 8.67 us -> none  [scatter_sum(): give.astype(BF16)]
    reduce_sum x3 -> x0, other arithmetic: 5.08 us -> none  [the longest x1 4.05 us: on_device(): jnp.sum(grad * hat, axis=0, keepdims=True)]
    convert_element_type x1 -> x0, other arithmetic: 4.42 us -> none  [on_device(): input_grad = (gmid + norm_pull(hat, scale, gains[0:1], grad)).astype(BF16)]
  transfers between devices with their start and end apart: 29 -> 0, of which waited for: 15 -> 0; matrix products, arithmetic and copies ran while one was open for 16% -> 0% of each run, Pallas kernels for 0% -> 0%
where the time goes in v3:
time: 265 us; the launch traced here: 264 us
  Pallas kernels  253 us (95%)
  local copies, waits for them, and re-layouts  9.42 us (4%)
    pallas_call x1, Pallas kernels, run_layer(): pl.pallas_call(functools.partial(layer_kernel, dp_size), out_shape=outs,...  253 us
    unnamed x10, local copies, waits for them, and re-layouts  6.19 us

profile of v3, /device:TPU:0, one launch (start us, length us, event | category | flops | bytes accessed | tf_op | source)
XLA Modules:
  0.0 264.2 jit_solution(7244699514474774014)
XLA Ops:
  1.3 253.5 %layer.1 = (bf16[1024,1024]{1,0:T(8,128)(2,1)}, bf16[1024,1024]{1,0:T(8,128)(2,1)}, bf16[1024,1024]{1,0:T(8,128)(2,1)}, f32[64,2048]{1,0:T(8,128)}, f32[64,2048]...) custom-call(s32[1]{0:T(128)S(6)} %copy.25.length_ref, bf16[1024,1024]{1,0:T(8,128)(2,1)} %tokens_hbm.1, ...), custom_call_target="tpu_custom_call" | custom-call | tf_op jit(solution)/shard_map/layer/pallas_call | solution.py:624
  254.8 1.3 fusion
  256.1 1.9 slice_bitcast_fusion
  258.0 0.0 copy-start
  258.0 3.2 %copy.26 = bf16[1024,1024]{1,0:T(8,128)(2,1)} copy(bf16[1024,1024]{1,0:T(8,128)(2,1)} %get-tuple-element.38) | data formatting | bytes 4194304
  261.2 0.0 copy-done
  261.2 0.0 copy-start.2
  261.2 0.0 copy-start.1
  261.2 1.3 copy.27
  262.6 0.1 copy-done.2
  262.6 0.8 copy.28
  263.4 0.0 copy-done.1
  263.4 0.8 copy.29
Async XLA Ops:
  258.0 3.2 %copy-start = (bf16[1024,1024]{1,0:T(8,128)(2,1)S(1)}, bf16[1024,1024]{1,0:T(8,128)(2,1)}, u32[]{:S(2)}) copy-start(bf16[1024,1024]{1,0:T(8,128)(2,1)} %get-tuple-element.39) | copy-start | bytes 6291460
  261.2 1.4 copy-start.2
  261.2 2.2 copy-start.1

commit v4 on v3

--- a/solution.py
+++ b/solution.py
@@ -11,7 +11,7 @@
 LANES = 128
 EPS = 1e-05
 CHUNK = 256
-BLOCK = 32
+BLOCK = 128
 NEG = -1000000000.0
 F32 = jnp.float32
 BF16 = jnp.bfloat16
@@ -23,8 +23,14 @@
 CUBE = 0.044715
 VMEM_BYTES = 61 * 1024 * 1024
 SLOTS = {
-    (2, 0): 0, (3, 0): 1, (0, 1): 4, (0, 2): 7, (0, 3): 10, (1, 1): 9, (1, 2): 12, (1, 3): 15, (2, 1): 14,
+    (2, 0): 0, (3, 0): 1, (0, 1): 5, (0, 2): 8, (0, 3): 12, (1, 1): 10, (1, 2): 13, (1, 3): 15, (2, 1): 14, (2, 2): 16,
+    (2, 3): 16, (3, 1): 16,
 }
+EARLY = 17
+PLAN = [
+    ("take", 3, 2), ("grad", 0, 0), ("take", 3, 3), ("take", 4, 1), ("grad", 1, 0), ("take", 4, 2), ("take", 5, 1), ("take", 4, 3),
+    ("grad", 2, 0), ("take", 6, 1), ("take", 5, 2), ("take", 6, 2), ("take", 6, 3), ("take", 5, 3), ("grad", 3, 0),
+]
 
 
 def dot(left, right, dims):
@@ -76,9 +82,9 @@
     length_ref, tokens_hbm, wq_hbm, wk_hbm, wv_hbm, wo_hbm, wu_hbm, wd_hbm, gain_ref, bias_ref, cot_hbm,
     result_hbm, ingrad_hbm, nin_hbm, up_ref, down_ref, attn_ref, norm_ref,
     tokens, wq, wk, wv, wo, wu, wd, cot,
-    nin, q, k, v, att, lse, own1, got1, own2, got2, got3, middle, hid, slope, gffn, gattn, gatt, gk, gv,
+    nin, q, k, v, att, lse, attn_total, own2, got2, got3, middle, hid, slope, gffn, gattn, gatt, gk, gv,
     stage, acc, norm_held, norm_box, norm_peer,
-    load_sem, save_sem, stage_sem, send_sem, recv_sem, give_sem, take_sem, free_sem,
+    token_sem, load_sem, wo_sem, save_sem, stage_sem, send_sem, recv_sem, give_sem, take_sem, free_sem,
 ):
     rows = tokens.shape[0]
     chunks = rows // CHUNK
@@ -93,11 +99,17 @@
     def save(index, source, target):
         return pltpu.make_async_copy(source, target, save_sem.at[index])
 
+    def token_load(c):
+        at = pl.ds(pl.multiple_of(c * CHUNK, CHUNK), CHUNK)
+        return pltpu.make_async_copy(tokens_hbm.at[at], tokens.at[at], token_sem.at[c])
+
+    for c in range(chunks):
+        token_load(c).start()
     loads = [
-        load(0, tokens_hbm, tokens), load(1, wq_hbm, wq), load(2, wk_hbm, wk), load(3, wv_hbm, wv),
-        load(4, wo_hbm, wo), load(5, wu_hbm, wu), load(6, wd_hbm, wd), load(7, cot_hbm, cot),
+        load(0, wq_hbm, wq), load(1, wk_hbm, wk), load(2, wv_hbm, wv),
+        load(3, wo_hbm, wo), load(4, wu_hbm, wu), load(5, wd_hbm, wd), load(6, cot_hbm, cot),
     ]
-    for copy in loads:
+    for copy in loads[:3]:
         copy.start()
 
     levels = dp_size.bit_length() - 1
@@ -123,6 +135,37 @@
 
     width = tokens.shape[1]
     blk = width // dp_size
+
+    core = lax.rem(me, 2)
+    split = local // 2
+    att_peer = gffn.at[:, pl.ds(0, local)]
+
+    def wo_piece(which, side):
+        start = pl.multiple_of(which * split, split)
+        return gffn.at[pl.ds(pl.multiple_of(side * local + start, split), split), pl.ds(width - local, local)]
+
+    def wo_cross(side):
+        return pltpu.make_async_remote_copy(
+            src_ref=wo_hbm.at[pl.ds(pl.multiple_of(core * split, split), split), pl.ds(side * local, local)],
+            dst_ref=wo_piece(core, side),
+            send_sem=wo_sem.at[side],
+            recv_sem=wo_sem.at[2 + side],
+            device_id=peer,
+            device_id_type=MESH,
+        )
+
+    def wo_share(side):
+        return pltpu.make_async_remote_copy(
+            src_ref=wo_piece(core, side),
+            dst_ref=wo_piece(core, side),
+            send_sem=wo_sem.at[4 + side],
+            recv_sem=wo_sem.at[6 + side],
+            device_id=partner[0],
+            device_id_type=MESH,
+        )
+
+    for side in range(2):
+        wo_cross(side).start()
     wide = 1024
     down_units = inner // wide
     units = 2 * down_units + 2
@@ -213,19 +256,18 @@
         if not last:
             send(unit, level + 1)
 
-    def weight_grad(left, right, targets):
+    def weight_grad(left, groups):
         span = 256
 
         def part(j, carry):
-            cols = pl.ds(pl.multiple_of(j * span, span), span)
-            grad = dot(left[:, cols], right[...], TN)
-            for i in range(span // blk):
-                start = pl.multiple_of(position(j * (span // blk) + i) * blk, 8)
-                piece = grad[i * blk : (i + 1) * blk].astype(BF16)
-                done = 0
-                for ref, count in targets:
-                    ref[pl.ds(start, blk), :] = piece[:, done : done + count]
-                    done += count
+            turned = left[:, pl.ds(pl.multiple_of(j * span, span), span)].T
+            starts = [
+                pl.multiple_of(position(j * (span // blk) + i) * blk, 8) for i in range(span // blk)
+            ]
+            for right, ref, at in groups:
+                grad = dot(turned, right[...], NN).astype(BF16)
+                for i, start in enumerate(starts):
+                    ref[pl.ds(start, blk), pl.ds(at, grad.shape[1])] = grad[i * blk : (i + 1) * blk]
             return carry
 
         lax.fori_loop(0, width // span, part, 0)
@@ -268,9 +310,9 @@
     gk[...] = jnp.zeros_like(gk)
     gv[...] = jnp.zeros_like(gv)
 
-    loads[0].wait()
-
     def project(c, carry):
+        token_load(c).wait()
+
         def norm_in(start, at):
             hat, _ = normalize(tokens[at, :].astype(F32))
             nin[at, :] = (hat * gain(0) + bias(0)).astype(BF16)
@@ -279,9 +321,10 @@
 
         @pl.when(c == 0)
         def _():
-            loads[1].wait()
-            loads[2].wait()
-            loads[3].wait()
+            for copy in loads[:3]:
+                copy.wait()
+            for copy in loads[3:]:
+                copy.start()
 
         at = rows_of(c)
         normed = nin[at, :]
@@ -292,7 +335,6 @@
 
     lax.fori_loop(0, chunks, project, 0)
     save(0, nin, nin_hbm).start()
-    loads[4].wait()
 
     key_bias = jnp.where(lane_index((1, rows)) < length, 0.0, NEG)
 
@@ -316,22 +358,37 @@
             return carry
 
         lax.fori_loop(0, pairs, pair, 0)
-        own1[at, :] = dot(att[at, :], wo[...], NN).astype(BF16)
-        exchange(0, c, own1, got1).start()
+        exchange(0, c, att, att_peer).start()
+
+        @pl.when(c == 0)
+        def _():
+            for side in range(2):
+                wo_cross(side).wait_recv()
+                wo_share(side).start()
+
         return carry
 
     lax.fori_loop(0, chunks, attend, 0)
-    loads[5].wait()
-    loads[6].wait()
+    for copy in loads[3:6]:
+        copy.wait()
+    for side in range(2):
+        wo_share(side).wait()
     save(0, nin, nin_hbm).wait()
     nmid = nin
 
     def feed(c, carry):
         at = rows_of(c)
-        exchange(0, c, own1, got1).wait_recv()
+        exchange(0, c, att, att_peer).wait_recv()
+        ours = dot(att[at, :], wo[...], NN).astype(BF16).astype(F32)
+        other = att_peer[at, :]
+        for side in range(2):
+            cols = pl.ds(side * local, local)
+            weight = gffn[pl.ds(side * local, local), pl.ds(width - local, local)]
+            theirs = dot(other, weight, NN).astype(BF16).astype(F32)
+            attn_total[at, cols] = ours[:, side * local : (side + 1) * local] + theirs
 
         def norms(start, at):
-            hat, _ = normalize(own1[at, :].astype(F32) + got1[at, :].astype(F32))
+            hat, _ = normalize(attn_total[at, :])
             mid = tokens[at, :].astype(F32) + (hat * gain(1) + bias(1))
             middle[at, :] = mid
             hat, _ = normalize(mid)
@@ -350,7 +407,7 @@
         return carry
 
     lax.fori_loop(0, chunks, feed, 0)
-    loads[7].wait()
+    loads[6].wait()
 
     def result_copy(c):
         slot = lax.rem(c, 2)
@@ -390,11 +447,14 @@
     lax.fori_loop(0, chunks, feed_back, 0)
     release(0, 0)
 
-    weight_grad(gffn, hid, [(held(u), wide) for u in range(down_units)])
+    def parts(source, first_unit):
+        return [(source.at[:, pl.ds(u * wide, wide)], held(first_unit + u), 0) for u in range(down_units)]
+
+    weight_grad(gffn, parts(hid, 0))
     release(1, 0)
     for u in range(down_units):
         send(u, 0)
-    weight_grad(nmid, slope, [(held(u), wide) for u in range(down_units, 2 * down_units)])
+    weight_grad(nmid, parts(slope, down_units))
     for level in range(levels):
         release(level, 1)
     for u in range(down_units, 2 * down_units):
@@ -404,16 +464,18 @@
     for u in range(down_units):
         take(u, 0)
 
-    agenda, later = {}, []
+    agenda, early, later = {}, [], []
     for u in range(2 * down_units):
         for level in range(0 if u >= down_units else 1, levels):
-            slot = SLOTS.get((u, level), chunks * pairs)
+            slot = SLOTS.get((u, level), EARLY)
             if slot < chunks * pairs:
                 agenda.setdefault(slot, []).append((u, level))
+            elif slot < EARLY:
+                early.append((u, level))
             else:
                 later.append((u, level))
 
-    tokens_back = pltpu.make_async_copy(tokens_hbm, own1, save_sem.at[2])
+    tokens_back = pltpu.make_async_copy(tokens_hbm, got2, save_sem.at[2])
 
     def attend_back(c, carry):
         at = rows_of(c)
@@ -427,7 +489,7 @@
             acc[1] += fold_rows(grad * hat)
             acc[4] += fold_rows(grad)
             middle[at, :] = mid
-            hat, scale = normalize(own1[at, :].astype(F32) + got1[at, :].astype(F32))
+            hat, scale = normalize(attn_total[at, :])
             gattn[at, :] = norm_pull(hat, scale, gain(1), mid).astype(BF16)
             acc[0] += fold_rows(mid * hat)
             acc[3] += fold_rows(mid)
@@ -437,8 +499,6 @@
         @pl.when(c == chunks - 1)
         def _():
             pl.semaphore_signal(free_sem.at[2 * levels], inc=1, device_id=peer, device_id_type=MESH)
-            for done in range(chunks):
-                exchange(0, done, own1, got1).wait_send()
             tokens_back.start()
 
         gatt[...] = dot(gattn[at, :], wo[...], NT).astype(BF16)
@@ -493,19 +553,17 @@
     lax.fori_loop(0, chunks, input_part, 0)
 
     nin_back.wait()
-    first = hid.at[:, pl.ds(0, local)]
-    second = hid.at[:, pl.ds(local, local)]
-    third = hid.at[:, pl.ds(2 * local, local)]
-    fourth = hid.at[:, pl.ds(3 * local, local)]
-    weight_grad(nin, q, [(first, local)])
-    weight_grad(nin, k, [(second, local)])
+    weight_grad(nin, [(q, hid, 0), (k, hid, local), (v, hid, 2 * local)])
     send(2 * down_units, 0)
-    weight_grad(nin, v, [(third, local)])
-    weight_grad(gattn, att, [(fourth, local)])
+    weight_grad(gattn, [(att, hid, 3 * local)])
     send(2 * down_units + 1, 0)
 
+    for u, level in early:
+        take(u, level)
+    for u in (2 * down_units, 2 * down_units + 1):
+        take(u, 0)
     tokens_back.wait()
-    back = own1
+    back = got2
 
     def first_norm(c, carry):
         def sums(start, at):
@@ -527,6 +585,7 @@
         spot = int(format(index, "b").zfill(levels)[::-1], 2)
         norm_held[8 * spot : 8 * spot + 8, :] = piece
     send(norm_unit, 0)
+    take(norm_unit, 0)
 
     def grad_copy(c):
         slot = lax.rem(c, 2)
@@ -548,14 +607,13 @@
         grad_copy(c).start()
 
     late = [2 * down_units, 2 * down_units + 1]
-    plan = [("take", u, l) for u, l in later if l <= 1] + [("take", u, 0) for u in late + [norm_unit]]
-    plan += [("take", u, l) for u, l in later if l > 1]
+    plan = [("take", u, l) for u, l in later]
     plan += [("take", norm_unit, l) for l in range(1, levels)]
-    plan += [("grad", 0, 0), ("grad", 1, 0), ("take", late[0], 1)]
-    plan += [("take", late[0], 2), ("grad", 2, 0), ("take", late[1], 1), ("take", late[0], 3)]
-    plan += [("take", late[1], l) for l in range(2, levels)]
-    plan += [("take", late[0], l) for l in range(4, levels)]
-    plan += [("grad", c, 0) for c in range(3, chunks)]
+    plan += [("take", u, l) for l in range(1, levels) for u in late]
+    plan = PLAN if levels == 4 else plan + [("grad", c, 0) for c in range(chunks)]
+    assert sorted(x for x in plan if x[0] == "take") == sorted(
+        [("take", u, l) for u, l in later] + [("take", u, l) for u in late + [norm_unit] for l in range(1, levels)]
+    )
     for kind, which, level in plan:
         if kind == "take":
             take(which, level)
@@ -579,10 +637,13 @@
         grad_copy(c).wait()
 
     def drain(c, carry):
+        exchange(0, c, att, att_peer).wait_send()
         exchange(3, c, own2, got3).wait_send()
         return carry
 
     lax.fori_loop(0, chunks, drain, 0)
+    for side in range(2):
+        wo_cross(side).wait_send()
     for unit in range(units + 1):
         for level in range(levels):
             hop(unit, level).wait_send()
@@ -610,13 +671,13 @@
         pltpu.VMEM(wo.shape, BF16), pltpu.VMEM(wu.shape, BF16), pltpu.VMEM(wd.shape, BF16), pltpu.VMEM(wide, BF16),
         pltpu.VMEM(wide, BF16), pltpu.VMEM(thin, BF16), pltpu.VMEM(thin, BF16), pltpu.VMEM(thin, BF16),
         pltpu.VMEM(thin, BF16), pltpu.VMEM((rows, LANES), F32),
-        pltpu.VMEM(wide, BF16), pltpu.VMEM(wide, BF16), pltpu.VMEM(wide, BF16), pltpu.VMEM(wide, BF16),
-        pltpu.VMEM(wide, BF16), pltpu.VMEM(wide, F32), pltpu.VMEM((rows, inner), BF16), pltpu.VMEM((rows, inner), BF16),
+        pltpu.VMEM(wide, F32), pltpu.VMEM(wide, BF16), pltpu.VMEM(wide, BF16), pltpu.VMEM(wide, BF16),
+        pltpu.VMEM(wide, F32), pltpu.VMEM((rows, inner), BF16), pltpu.VMEM((rows, inner), BF16),
         pltpu.VMEM(wide, BF16), pltpu.VMEM(wide, BF16), pltpu.VMEM((CHUNK, local), BF16),
         pltpu.VMEM(thin, F32), pltpu.VMEM(thin, F32),
         pltpu.VMEM((2, CHUNK, width), BF16), pltpu.VMEM((8, 8, width), F32),
         pltpu.VMEM((8 * dp_size, LANES), F32), pltpu.VMEM((8 * dp_size, LANES), F32), pltpu.VMEM((8, LANES), F32),
-        pltpu.SemaphoreType.DMA((8,)), pltpu.SemaphoreType.DMA((3,)), pltpu.SemaphoreType.DMA((2,)),
+        pltpu.SemaphoreType.DMA((chunks,)), pltpu.SemaphoreType.DMA((7,)), pltpu.SemaphoreType.DMA((8,)), pltpu.SemaphoreType.DMA((3,)), pltpu.SemaphoreType.DMA((2,)),
         pltpu.SemaphoreType.DMA((4 * chunks + 1,)), pltpu.SemaphoreType.DMA((4 * chunks + 1,)),
         pltpu.SemaphoreType.DMA(((units + 1) * levels,)), pltpu.SemaphoreType.DMA(((units + 1) * levels,)),
         pltpu.SemaphoreType.REGULAR((2 * levels + 1,)),

time: 265 us -> 210 us (0.79)
  Pallas kernels: 253 us -> 199 us
    pallas_call x1, Pallas kernels: 253 us -> 199 us  [run_layer(): pl.pallas_call(functools.partial(layer_kernel, dp_size), out_shape=outs,...]
where the time goes in v4:
time: 210 us
  Pallas kernels  199 us (95%)
  local copies, waits for them, and re-layouts  9.42 us (4%)
    pallas_call x1, Pallas kernels, run_layer(): pl.pallas_call(functools.partial(layer_kernel, dp_size), out_shape=outs,...  199 us
    unnamed x10, local copies, waits for them, and re-layouts  6.19 us

profile of v4, /device:TPU:0, one launch (start us, length us, event | category | flops | bytes accessed | tf_op | source)
XLA Modules:
  0.0 209.6 jit_solution(3219627150783122816)
XLA Ops:
  1.3 198.8 %layer.1 = (bf16[1024,1024]{1,0:T(8,128)(2,1)}, bf16[1024,1024]{1,0:T(8,128)(2,1)}, bf16[1024,1024]{1,0:T(8,128)(2,1)}, f32[64,2048]{1,0:T(8,128)}, f32[64,2048]...) custom-call(s32[1]{0:T(128)S(6)} %copy.25.length_ref, bf16[1024,1024]{1,0:T(8,128)(2,1)} %tokens_hbm.1, ...), custom_call_target="tpu_custom_call" | custom-call | tf_op jit(solution)/shard_map/layer/pallas_call | solution.py:685
  200.1 1.3 fusion
  201.5 1.9 slice_bitcast_fusion
  203.4 0.0 copy-start
  203.4 3.2 %copy.26 = bf16[1024,1024]{1,0:T(8,128)(2,1)} copy(bf16[1024,1024]{1,0:T(8,128)(2,1)} %get-tuple-element.38) | data formatting | bytes 4194304
  206.6 0.0 copy-done
  206.6 0.0 copy-start.2
  206.6 0.0 copy-start.1
  206.6 1.3 copy.27
  207.9 0.1 copy-done.2
  208.0 0.8 copy.28
  208.8 0.0 copy-done.1
  208.8 0.8 copy.29
Async XLA Ops:
  203.4 3.2 %copy-start = (bf16[1024,1024]{1,0:T(8,128)(2,1)S(1)}, bf16[1024,1024]{1,0:T(8,128)(2,1)}, u32[]{:S(2)}) copy-start(bf16[1024,1024]{1,0:T(8,128)(2,1)} %get-tuple-element.39) | copy-start | bytes 6291460
  206.6 1.4 copy-start.2
  206.6 2.2 %copy-start.1 = (f32[64,2048]{1,0:T(8,128)S(1)}, f32[64,2048]{1,0:T(8,128)}, u32[]{:S(2)}) copy-start(f32[64,2048]{1,0:T(8,128)} %get-tuple-element.20) | copy-start | bytes 1572868

commit v5 on v4

--- a/solution.py
+++ b/solution.py
@@ -21,15 +21,14 @@
 TN = (((0,), (0,)), ((), ()))
 ROOT = 0.7978845608028654
 CUBE = 0.044715
+GROUP = 2
+UNROLL = 2
 VMEM_BYTES = 61 * 1024 * 1024
-SLOTS = {
-    (2, 0): 0, (3, 0): 1, (0, 1): 5, (0, 2): 8, (0, 3): 12, (1, 1): 10, (1, 2): 13, (1, 3): 15, (2, 1): 14, (2, 2): 16,
-    (2, 3): 16, (3, 1): 16,
-}
-EARLY = 17
+SLOTS = {(2, 0): 0, (3, 0): 1, (0, 1): 4, (2, 1): 5, (0, 2): 7, (1, 1): 7}
 PLAN = [
-    ("take", 3, 2), ("grad", 0, 0), ("take", 3, 3), ("take", 4, 1), ("grad", 1, 0), ("take", 4, 2), ("take", 5, 1), ("take", 4, 3),
-    ("grad", 2, 0), ("take", 6, 1), ("take", 5, 2), ("take", 6, 2), ("take", 6, 3), ("take", 5, 3), ("grad", 3, 0),
+    0, (3, 1), (2, 2), "project", (0, 3), (1, 2), 1, "out", (4, 0), 2, (5, 0), (6, 0), 3, "norm", (7, 0), (2, 3), (3, 2), (1, 3),
+    ("grad", 0), (6, 1), (3, 3), (4, 1), ("grad", 1), (7, 1), (5, 1), (6, 2), (7, 2), (4, 2), (7, 3), (6, 3), (5, 2), ("grad", 2),
+    (5, 3), (4, 3), ("grad", 3),
 ]
 
 
@@ -114,145 +113,148 @@
 
     levels = dp_size.bit_length() - 1
     me = lax.axis_index("dp")
-    partner, keep, give, half = [], [], [], []
-    base, size = 0, dp_size
-    for level in range(levels):
-        bit = lax.rem(me // (1 << level), 2)
-        partner.append({"dp": me + (1 << level) * (1 - 2 * bit)})
-        size //= 2
-        keep.append(base + bit * size)
-        give.append(base + (1 - bit) * size)
-        half.append(size)
-        base = keep[-1]
-
-    def position(index):
-        return sum(lax.rem(index // (1 << b), 2) * (1 << (levels - 1 - b)) for b in range(levels))
+    bits = [lax.rem(me // (1 << b), 2) for b in range(levels)]
+    partner = [{"dp": me + (1 << b) * (1 - 2 * bits[b])} for b in range(levels)]
+    half = [dp_size >> (level + 1) for level in range(levels)]
+    routes = [list(range(levels)), [0] + list(range(2, levels)) + [1]]
+    keep, give = [], []
+    for route in routes:
+        base, kept, given = 0, [], []
+        for level in range(levels):
+            kept.append(base + bits[route[level]] * half[level])
+            given.append(base + (1 - bits[route[level]]) * half[level])
+            base = kept[-1]
+        keep.append(kept)
+        give.append(given)
+
+    def position(index, way):
+        return sum(lax.rem(index // (1 << b), 2) * half[level] for level, b in enumerate(routes[way]))
+
+    def fixed_position(index, way):
+        return sum((index >> b) % 2 * half[level] for level, b in enumerate(routes[way]))
 
     barrier = pltpu.get_barrier_semaphore()
     for other in [peer] + partner:
         pl.semaphore_signal(barrier, inc=1, device_id=other, device_id_type=MESH)
-    pl.semaphore_wait(barrier, levels + 1)
 
     width = tokens.shape[1]
     blk = width // dp_size
 
-    core = lax.rem(me, 2)
-    split = local // 2
+    split = local // 4
+    mine, far = lax.rem(me, 4), lax.rem(me + 2, 4)
     att_peer = gffn.at[:, pl.ds(0, local)]
 
     def wo_piece(which, side):
-        start = pl.multiple_of(which * split, split)
-        return gffn.at[pl.ds(pl.multiple_of(side * local + start, split), split), pl.ds(width - local, local)]
+        start = pl.multiple_of(side * local + which * split, split)
+        return gffn.at[pl.ds(start, split), pl.ds(width - local, local)]
 
     def wo_cross(side):
         return pltpu.make_async_remote_copy(
-            src_ref=wo_hbm.at[pl.ds(pl.multiple_of(core * split, split), split), pl.ds(side * local, local)],
-            dst_ref=wo_piece(core, side),
+            src_ref=wo_hbm.at[pl.ds(pl.multiple_of(mine * split, split), split), pl.ds(side * local, local)],
+            dst_ref=wo_piece(mine, side),
             send_sem=wo_sem.at[side],
             recv_sem=wo_sem.at[2 + side],
             device_id=peer,
             device_id_type=MESH,
         )
 
-    def wo_share(side):
+    def wo_share(step, side):
+        which = far if step == 2 else mine
         return pltpu.make_async_remote_copy(
-            src_ref=wo_piece(core, side),
-            dst_ref=wo_piece(core, side),
-            send_sem=wo_sem.at[4 + side],
-            recv_sem=wo_sem.at[6 + side],
-            device_id=partner[0],
+            src_ref=wo_piece(which, side),
+            dst_ref=wo_piece(which, side),
+            send_sem=wo_sem.at[4 * step + 4 + side],
+            recv_sem=wo_sem.at[4 * step + 6 + side],
+            device_id=partner[1] if step == 0 else partner[0],
             device_id_type=MESH,
         )
 
-    for side in range(2):
-        wo_cross(side).start()
     wide = 1024
-    down_units = inner // wide
-    units = 2 * down_units + 2
-    norm_unit = units
+    count = inner // wide
+    rows_at = lambda ref, start, size: ref.at[pl.ds(start, size), :]
+    cols_at = lambda ref, start, size: ref.at[:, pl.ds(start, size)]
+    table = [(rows_at(wd, u * width, width), cols_at(down_ref, u * wide, wide), None, 0) for u in range(count)]
+    table += [
+        (cols_at(wu, u * wide, wide), cols_at(up_ref, u * wide, wide), None, 1 if u == 0 else 0) for u in range(count)
+    ]
+    attn_first = 2 * count
+    for start, size, way in ((0, 2 * local, 0), (2 * local, local, 0), (3 * local, local, 1)):
+        table.append((cols_at(hid, start, size), cols_at(attn_ref, start, size), pl.ds(start, size), way))
+    norm_unit = len(table)
+    table.append((norm_held, norm_ref, None, 0))
 
     def held(unit):
-        if unit < down_units:
-            return wd.at[pl.ds(unit * width, width), :]
-        if unit < 2 * down_units:
-            return wu.at[:, pl.ds((unit - down_units) * wide, wide)]
-        if unit < units:
-            return hid.at[:, pl.ds((unit - 2 * down_units) * wide, wide)]
-        return norm_held
+        return table[unit][0]
 
     def inbox(unit, level):
         if unit == norm_unit:
             return norm_box.at[pl.ds(8 * (dp_size - 2 * half[level]), 8 * half[level]), :]
-        count = half[level] * blk
-        if unit >= 2 * down_units:
-            start = width - 2 * count
-            return slope.at[pl.ds(start, count), pl.ds((unit - 2 * down_units) * wide, wide)]
+        size = half[level] * blk
+        if unit >= attn_first:
+            return slope.at[pl.ds(width - 2 * size, size), table[unit][2]]
         if level == 0:
-            room = got2 if unit < down_units else tokens
-            return room.at[pl.ds((unit % down_units) * count, count), :]
+            return rows_at(got2 if unit < count else tokens, (unit % count) * size, size)
         if level == 1:
-            return gffn.at[pl.ds(unit * count, count), :]
-        start = width // 4 - 2 * count
-        return tokens.at[pl.ds(2 * down_units * start + unit * count, count), :]
+            return rows_at(gffn, unit * size, size)
+        return rows_at(tokens, 2 * count * (width // 4 - 2 * size) + unit * size, size)
 
     def block_of(unit):
         return 8 if unit == norm_unit else blk
 
     def hop(unit, level):
+        way = table[unit][3]
         rows_each = block_of(unit)
         index = unit * levels + level
-        start = pl.multiple_of(give[level] * rows_each, 8)
+        start = pl.multiple_of(give[way][level] * rows_each, 8)
         return pltpu.make_async_remote_copy(
             src_ref=held(unit).at[pl.ds(start, half[level] * rows_each), :],
             dst_ref=inbox(unit, level),
             send_sem=give_sem.at[index],
             recv_sem=take_sem.at[index],
-            device_id=partner[level],
+            device_id=partner[routes[way][level]],
             device_id_type=MESH,
         )
 
-    def release(level, phase):
-        pl.semaphore_signal(
-            free_sem.at[2 * level + phase], inc=1, device_id=partner[level], device_id_type=MESH
-        )
+    def credit(unit, level):
+        return free_sem.at[(2 * levels if unit >= attn_first else 0) + 2 * level + table[unit][3]]
+
+    def release(which, level):
+        for way in range(2):
+            same = [u for u in which if table[u][3] == way]
+            if same:
+                pl.semaphore_signal(
+                    credit(same[0], level), inc=len(same), device_id=partner[routes[way][level]], device_id_type=MESH
+                )
 
     def send(unit, level):
-        if unit == 0 or unit == 2 * down_units:
-            pl.semaphore_wait(free_sem.at[2 * level + (0 if unit == 0 else 1)], 1)
+        if unit != norm_unit:
+            pl.semaphore_wait(credit(unit, level), 1)
         hop(unit, level).start()
-
-    def final(unit):
-        if unit < down_units:
-            return down_ref.at[:, pl.ds(unit * wide, wide)]
-        if unit < 2 * down_units:
-            return up_ref.at[:, pl.ds((unit - down_units) * wide, wide)]
-        if unit < units:
-            return attn_ref.at[:, pl.ds((unit - 2 * down_units) * wide, wide)]
-        return norm_ref
 
     def take(unit, level):
         hop(unit, level).wait_recv()
         rows_each = block_of(unit)
-        count = half[level] * rows_each
-        step_rows = min(count, 32)
-        mine, came = held(unit), inbox(unit, level)
+        size = half[level] * rows_each
+        step_rows = min(size, 32)
+        ours, came = held(unit), inbox(unit, level)
         last = level == levels - 1
-        target = final(unit)
+        target = table[unit][1]
+        first = keep[table[unit][3]][level] * rows_each
 
         def add(b, carry):
             here = pl.multiple_of(b * step_rows, step_rows)
-            there = pl.multiple_of(keep[level] * rows_each + b * step_rows, 8)
-            total = mine[pl.ds(there, step_rows), :].astype(F32) + came[pl.ds(here, step_rows), :].astype(F32)
+            there = pl.multiple_of(first + b * step_rows, 8)
+            total = ours[pl.ds(there, step_rows), :].astype(F32) + came[pl.ds(here, step_rows), :].astype(F32)
             if last:
                 target[pl.ds(here, step_rows), :] = total
             else:
-                mine[pl.ds(there, step_rows), :] = total.astype(mine.dtype)
+                ours[pl.ds(there, step_rows), :] = total.astype(ours.dtype)
             return carry
 
-        lax.fori_loop(0, count // step_rows, add, 0)
-        if unit == 2 * down_units - 1 and level == 0:
+        lax.fori_loop(0, size // step_rows, add, 0)
+        if unit == 2 * count - 1 and level == 0:
             for other in range(2, levels):
-                release(other, 0)
+                release(range(2 * count), other)
         if not last:
             send(unit, level + 1)
 
@@ -261,12 +263,10 @@
 
         def part(j, carry):
             turned = left[:, pl.ds(pl.multiple_of(j * span, span), span)].T
-            starts = [
-                pl.multiple_of(position(j * (span // blk) + i) * blk, 8) for i in range(span // blk)
-            ]
-            for right, ref, at in groups:
+            for right, ref, at, way in groups:
                 grad = dot(turned, right[...], NN).astype(BF16)
-                for i, start in enumerate(starts):
+                for i in range(span // blk):
+                    start = pl.multiple_of(position(j * (span // blk) + i, way) * blk, 8)
                     ref[pl.ds(start, blk), pl.ds(at, grad.shape[1])] = grad[i * blk : (i + 1) * blk]
             return carry
 
@@ -307,8 +307,6 @@
         return jnp.where(index < length, 1.0, 0.0)
 
     acc[...] = jnp.zeros_like(acc)
-    gk[...] = jnp.zeros_like(gk)
-    gv[...] = jnp.zeros_like(gv)
 
     def project(c, carry):
         token_load(c).wait()
@@ -319,8 +317,7 @@
 
         blocks(c, norm_in)
 
-        @pl.when(c == 0)
-        def _():
+        if isinstance(c, int):
             for copy in loads[:3]:
                 copy.wait()
             for copy in loads[3:]:
@@ -333,7 +330,11 @@
         v[at, :] = dot(normed, wv[...], NN).astype(BF16)
         return carry
 
-    lax.fori_loop(0, chunks, project, 0)
+    project(0, 0)
+    pl.semaphore_wait(barrier, levels + 1)
+    for side in range(2):
+        wo_cross(side).start()
+    lax.fori_loop(1, chunks, project, 0)
     save(0, nin, nin_hbm).start()
 
     key_bias = jnp.where(lane_index((1, rows)) < length, 0.0, NEG)
@@ -357,14 +358,21 @@
             att[at, cols] = join_pair(*mixed).astype(BF16)
             return carry
 
-        lax.fori_loop(0, pairs, pair, 0)
+        lax.fori_loop(0, pairs, pair, 0, unroll=UNROLL)
         exchange(0, c, att, att_peer).start()
 
         @pl.when(c == 0)
         def _():
             for side in range(2):
                 wo_cross(side).wait_recv()
-                wo_share(side).start()
+                wo_share(0, side).start()
+                wo_share(1, side).start()
+
+        @pl.when(c == chunks - 2)
+        def _():
+            for side in range(2):
+                wo_share(0, side).wait_recv()
+                wo_share(2, side).start()
 
         return carry
 
@@ -372,7 +380,9 @@
     for copy in loads[3:6]:
         copy.wait()
     for side in range(2):
-        wo_share(side).wait()
+        wo_share(0, side).wait_send()
+        wo_share(1, side).wait()
+        wo_share(2, side).wait()
     save(0, nin, nin_hbm).wait()
     nmid = nin
 
@@ -445,35 +455,31 @@
         return carry
 
     lax.fori_loop(0, chunks, feed_back, 0)
-    release(0, 0)
+    release(range(2 * count), 0)
 
     def parts(source, first_unit):
-        return [(source.at[:, pl.ds(u * wide, wide)], held(first_unit + u), 0) for u in range(down_units)]
+        units = range(first_unit, first_unit + count)
+        return [(cols_at(source, i * wide, wide), held(u), 0, table[u][3]) for i, u in enumerate(units)]
 
     weight_grad(gffn, parts(hid, 0))
-    release(1, 0)
-    for u in range(down_units):
+    release(range(2 * count), 1)
+    for u in range(count):
         send(u, 0)
-    weight_grad(nmid, parts(slope, down_units))
+    weight_grad(nmid, parts(slope, count))
     for level in range(levels):
-        release(level, 1)
-    for u in range(down_units, 2 * down_units):
+        release(range(attn_first, norm_unit), level)
+    for u in range(count, 2 * count):
         send(u, 0)
     nin_back = pltpu.make_async_copy(nin_hbm, nin, save_sem.at[1])
     nin_back.start()
-    for u in range(down_units):
+    for u in range(count):
         take(u, 0)
-
-    agenda, early, later = {}, [], []
-    for u in range(2 * down_units):
-        for level in range(0 if u >= down_units else 1, levels):
-            slot = SLOTS.get((u, level), EARLY)
-            if slot < chunks * pairs:
-                agenda.setdefault(slot, []).append((u, level))
-            elif slot < EARLY:
-                early.append((u, level))
-            else:
-                later.append((u, level))
+    gk[...] = jnp.zeros_like(gk)
+    gv[...] = jnp.zeros_like(gv)
+
+    agenda = {}
+    for (u, level), slot in sorted(SLOTS.items(), key=lambda item: item[1]):
+        agenda.setdefault(slot, []).append((u, level))
 
     tokens_back = pltpu.make_async_copy(tokens_hbm, got2, save_sem.at[2])
 
@@ -498,19 +504,12 @@
 
         @pl.when(c == chunks - 1)
         def _():
-            pl.semaphore_signal(free_sem.at[2 * levels], inc=1, device_id=peer, device_id_type=MESH)
+            pl.semaphore_signal(free_sem.at[4 * levels], inc=1, device_id=peer, device_id_type=MESH)
             tokens_back.start()
 
         gatt[...] = dot(gattn[at, :], wo[...], NT).astype(BF16)
 
-        def pair(p, carry):
-            for slot, work in agenda.items():
-
-                @pl.when(c * pairs + p == slot)
-                def _(work=work):
-                    for unit, level in work:
-                        take(unit, level)
-
+        def pair(p):
             cols = pl.ds(pl.multiple_of(p * LANES, LANES), LANES)
             query, keys, values, grad = q[at, cols], k[:, cols], v[:, cols], gatt[:, cols]
             through = grad.astype(F32) * att[at, cols].astype(F32)
@@ -526,66 +525,80 @@
                 shift = jnp.sum(head_of_pair(through, side), axis=1, keepdims=True)
                 slopes = (weights * (dot(one_grad, values, NT) - shift)).astype(BF16)
                 parts.append(dot(slopes, keys, NN))
-                key_part = key_part + dot(slopes, one_query, TN)
-                value_part = value_part + dot(weights.astype(BF16), one_grad, TN)
+                key_part = key_part + dot(one_query, slopes, TN)
+                value_part = value_part + dot(one_grad, weights.astype(BF16), TN)
             q[at, cols] = (join_pair(*parts) * 0.125).astype(BF16)
-            gk[:, cols] += key_part
-            gv[:, cols] += value_part
+            gk[cols, :] += key_part
+            gv[cols, :] += value_part
+
+        def some_pairs(h, carry):
+            for slot, work in agenda.items():
+
+                @pl.when(c * (pairs // GROUP) + h == slot)
+                def _(work=work):
+                    for unit, level in work:
+                        take(unit, level)
+
+            for i in range(GROUP):
+                pair(h * GROUP + i)
             return carry
 
-        lax.fori_loop(0, pairs, pair, 0)
+        lax.fori_loop(0, pairs // GROUP, some_pairs, 0)
         return carry
 
     lax.fori_loop(0, chunks, attend_back, 0)
-    k[...] = gk[...].astype(BF16)
-    v[...] = gv[...].astype(BF16)
-
-    pl.semaphore_wait(free_sem.at[2 * levels], 1)
-
-    def input_part(c, carry):
+    pl.semaphore_wait(free_sem.at[4 * levels], 1)
+    back = got2
+
+    def turn(c):
         at = rows_of(c)
+        k[at, :] = gk[:, at].astype(BF16).T
+        v[at, :] = gv[:, at].astype(BF16).T
+
+    def input_part(c):
+        at = rows_of(c)
+        if c == 0:
+            turn(c)
         exchange(2, c, own2, got3).wait_send()
         part = dot(q[at, :], wq[...], NT) + dot(k[at, :], wk[...], NT) + dot(v[at, :], wv[...], NT)
         own2[at, :] = part.astype(BF16)
         exchange(3, c, own2, got3).start()
-        return carry
-
-    lax.fori_loop(0, chunks, input_part, 0)
-
-    nin_back.wait()
-    weight_grad(nin, [(q, hid, 0), (k, hid, local), (v, hid, 2 * local)])
-    send(2 * down_units, 0)
-    weight_grad(gattn, [(att, hid, 3 * local)])
-    send(2 * down_units + 1, 0)
-
-    for u, level in early:
-        take(u, level)
-    for u in (2 * down_units, 2 * down_units + 1):
-        take(u, 0)
-    tokens_back.wait()
-    back = got2
-
-    def first_norm(c, carry):
-        def sums(start, at):
-            hat, _ = normalize(back[at, :].astype(F32))
-            grad = own2[at, :].astype(F32)
-            acc[6] += fold_rows(grad * hat)
-            acc[7] += fold_rows(grad)
-
-        blocks(c, sums)
-        return carry
-
-    lax.fori_loop(0, chunks, first_norm, 0)
-    table = jnp.concatenate([jnp.sum(acc[j], axis=0, keepdims=True) for j in (6, 0, 1, 2, 7, 3, 4, 5)])
-    for index in range(dp_size):
-        tile, shift = divmod(index * blk, LANES)
-        piece = table[:, tile * LANES : (tile + 1) * LANES]
-        if shift:
-            piece = pltpu.roll(piece, LANES - shift, 1)
-        spot = int(format(index, "b").zfill(levels)[::-1], 2)
-        norm_held[8 * spot : 8 * spot + 8, :] = piece
-    send(norm_unit, 0)
-    take(norm_unit, 0)
+
+    def project_grads():
+        for c in range(1, chunks):
+            turn(c)
+        nin_back.wait()
+        weight_grad(nin, [(q, hid, 0, 0), (k, hid, local, 0), (v, hid, 2 * local, 0)])
+        send(attn_first, 0)
+        send(attn_first + 1, 0)
+
+    def out_grad():
+        weight_grad(gattn, [(att, hid, 3 * local, table[attn_first + 2][3])])
+        send(attn_first + 2, 0)
+
+    def norm_grads():
+        tokens_back.wait()
+
+        def first_norm(c, carry):
+            def sums(start, at):
+                hat, _ = normalize(back[at, :].astype(F32))
+                grad = own2[at, :].astype(F32)
+                acc[6] += fold_rows(grad * hat)
+                acc[7] += fold_rows(grad)
+
+            blocks(c, sums)
+            return carry
+
+        lax.fori_loop(0, chunks, first_norm, 0)
+        sums = jnp.concatenate([jnp.sum(acc[j], axis=0, keepdims=True) for j in (6, 0, 1, 2, 7, 3, 4, 5)])
+        for index in range(dp_size):
+            tile, shift = divmod(index * blk, LANES)
+            piece = sums[:, tile * LANES : (tile + 1) * LANES]
+            if shift:
+                piece = pltpu.roll(piece, LANES - shift, 1)
+            spot = 8 * fixed_position(index, 0)
+            norm_held[spot : spot + 8, :] = piece
+        send(norm_unit, 0)
 
     def grad_copy(c):
         slot = lax.rem(c, 2)
@@ -606,29 +619,36 @@
         blocks(c, norms)
         grad_copy(c).start()
 
-    late = [2 * down_units, 2 * down_units + 1]
-    plan = [("take", u, l) for u, l in later]
-    plan += [("take", norm_unit, l) for l in range(1, levels)]
-    plan += [("take", u, l) for l in range(1, levels) for u in late]
-    plan = PLAN if levels == 4 else plan + [("grad", c, 0) for c in range(chunks)]
-    assert sorted(x for x in plan if x[0] == "take") == sorted(
-        [("take", u, l) for u, l in later] + [("take", u, l) for u in late + [norm_unit] for l in range(1, levels)]
+    tell = pltpu.make_async_remote_copy(
+        src_ref=norm_ref,
+        dst_ref=norm_peer,
+        send_sem=send_sem.at[4 * chunks],
+        recv_sem=recv_sem.at[4 * chunks],
+        device_id=peer,
+        device_id_type=MESH,
     )
-    for kind, which, level in plan:
-        if kind == "take":
-            take(which, level)
-            if which == norm_unit and level == levels - 1:
-                tell = pltpu.make_async_remote_copy(
-                    src_ref=norm_ref,
-                    dst_ref=norm_peer,
-                    send_sem=send_sem.at[4 * chunks],
-                    recv_sem=recv_sem.at[4 * chunks],
-                    device_id=peer,
-                    device_id_type=MESH,
-                )
+    everything = [(u, level) for level in range(levels) for u in range(norm_unit + 1)]
+    early = set(SLOTS) | {(u, 0) for u in range(count)}
+    plan = PLAN
+    if levels != 4:
+        plan = [0, "project", 1, "out", 2, 3, "norm"] + [x for x in everything if x not in early]
+        plan += [("grad", c) for c in range(chunks)]
+    assert sorted(x for x in plan if isinstance(x, tuple) and x[0] != "grad") == sorted(set(everything) - early)
+    for item in plan:
+        if isinstance(item, int):
+            input_part(item)
+        elif item == "project":
+            project_grads()
+        elif item == "out":
+            out_grad()
+        elif item == "norm":
+            norm_grads()
+        elif item[0] == "grad":
+            input_grad(item[1])
+        else:
+            take(*item)
+            if item == (norm_unit, levels - 1):
                 tell.start()
-        else:
-            input_grad(which)
     tell.wait()
     row = lax.broadcasted_iota(jnp.int32, norm_ref.shape, 0)
     norm_ref[...] += jnp.where(lax.rem(row, 4) == 0, norm_peer[...], 0.0)
@@ -644,7 +664,7 @@
     lax.fori_loop(0, chunks, drain, 0)
     for side in range(2):
         wo_cross(side).wait_send()
-    for unit in range(units + 1):
+    for unit in range(norm_unit + 1):
         for level in range(levels):
             hop(unit, level).wait_send()
 
@@ -655,7 +675,7 @@
     local, inner = wq.shape[1], wu.shape[1]
     chunks = rows // CHUNK
     levels = dp_size.bit_length() - 1
-    units = 2 * (inner // 1024) + 2
+    units = 2 * (inner // 1024) + 4
     shape = jax.ShapeDtypeStruct
     anywhere = pl.BlockSpec(memory_space=pl.ANY)
     vmem = pl.BlockSpec(memory_space=pltpu.VMEM)
@@ -674,13 +694,13 @@
         pltpu.VMEM(wide, F32), pltpu.VMEM(wide, BF16), pltpu.VMEM(wide, BF16), pltpu.VMEM(wide, BF16),
         pltpu.VMEM(wide, F32), pltpu.VMEM((rows, inner), BF16), pltpu.VMEM((rows, inner), BF16),
         pltpu.VMEM(wide, BF16), pltpu.VMEM(wide, BF16), pltpu.VMEM((CHUNK, local), BF16),
-        pltpu.VMEM(thin, F32), pltpu.VMEM(thin, F32),
+        pltpu.VMEM((local, rows), F32), pltpu.VMEM((local, rows), F32),
         pltpu.VMEM((2, CHUNK, width), BF16), pltpu.VMEM((8, 8, width), F32),
         pltpu.VMEM((8 * dp_size, LANES), F32), pltpu.VMEM((8 * dp_size, LANES), F32), pltpu.VMEM((8, LANES), F32),
-        pltpu.SemaphoreType.DMA((chunks,)), pltpu.SemaphoreType.DMA((7,)), pltpu.SemaphoreType.DMA((8,)), pltpu.SemaphoreType.DMA((3,)), pltpu.SemaphoreType.DMA((2,)),
+        pltpu.SemaphoreType.DMA((chunks,)), pltpu.SemaphoreType.DMA((7,)), pltpu.SemaphoreType.DMA((16,)), pltpu.SemaphoreType.DMA((3,)), pltpu.SemaphoreType.DMA((2,)),
         pltpu.SemaphoreType.DMA((4 * chunks + 1,)), pltpu.SemaphoreType.DMA((4 * chunks + 1,)),
-        pltpu.SemaphoreType.DMA(((units + 1) * levels,)), pltpu.SemaphoreType.DMA(((units + 1) * levels,)),
-        pltpu.SemaphoreType.REGULAR((2 * levels + 1,)),
+        pltpu.SemaphoreType.DMA((units * levels,)), pltpu.SemaphoreType.DMA((units * levels,)),
+        pltpu.SemaphoreType.REGULAR((4 * levels + 1,)),
     ]
     return pl.pallas_call(
         functools.partial(layer_kernel, dp_size),
@@ -695,14 +715,50 @@
     )(lengths, tokens, wq, wk, wv, wo, wu, wd, gains, biases, cot)
 
 
+def finish_kernel(
+    result_in, ingrad_in, up_in, down_in, attn_in, norm_in, result, ingrad, query, key, value, out, up, down, gain, bias
+):
+    local = query.shape[1]
+    result[...] = result_in[...]
+    ingrad[...] = ingrad_in[...]
+    up[...] = up_in[...]
+    down[...] = down_in[...]
+    for i, ref in enumerate((query, key, value, out)):
+        ref[...] = attn_in[:, i * local : (i + 1) * local]
+    blk = gain.shape[1]
+    gain[...] = norm_in[:4, :blk]
+    bias[...] = norm_in[4:, :blk]
+
+
 def on_device(tokens, lengths, wq, wk, wv, wo, wu, wd, gains, biases, cot):
-    local = wq.shape[1]
+    local, inner = wq.shape[1], wu.shape[1]
     result, input_grad, _, up, down, attn, norms = run_layer(
         lengths, tokens, wq, wk, wv, wo, wu, wd, gains, biases, cot
     )
     blk = up.shape[0]
-    query, key, value, out = (attn[:, i * local : (i + 1) * local] for i in range(4))
-    return result, input_grad, query, key, value, out.T, up, down.T, norms[:4, :blk], norms[4:, :blk]
+    shape = jax.ShapeDtypeStruct
+    steps = 2 if blk % 16 == 0 else 1
+
+    def part(rows, columns):
+        return pl.BlockSpec((rows // steps, columns), lambda i: (i, 0))
+
+    def whole(*dims):
+        return pl.BlockSpec(dims, lambda i: (0, 0))
+
+    rows, width = result.shape
+    result, input_grad, query, key, value, out, up, down, gain, bias = pl.pallas_call(
+        finish_kernel,
+        grid=(steps,),
+        out_shape=[shape(result.shape, BF16), shape(result.shape, BF16)]
+        + [shape((blk, local), F32)] * 4
+        + [shape((blk, inner), F32)] * 2
+        + [shape((4, blk), F32)] * 2,
+        in_specs=[part(rows, width)] * 2 + [part(blk, inner)] * 2 + [part(blk, 4 * local), whole(8, LANES)],
+        out_specs=[part(rows, width)] * 2 + [part(blk, local)] * 4 + [part(blk, inner)] * 2 + [whole(4, blk)] * 2,
+        compiler_params=pltpu.CompilerParams(vmem_limit_bytes=VMEM_BYTES),
+        name="finish",
+    )(result, input_grad, up, down, attn, norms)
+    return result, input_grad, query, key, value, out.T, up, down.T, gain, bias
 
 
 def solution(mesh):

time: 210 us -> 194 us (0.924)
  local copies, waits for them, and re-layouts: 9.42 us -> 0 us
  Pallas kernels: 199 us -> 192 us
    pallas_call x1, Pallas kernels: 199 us -> 187 us  [run_layer(): pl.pallas_call(functools.partial(layer_kernel, dp_size), out_shape=outs,...]
    unnamed x10 -> x0, local copies, waits for them, and re-layouts: 6.19 us -> none
    pallas_call x0 -> x1, Pallas kernels: none -> 4.98 us  [on_device(): pl.pallas_call(finish_kernel, grid=(steps,), out_shape=[shape(result.shap...]
where the time goes in v5:
time: 194 us
  Pallas kernels  192 us (99%)
    pallas_call x1, Pallas kernels, run_layer(): pl.pallas_call(functools.partial(layer_kernel, dp_size), out_shape=outs,...  187 us
    pallas_call x1, Pallas kernels, on_device(): pl.pallas_call(finish_kernel, grid=(steps,), out_shape=[shape(result.shap...  4.98 us

profile of v5, /device:TPU:0, one launch (start us, length us, event | category | flops | bytes accessed | tf_op | source)
XLA Modules:
  0.0 193.7 jit_solution(10798665303077440757)
XLA Ops:
  1.3 187.2 %layer.1 = (bf16[1024,1024]{1,0:T(8,128)(2,1)}, bf16[1024,1024]{1,0:T(8,128)(2,1)}, bf16[1024,1024]{1,0:T(8,128)(2,1)}, f32[64,2048]{1,0:T(8,128)}, f32[64,2048]...) custom-call(s32[1]{0:T(128)S(6)} %copy.21.length_ref, bf16[1024,1024]{1,0:T(8,128)(2,1)} %tokens_hbm.1, ...), custom_call_target="tpu_custom_call" | custom-call | tf_op jit(solution)/shard_map/layer/pallas_call | solution.py:705
  188.5 5.0 %finish.1 = (bf16[1024,1024]{1,0:T(8,128)(2,1)}, bf16[1024,1024]{1,0:T(8,128)(2,1)}, f32[64,512]{1,0:T(8,128)}, f32[64,512]{1,0:T(8,128)}, f32[64,512]{1,0:T(8,1...) custom-call(bf16[1024,1024]{1,0:T(8,128)(2,1)} %get-tuple-element.26, ...), custom_call_target="tpu_custom_call" | custom-call | tf_op jit(solution)/shard_map/finish/pallas_call | solution.py:749

commit v6 on v5

--- a/solution.py
+++ b/solution.py
@@ -10,7 +10,8 @@
 HD = 64
 LANES = 128
 EPS = 1e-05
-CHUNK = 256
+CHUNK = 128
+PROJECT = 256
 BLOCK = 128
 NEG = -1000000000.0
 F32 = jnp.float32
@@ -21,14 +22,15 @@
 TN = (((0,), (0,)), ((), ()))
 ROOT = 0.7978845608028654
 CUBE = 0.044715
-GROUP = 2
 UNROLL = 2
 VMEM_BYTES = 61 * 1024 * 1024
-SLOTS = {(2, 0): 0, (3, 0): 1, (0, 1): 4, (2, 1): 5, (0, 2): 7, (1, 1): 7}
+WAYS = (0, 0, 1, 0, 0, 0, 0, 0)
+SLOTS = {(2, 0): 1, (3, 0): 1, (0, 1): 4, (2, 1): 5, (0, 2): 7, (1, 1): 7}
 PLAN = [
-    0, (3, 1), (2, 2), "project", (0, 3), (1, 2), 1, "out", (4, 0), 2, (5, 0), (6, 0), 3, "norm", (7, 0), (2, 3), (3, 2), (1, 3),
-    ("grad", 0), (6, 1), (3, 3), (4, 1), ("grad", 1), (7, 1), (5, 1), (6, 2), (7, 2), (4, 2), (7, 3), (6, 3), (5, 2), ("grad", 2),
-    (5, 3), (4, 3), ("grad", 3),
+    ("part", 0, 1), ("part", 1, 1), (3, 1), "project", (2, 2), ("part", 2, 2), "out", (4, 0), (5, 0), (1, 2), (0, 3),
+    ("part", 4, 2), ("part", 6, 2), "norm", (6, 0), (8, 0), (7, 0), (3, 2), (2, 3), ("grad", 0), ("grad", 1), (4, 1),
+    (1, 3), ("grad", 2), (5, 1), (8, 1), (4, 2), (8, 2), (3, 3), ("grad", 3), (5, 2), (6, 1), (8, 3), (4, 3), ("grad", 4),
+    (5, 3), (7, 1), (6, 2), ("grad", 5), (7, 2), (6, 3), ("grad", 6), (7, 3), ("grad", 7),
 ]
 
 
@@ -68,7 +70,12 @@
     return jnp.where(low if side == 0 else jnp.logical_not(low), values, jnp.zeros_like(values))
 
 
-def join_pair(first, second):
+def stack_pair(values):
+    return jnp.concatenate([head_of_pair(values, 0), head_of_pair(values, 1)], axis=0)
+
+
+def join_pair(stacked):
+    first, second = jnp.split(stacked, 2, axis=0)
     return jnp.where(lane_index(first.shape) < HD, first, second)
 
 
@@ -79,11 +86,11 @@
 def layer_kernel(
     dp_size,
     length_ref, tokens_hbm, wq_hbm, wk_hbm, wv_hbm, wo_hbm, wu_hbm, wd_hbm, gain_ref, bias_ref, cot_hbm,
-    result_hbm, ingrad_hbm, nin_hbm, up_ref, down_ref, attn_ref, norm_ref,
+    result_hbm, ingrad_hbm, nin_hbm, up_hbm, down_hbm, attn_hbm, norm_ref,
     tokens, wq, wk, wv, wo, wu, wd, cot,
     nin, q, k, v, att, lse, attn_total, own2, got2, got3, middle, hid, slope, gffn, gattn, gatt, gk, gv,
-    stage, acc, norm_held, norm_box, norm_peer,
-    token_sem, load_sem, wo_sem, save_sem, stage_sem, send_sem, recv_sem, give_sem, take_sem, free_sem,
+    stage, acc, up_ref, down_ref, attn_ref, norm_held, norm_box, norm_peer,
+    final_sem, token_sem, load_sem, wo_sem, save_sem, stage_sem, send_sem, recv_sem, give_sem, take_sem, free_sem,
 ):
     rows = tokens.shape[0]
     chunks = rows // CHUNK
@@ -98,11 +105,14 @@
     def save(index, source, target):
         return pltpu.make_async_copy(source, target, save_sem.at[index])
 
+    def span_of(c):
+        return pl.ds(pl.multiple_of(c * PROJECT, PROJECT), PROJECT)
+
     def token_load(c):
-        at = pl.ds(pl.multiple_of(c * CHUNK, CHUNK), CHUNK)
+        at = span_of(c)
         return pltpu.make_async_copy(tokens_hbm.at[at], tokens.at[at], token_sem.at[c])
 
-    for c in range(chunks):
+    for c in range(rows // PROJECT):
         token_load(c).start()
     loads = [
         load(0, wq_hbm, wq), load(1, wk_hbm, wk), load(2, wv_hbm, wv),
@@ -173,15 +183,23 @@
     count = inner // wide
     rows_at = lambda ref, start, size: ref.at[pl.ds(start, size), :]
     cols_at = lambda ref, start, size: ref.at[:, pl.ds(start, size)]
-    table = [(rows_at(wd, u * width, width), cols_at(down_ref, u * wide, wide), None, 0) for u in range(count)]
+    table = [(rows_at(wd, u * width, width), cols_at(down_ref, u * wide, wide), None, WAYS[u]) for u in range(count)]
     table += [
-        (cols_at(wu, u * wide, wide), cols_at(up_ref, u * wide, wide), None, 1 if u == 0 else 0) for u in range(count)
+        (cols_at(wu, u * wide, wide), cols_at(up_ref, u * wide, wide), None, WAYS[count + u]) for u in range(count)
     ]
     attn_first = 2 * count
-    for start, size, way in ((0, 2 * local, 0), (2 * local, local, 0), (3 * local, local, 1)):
-        table.append((cols_at(hid, start, size), cols_at(attn_ref, start, size), pl.ds(start, size), way))
+    for i in range(4):
+        cols = pl.ds(i * local, local)
+        table.append((hid.at[:, cols], attn_ref.at[:, cols], cols, WAYS[attn_first + i]))
     norm_unit = len(table)
     table.append((norm_held, norm_ref, None, 0))
+
+    outputs = [cols_at(down_hbm, u * wide, wide) for u in range(count)]
+    outputs += [cols_at(up_hbm, u * wide, wide) for u in range(count)]
+    outputs += [cols_at(attn_hbm, i * local, local) for i in range(4)]
+
+    def final_copy(unit):
+        return pltpu.make_async_copy(table[unit][1], outputs[unit], final_sem.at[unit])
 
     def held(unit):
         return table[unit][0]
@@ -252,6 +270,8 @@
             return carry
 
         lax.fori_loop(0, size // step_rows, add, 0)
+        if last and unit != norm_unit:
+            final_copy(unit).start()
         if unit == 2 * count - 1 and level == 0:
             for other in range(2, levels):
                 release(range(2 * count), other)
@@ -294,13 +314,13 @@
     def bias(j):
         return bias_ref[j : j + 1, :]
 
-    def blocks(c, body):
+    def blocks(c, body, size=CHUNK):
         def step(b, carry):
-            start = pl.multiple_of(c * CHUNK + b * BLOCK, BLOCK)
+            start = pl.multiple_of(c * size + b * BLOCK, BLOCK)
             body(start, pl.ds(start, BLOCK))
             return carry
 
-        lax.fori_loop(0, CHUNK // BLOCK, step, 0)
+        lax.fori_loop(0, size // BLOCK, step, 0)
 
     def real_rows(start):
         index = start + lax.broadcasted_iota(jnp.int32, (BLOCK, 1), 0)
@@ -308,33 +328,29 @@
 
     acc[...] = jnp.zeros_like(acc)
 
-    def project(c, carry):
+    def query_rows(at):
+        q[at, :] = (dot(nin[at, :], wq[...], NN) * 0.125).astype(BF16)
+
+    def norm_in(start, at):
+        hat, _ = normalize(tokens[at, :].astype(F32))
+        nin[at, :] = (hat * gain(0) + bias(0)).astype(BF16)
+
+    for c in range(rows // PROJECT):
         token_load(c).wait()
-
-        def norm_in(start, at):
-            hat, _ = normalize(tokens[at, :].astype(F32))
-            nin[at, :] = (hat * gain(0) + bias(0)).astype(BF16)
-
-        blocks(c, norm_in)
-
-        if isinstance(c, int):
-            for copy in loads[:3]:
-                copy.wait()
-            for copy in loads[3:]:
-                copy.start()
-
-        at = rows_of(c)
-        normed = nin[at, :]
-        q[at, :] = (dot(normed, wq[...], NN) * 0.125).astype(BF16)
-        k[at, :] = dot(normed, wk[...], NN).astype(BF16)
-        v[at, :] = dot(normed, wv[...], NN).astype(BF16)
-        return carry
-
-    project(0, 0)
+        blocks(c, norm_in, PROJECT)
+    for copy in loads[3:]:
+        copy.start()
     pl.semaphore_wait(barrier, levels + 1)
     for side in range(2):
         wo_cross(side).start()
-    lax.fori_loop(1, chunks, project, 0)
+    for copy in loads[:3]:
+        copy.wait()
+    query_rows(span_of(0))
+    for c in range(rows // (2 * PROJECT)):
+        at = pl.ds(2 * PROJECT * c, 2 * PROJECT)
+        normed = nin[at, :]
+        k[at, :] = dot(normed, wk[...], NN).astype(BF16)
+        v[at, :] = dot(normed, wv[...], NN).astype(BF16)
     save(0, nin, nin_hbm).start()
 
     key_bias = jnp.where(lane_index((1, rows)) < length, 0.0, NEG)
@@ -342,26 +358,31 @@
     def attend(c, carry):
         at = rows_of(c)
 
+        ratio = PROJECT // CHUNK
+
+        @pl.when(jnp.logical_and(lax.rem(c, ratio) == 0, c > 0))
+        def _():
+            query_rows(span_of(c // ratio))
+
         def pair(p, carry):
             cols = pl.ds(pl.multiple_of(p * LANES, LANES), LANES)
-            query, keys, values = q[at, cols], k[:, cols], v[:, cols]
-            mixed = []
+            keys, values = k[:, cols], v[:, cols]
+            scores = dot(stack_pair(q[at, cols]), keys, NT) + key_bias
+            top = jnp.max(scores, axis=1, keepdims=True)
+            weights = jnp.exp(scores - top)
+            total = jnp.sum(weights, axis=1, keepdims=True)
+            mixed = dot(weights.astype(BF16), values, NN) / total
+            first, second = jnp.split(top + jnp.log(total), 2, axis=0)
             logs = lse[at, :]
-            for side in range(2):
-                scores = dot(head_of_pair(query, side), keys, NT) + key_bias
-                top = jnp.max(scores, axis=1, keepdims=True)
-                weights = jnp.exp(scores - top)
-                total = jnp.sum(weights, axis=1, keepdims=True)
-                mixed.append(dot(weights.astype(BF16), values, NN) / total)
-                logs = jnp.where(lane_index(logs.shape) == 2 * p + side, top + jnp.log(total), logs)
-            lse[at, :] = logs
-            att[at, cols] = join_pair(*mixed).astype(BF16)
+            lane = lane_index(logs.shape)
+            lse[at, :] = jnp.where(lane == 2 * p, first, jnp.where(lane == 2 * p + 1, second, logs))
+            att[at, cols] = join_pair(mixed).astype(BF16)
             return carry
 
         lax.fori_loop(0, pairs, pair, 0, unroll=UNROLL)
         exchange(0, c, att, att_peer).start()
 
-        @pl.when(c == 0)
+        @pl.when(c == 2)
         def _():
             for side in range(2):
                 wo_cross(side).wait_recv()
@@ -398,7 +419,9 @@
             attn_total[at, cols] = ours[:, side * local : (side + 1) * local] + theirs
 
         def norms(start, at):
-            hat, _ = normalize(attn_total[at, :])
+            hat, scale = normalize(attn_total[at, :])
+            attn_total[at, :] = hat
+            lse[at, :] = jnp.where(lane_index((BLOCK, LANES)) == 2 * pairs, scale, lse[at, :])
             mid = tokens[at, :].astype(F32) + (hat * gain(1) + bias(1))
             middle[at, :] = mid
             hat, _ = normalize(mid)
@@ -440,6 +463,9 @@
             gffn[at, :] = norm_pull(hat, scale, gain(3), grad).astype(BF16)
             acc[2] += fold_rows(grad * hat)
             acc[5] += fold_rows(grad)
+            hat, scale = normalize(middle[at, :])
+            middle[at, :] = hat
+            lse[at, :] = jnp.where(lane_index((BLOCK, LANES)) == 2 * pairs + 1, scale, lse[at, :])
 
         blocks(c, norms)
         result_copy(c).start()
@@ -489,13 +515,13 @@
 
         def norms(start, at):
             grad = own2[at, :].astype(F32) + got3[at, :].astype(F32)
-            hat, scale = normalize(middle[at, :])
+            hat, scale = middle[at, :], lse[at, 2 * pairs + 1 : 2 * pairs + 2]
             out = cot[at, :].astype(F32) * real_rows(start)
             mid = out + norm_pull(hat, scale, gain(2), grad)
             acc[1] += fold_rows(grad * hat)
             acc[4] += fold_rows(grad)
             middle[at, :] = mid
-            hat, scale = normalize(attn_total[at, :])
+            hat, scale = attn_total[at, :], lse[at, 2 * pairs : 2 * pairs + 1]
             gattn[at, :] = norm_pull(hat, scale, gain(1), mid).astype(BF16)
             acc[0] += fold_rows(mid * hat)
             acc[3] += fold_rows(mid)
@@ -510,71 +536,64 @@
         gatt[...] = dot(gattn[at, :], wo[...], NT).astype(BF16)
 
         def pair(p):
-            cols = pl.ds(pl.multiple_of(p * LANES, LANES), LANES)
-            query, keys, values, grad = q[at, cols], k[:, cols], v[:, cols], gatt[:, cols]
-            through = grad.astype(F32) * att[at, cols].astype(F32)
+            cols = pl.ds(p * LANES, LANES)
+            keys, values, grad = k[:, cols], v[:, cols], gatt[:, cols]
+            query, grads = stack_pair(q[at, cols]), stack_pair(grad)
+            through = stack_pair(grad.astype(F32) * att[at, cols].astype(F32))
+            shift = jnp.sum(through, axis=1, keepdims=True)
             logs = lse[at, :]
-            parts = []
-            key_part = value_part = 0.0
-            for side in range(2):
-                one_query, one_grad = head_of_pair(query, side), head_of_pair(grad, side)
-                log = jnp.sum(
-                    jnp.where(lane_index(logs.shape) == 2 * p + side, logs, 0.0), axis=1, keepdims=True
-                )
-                weights = jnp.exp(dot(one_query, keys, NT) + key_bias - log)
-                shift = jnp.sum(head_of_pair(through, side), axis=1, keepdims=True)
-                slopes = (weights * (dot(one_grad, values, NT) - shift)).astype(BF16)
-                parts.append(dot(slopes, keys, NN))
-                key_part = key_part + dot(one_query, slopes, TN)
-                value_part = value_part + dot(one_grad, weights.astype(BF16), TN)
-            q[at, cols] = (join_pair(*parts) * 0.125).astype(BF16)
-            gk[cols, :] += key_part
-            gv[cols, :] += value_part
-
-        def some_pairs(h, carry):
-            for slot, work in agenda.items():
-
-                @pl.when(c * (pairs // GROUP) + h == slot)
-                def _(work=work):
-                    for unit, level in work:
-                        take(unit, level)
-
-            for i in range(GROUP):
-                pair(h * GROUP + i)
-            return carry
-
-        lax.fori_loop(0, pairs // GROUP, some_pairs, 0)
+            log = jnp.concatenate([logs[:, 2 * p : 2 * p + 1], logs[:, 2 * p + 1 : 2 * p + 2]], axis=0)
+            weights = jnp.exp(dot(query, keys, NT) + key_bias - log)
+            slopes = (weights * (dot(grads, values, NT) - shift)).astype(BF16)
+            q[at, cols] = (join_pair(dot(slopes, keys, NN)) * 0.125).astype(BF16)
+            gk[cols, :] += dot(query, slopes, TN)
+            gv[cols, :] += dot(grads, weights.astype(BF16), TN)
+
+        for slot, work in agenda.items():
+
+            @pl.when(c == slot)
+            def _(work=work):
+                for unit, level in work:
+                    take(unit, level)
+
+        for p in range(pairs):
+            pair(p)
         return carry
 
     lax.fori_loop(0, chunks, attend_back, 0)
     pl.semaphore_wait(free_sem.at[4 * levels], 1)
     back = got2
 
+    turned = set()
+
     def turn(c):
-        at = rows_of(c)
-        k[at, :] = gk[:, at].astype(BF16).T
-        v[at, :] = gv[:, at].astype(BF16).T
-
-    def input_part(c):
-        at = rows_of(c)
-        if c == 0:
+        if c not in turned:
+            turned.add(c)
+            at = rows_of(c)
+            k[at, :] = gk[:, at].astype(BF16).T
+            v[at, :] = gv[:, at].astype(BF16).T
+
+    def input_part(first, number):
+        at = pl.ds(first * CHUNK, number * CHUNK)
+        for c in range(first, first + number):
             turn(c)
-        exchange(2, c, own2, got3).wait_send()
+            exchange(2, c, own2, got3).wait_send()
         part = dot(q[at, :], wq[...], NT) + dot(k[at, :], wk[...], NT) + dot(v[at, :], wv[...], NT)
         own2[at, :] = part.astype(BF16)
-        exchange(3, c, own2, got3).start()
+        for c in range(first, first + number):
+            exchange(3, c, own2, got3).start()
 
     def project_grads():
-        for c in range(1, chunks):
+        for c in range(chunks):
             turn(c)
         nin_back.wait()
-        weight_grad(nin, [(q, hid, 0, 0), (k, hid, local, 0), (v, hid, 2 * local, 0)])
-        send(attn_first, 0)
-        send(attn_first + 1, 0)
+        weight_grad(nin, [(ref, hid, i * local, WAYS[attn_first + i]) for i, ref in enumerate((q, k, v))])
+        for u in range(attn_first, attn_first + 3):
+            send(u, 0)
 
     def out_grad():
-        weight_grad(gattn, [(att, hid, 3 * local, table[attn_first + 2][3])])
-        send(attn_first + 2, 0)
+        weight_grad(gattn, [(att, hid, 3 * local, WAYS[attn_first + 3])])
+        send(attn_first + 3, 0)
 
     def norm_grads():
         tokens_back.wait()
@@ -631,18 +650,18 @@
     early = set(SLOTS) | {(u, 0) for u in range(count)}
     plan = PLAN
     if levels != 4:
-        plan = [0, "project", 1, "out", 2, 3, "norm"] + [x for x in everything if x not in early]
+        plan = [("part", 0, 1), "project", "out", ("part", 1, chunks - 1), "norm"] + [x for x in everything if x not in early]
         plan += [("grad", c) for c in range(chunks)]
-    assert sorted(x for x in plan if isinstance(x, tuple) and x[0] != "grad") == sorted(set(everything) - early)
+    assert sorted(x for x in plan if not isinstance(x[0], str)) == sorted(set(everything) - early)
     for item in plan:
-        if isinstance(item, int):
-            input_part(item)
-        elif item == "project":
+        if item == "project":
             project_grads()
         elif item == "out":
             out_grad()
         elif item == "norm":
             norm_grads()
+        elif item[0] == "part":
+            input_part(*item[1:])
         elif item[0] == "grad":
             input_grad(item[1])
         else:
@@ -664,6 +683,8 @@
     lax.fori_loop(0, chunks, drain, 0)
     for side in range(2):
         wo_cross(side).wait_send()
+    for unit in range(norm_unit):
+        final_copy(unit).wait()
     for unit in range(norm_unit + 1):
         for level in range(levels):
             hop(unit, level).wait_send()
@@ -675,7 +696,7 @@
     local, inner = wq.shape[1], wu.shape[1]
     chunks = rows // CHUNK
     levels = dp_size.bit_length() - 1
-    units = 2 * (inner // 1024) + 4
+    units = 2 * (inner // 1024) + 5
     shape = jax.ShapeDtypeStruct
     anywhere = pl.BlockSpec(memory_space=pl.ANY)
     vmem = pl.BlockSpec(memory_space=pltpu.VMEM)
@@ -696,8 +717,9 @@
         pltpu.VMEM(wide, BF16), pltpu.VMEM(wide, BF16), pltpu.VMEM((CHUNK, local), BF16),
         pltpu.VMEM((local, rows), F32), pltpu.VMEM((local, rows), F32),
         pltpu.VMEM((2, CHUNK, width), BF16), pltpu.VMEM((8, 8, width), F32),
+        pltpu.VMEM((blk, inner), F32), pltpu.VMEM((blk, inner), F32), pltpu.VMEM((blk, 4 * local), F32),
         pltpu.VMEM((8 * dp_size, LANES), F32), pltpu.VMEM((8 * dp_size, LANES), F32), pltpu.VMEM((8, LANES), F32),
-        pltpu.SemaphoreType.DMA((chunks,)), pltpu.SemaphoreType.DMA((7,)), pltpu.SemaphoreType.DMA((16,)), pltpu.SemaphoreType.DMA((3,)), pltpu.SemaphoreType.DMA((2,)),
+        pltpu.SemaphoreType.DMA((units,)), pltpu.SemaphoreType.DMA((rows // PROJECT,)), pltpu.SemaphoreType.DMA((7,)), pltpu.SemaphoreType.DMA((16,)), pltpu.SemaphoreType.DMA((3,)), pltpu.SemaphoreType.DMA((2,)),
         pltpu.SemaphoreType.DMA((4 * chunks + 1,)), pltpu.SemaphoreType.DMA((4 * chunks + 1,)),
         pltpu.SemaphoreType.DMA((units * levels,)), pltpu.SemaphoreType.DMA((units * levels,)),
         pltpu.SemaphoreType.REGULAR((4 * levels + 1,)),
@@ -706,7 +728,7 @@
         functools.partial(layer_kernel, dp_size),
         out_shape=outs,
         in_specs=[pl.BlockSpec(memory_space=pltpu.SMEM)] + [anywhere] * 7 + [vmem, vmem, anywhere],
-        out_specs=[anywhere] * 3 + [vmem] * 4,
+        out_specs=[anywhere] * 6 + [vmem],
         scratch_shapes=scratch,
         compiler_params=pltpu.CompilerParams(
             collective_id=0, has_side_effects=True, vmem_limit_bytes=VMEM_BYTES

time: 194 us -> 187 us (0.964)
  Pallas kernels: 192 us -> 186 us
    pallas_call x1, Pallas kernels: 187 us -> 181 us  [run_layer(): pl.pallas_call(functools.partial(layer_kernel, dp_size), out_shape=outs,...]
where the time goes in v6:
time: 187 us
  Pallas kernels  186 us (99%)
    pallas_call x1, Pallas kernels, run_layer(): pl.pallas_call(functools.partial(layer_kernel, dp_size), out_shape=outs,...  181 us
    pallas_call x1, Pallas kernels, on_device(): pl.pallas_call(finish_kernel, grid=(steps,), out_shape=[shape(result.shap...  4.98 us

profile of v6, /device:TPU:0, one launch (start us, length us, event | category | flops | bytes accessed | tf_op | source)
XLA Modules:
  0.0 187.1 jit_solution(3836902694768594543)
XLA Ops:
  1.3 180.7 %layer.1 = (bf16[1024,1024]{1,0:T(8,128)(2,1)}, bf16[1024,1024]{1,0:T(8,128)(2,1)}, bf16[1024,1024]{1,0:T(8,128)(2,1)}, f32[64,2048]{1,0:T(8,128)}, f32[64,2048]...) custom-call(s32[1]{0:T(128)S(6)} %copy.21.length_ref, bf16[1024,1024]{1,0:T(8,128)(2,1)} %tokens_hbm.1, ...), custom_call_target="tpu_custom_call" | custom-call | tf_op jit(solution)/shard_map/layer/pallas_call | solution.py:727
  182.0 5.0 %finish.1 = (bf16[1024,1024]{1,0:T(8,128)(2,1)}, bf16[1024,1024]{1,0:T(8,128)(2,1)}, f32[64,512]{1,0:T(8,128)}, f32[64,512]{1,0:T(8,128)}, f32[64,512]{1,0:T(8,1...) custom-call(bf16[1024,1024]{1,0:T(8,128)(2,1)} %get-tuple-element.26, ...), custom_call_target="tpu_custom_call" | custom-call | tf_op jit(solution)/shard_map/finish/pallas_call | solution.py:771

commit v7 on v6

--- a/solution.py
+++ b/solution.py
@@ -23,7 +23,7 @@
 ROOT = 0.7978845608028654
 CUBE = 0.044715
 UNROLL = 2
-VMEM_BYTES = 61 * 1024 * 1024
+VMEM_BYTES = 127 * 512 * 1024
 WAYS = (0, 0, 1, 0, 0, 0, 0, 0)
 SLOTS = {(2, 0): 1, (3, 0): 1, (0, 1): 4, (2, 1): 5, (0, 2): 7, (1, 1): 7}
 PLAN = [
@@ -86,11 +86,11 @@
 def layer_kernel(
     dp_size,
     length_ref, tokens_hbm, wq_hbm, wk_hbm, wv_hbm, wo_hbm, wu_hbm, wd_hbm, gain_ref, bias_ref, cot_hbm,
-    result_hbm, ingrad_hbm, nin_hbm, up_hbm, down_hbm, attn_hbm, norm_ref,
+    result_ref, ingrad_ref, nin_hbm, up_ref, down_ref, attn_ref, norm_ref,
     tokens, wq, wk, wv, wo, wu, wd, cot,
     nin, q, k, v, att, lse, attn_total, own2, got2, got3, middle, hid, slope, gffn, gattn, gatt, gk, gv,
-    stage, acc, up_ref, down_ref, attn_ref, norm_held, norm_box, norm_peer,
-    final_sem, token_sem, load_sem, wo_sem, save_sem, stage_sem, send_sem, recv_sem, give_sem, take_sem, free_sem,
+    acc, norm_held, norm_box, norm_peer,
+    token_sem, load_sem, wo_sem, save_sem, send_sem, recv_sem, give_sem, take_sem, free_sem,
 ):
     rows = tokens.shape[0]
     chunks = rows // CHUNK
@@ -194,13 +194,6 @@
     norm_unit = len(table)
     table.append((norm_held, norm_ref, None, 0))
 
-    outputs = [cols_at(down_hbm, u * wide, wide) for u in range(count)]
-    outputs += [cols_at(up_hbm, u * wide, wide) for u in range(count)]
-    outputs += [cols_at(attn_hbm, i * local, local) for i in range(4)]
-
-    def final_copy(unit):
-        return pltpu.make_async_copy(table[unit][1], outputs[unit], final_sem.at[unit])
-
     def held(unit):
         return table[unit][0]
 
@@ -270,8 +263,6 @@
             return carry
 
         lax.fori_loop(0, size // step_rows, add, 0)
-        if last and unit != norm_unit:
-            final_copy(unit).start()
         if unit == 2 * count - 1 and level == 0:
             for other in range(2, levels):
                 release(range(2 * count), other)
@@ -442,23 +433,14 @@
     lax.fori_loop(0, chunks, feed, 0)
     loads[6].wait()
 
-    def result_copy(c):
-        slot = lax.rem(c, 2)
-        return pltpu.make_async_copy(stage.at[slot], result_hbm.at[rows_of(c)], stage_sem.at[slot])
-
     def feed_back(c, carry):
         at = rows_of(c)
-        slot = lax.rem(c, 2)
         exchange(1, c, own2, got2).wait_recv()
-
-        @pl.when(c >= 2)
-        def _():
-            result_copy(c - 2).wait()
 
         def norms(start, at):
             hat, scale = normalize(own2[at, :].astype(F32) + got2[at, :].astype(F32))
             out = middle[at, :] + (hat * gain(3) + bias(3))
-            stage[slot, pl.ds(pl.multiple_of(start - c * CHUNK, BLOCK), BLOCK), :] = out.astype(BF16)
+            result_ref[at, :] = out.astype(BF16)
             grad = cot[at, :].astype(F32) * real_rows(start)
             gffn[at, :] = norm_pull(hat, scale, gain(3), grad).astype(BF16)
             acc[2] += fold_rows(grad * hat)
@@ -468,7 +450,6 @@
             lse[at, :] = jnp.where(lane_index((BLOCK, LANES)) == 2 * pairs + 1, scale, lse[at, :])
 
         blocks(c, norms)
-        result_copy(c).start()
         grad = gffn[at, :]
         span = 512
         for n in range(inner // span):
@@ -619,24 +600,17 @@
             norm_held[spot : spot + 8, :] = piece
         send(norm_unit, 0)
 
-    def grad_copy(c):
-        slot = lax.rem(c, 2)
-        return pltpu.make_async_copy(stage.at[slot], ingrad_hbm.at[rows_of(c)], stage_sem.at[slot])
-
     def input_grad(c):
         at = rows_of(c)
-        slot = c % 2
         exchange(3, c, own2, got3).wait_recv()
-        (result_copy if c < 2 else grad_copy)(chunks - 2 + c if c < 2 else c - 2).wait()
 
         def norms(start, at):
             grad = own2[at, :].astype(F32) + got3[at, :].astype(F32)
             hat, scale = normalize(back[at, :].astype(F32))
             total = middle[at, :] + norm_pull(hat, scale, gain(0), grad)
-            stage[slot, pl.ds(pl.multiple_of(start - c * CHUNK, BLOCK), BLOCK), :] = total.astype(BF16)
+            ingrad_ref[at, :] = total.astype(BF16)
 
         blocks(c, norms)
-        grad_copy(c).start()
 
     tell = pltpu.make_async_remote_copy(
         src_ref=norm_ref,
@@ -672,9 +646,6 @@
     row = lax.broadcasted_iota(jnp.int32, norm_ref.shape, 0)
     norm_ref[...] += jnp.where(lax.rem(row, 4) == 0, norm_peer[...], 0.0)
 
-    for c in range(max(chunks - 2, 0), chunks):
-        grad_copy(c).wait()
-
     def drain(c, carry):
         exchange(0, c, att, att_peer).wait_send()
         exchange(3, c, own2, got3).wait_send()
@@ -683,8 +654,6 @@
     lax.fori_loop(0, chunks, drain, 0)
     for side in range(2):
         wo_cross(side).wait_send()
-    for unit in range(norm_unit):
-        final_copy(unit).wait()
     for unit in range(norm_unit + 1):
         for level in range(levels):
             hop(unit, level).wait_send()
@@ -704,8 +673,9 @@
     thin = (rows, local)
     blk = width // dp_size
     outs = [
-        shape(wide, BF16), shape(wide, BF16), shape(wide, BF16),
-        shape((blk, inner), F32), shape((blk, inner), F32), shape((blk, 4 * local), F32), shape((8, LANES), F32),
+        pltpu.VMEM(wide, BF16), pltpu.VMEM(wide, BF16), shape(wide, BF16),
+        pltpu.VMEM((blk, inner), F32), pltpu.VMEM((blk, inner), F32), pltpu.VMEM((blk, 4 * local), F32),
+        pltpu.VMEM((8, LANES), F32),
     ]
     scratch = [
         pltpu.VMEM(wide, BF16), pltpu.VMEM(wq.shape, BF16), pltpu.VMEM(wk.shape, BF16), pltpu.VMEM(wv.shape, BF16),
@@ -716,10 +686,9 @@
         pltpu.VMEM(wide, F32), pltpu.VMEM((rows, inner), BF16), pltpu.VMEM((rows, inner), BF16),
         pltpu.VMEM(wide, BF16), pltpu.VMEM(wide, BF16), pltpu.VMEM((CHUNK, local), BF16),
         pltpu.VMEM((local, rows), F32), pltpu.VMEM((local, rows), F32),
-        pltpu.VMEM((2, CHUNK, width), BF16), pltpu.VMEM((8, 8, width), F32),
-        pltpu.VMEM((blk, inner), F32), pltpu.VMEM((blk, inner), F32), pltpu.VMEM((blk, 4 * local), F32),
+        pltpu.VMEM((8, 8, width), F32),
         pltpu.VMEM((8 * dp_size, LANES), F32), pltpu.VMEM((8 * dp_size, LANES), F32), pltpu.VMEM((8, LANES), F32),
-        pltpu.SemaphoreType.DMA((units,)), pltpu.SemaphoreType.DMA((rows // PROJECT,)), pltpu.SemaphoreType.DMA((7,)), pltpu.SemaphoreType.DMA((16,)), pltpu.SemaphoreType.DMA((3,)), pltpu.SemaphoreType.DMA((2,)),
+        pltpu.SemaphoreType.DMA((rows // PROJECT,)), pltpu.SemaphoreType.DMA((7,)), pltpu.SemaphoreType.DMA((16,)), pltpu.SemaphoreType.DMA((3,)),
         pltpu.SemaphoreType.DMA((4 * chunks + 1,)), pltpu.SemaphoreType.DMA((4 * chunks + 1,)),
         pltpu.SemaphoreType.DMA((units * levels,)), pltpu.SemaphoreType.DMA((units * levels,)),
         pltpu.SemaphoreType.REGULAR((4 * levels + 1,)),
@@ -728,28 +697,29 @@
         functools.partial(layer_kernel, dp_size),
         out_shape=outs,
         in_specs=[pl.BlockSpec(memory_space=pltpu.SMEM)] + [anywhere] * 7 + [vmem, vmem, anywhere],
-        out_specs=[anywhere] * 6 + [vmem],
+        out_specs=[vmem, vmem, anywhere] + [vmem] * 4,
         scratch_shapes=scratch,
         compiler_params=pltpu.CompilerParams(
-            collective_id=0, has_side_effects=True, vmem_limit_bytes=VMEM_BYTES
+            collective_id=0, has_side_effects=True, vmem_limit_bytes=VMEM_BYTES - 4 * rows * width - 8 * blk * (inner + 2 * local)
         ),
         name="layer",
     )(lengths, tokens, wq, wk, wv, wo, wu, wd, gains, biases, cot)
 
 
 def finish_kernel(
-    result_in, ingrad_in, up_in, down_in, attn_in, norm_in, result, ingrad, query, key, value, out, up, down, gain, bias
+    result_in, ingrad_in, up_in, down_in, attn_in, norm_in, result, ingrad, query, key, value, out, up, down, gain, bias, sem
 ):
     local = query.shape[1]
-    result[...] = result_in[...]
-    ingrad[...] = ingrad_in[...]
-    up[...] = up_in[...]
-    down[...] = down_in[...]
-    for i, ref in enumerate((query, key, value, out)):
-        ref[...] = attn_in[:, i * local : (i + 1) * local]
+    pairs = [(result_in, result), (ingrad_in, ingrad), (up_in, up), (down_in, down)]
+    pairs += [(attn_in.at[:, pl.ds(i * local, local)], ref) for i, ref in enumerate((query, key, value, out))]
+    copies = [pltpu.make_async_copy(source, target, sem.at[i]) for i, (source, target) in enumerate(pairs)]
+    for copy in copies:
+        copy.start()
     blk = gain.shape[1]
     gain[...] = norm_in[:4, :blk]
     bias[...] = norm_in[4:, :blk]
+    for copy in copies:
+        copy.wait()
 
 
 def on_device(tokens, lengths, wq, wk, wv, wo, wu, wd, gains, biases, cot):
@@ -759,25 +729,18 @@
     )
     blk = up.shape[0]
     shape = jax.ShapeDtypeStruct
-    steps = 2 if blk % 16 == 0 else 1
-
-    def part(rows, columns):
-        return pl.BlockSpec((rows // steps, columns), lambda i: (i, 0))
-
-    def whole(*dims):
-        return pl.BlockSpec(dims, lambda i: (0, 0))
-
-    rows, width = result.shape
+    anywhere = pl.BlockSpec(memory_space=pl.ANY)
+    vmem = pl.BlockSpec(memory_space=pltpu.VMEM)
     result, input_grad, query, key, value, out, up, down, gain, bias = pl.pallas_call(
         finish_kernel,
-        grid=(steps,),
         out_shape=[shape(result.shape, BF16), shape(result.shape, BF16)]
         + [shape((blk, local), F32)] * 4
         + [shape((blk, inner), F32)] * 2
         + [shape((4, blk), F32)] * 2,
-        in_specs=[part(rows, width)] * 2 + [part(blk, inner)] * 2 + [part(blk, 4 * local), whole(8, LANES)],
-        out_specs=[part(rows, width)] * 2 + [part(blk, local)] * 4 + [part(blk, inner)] * 2 + [whole(4, blk)] * 2,
-        compiler_params=pltpu.CompilerParams(vmem_limit_bytes=VMEM_BYTES),
+        in_specs=[vmem] * 6,
+        out_specs=[anywhere] * 8 + [vmem] * 2,
+        scratch_shapes=[pltpu.SemaphoreType.DMA((8,))],
+        compiler_params=pltpu.CompilerParams(vmem_limit_bytes=4 * 1024 * 1024),
         name="finish",
     )(result, input_grad, up, down, attn, norms)
     return result, input_grad, query, key, value, out.T, up, down.T, gain, bias

time: 187 us -> 184 us (0.984)
  Pallas kernels: 186 us -> 182 us
where the time goes in v7:
time: 184 us
  Pallas kernels  182 us (99%)
    pallas_call x1, Pallas kernels, run_layer(): pl.pallas_call(functools.partial(layer_kernel, dp_size), out_shape=outs,...  179 us

profile of v7, /device:TPU:0, one launch (start us, length us, event | category | flops | bytes accessed | tf_op | source)
XLA Modules:
  0.0 183.9 jit_solution(11026679265239646896)
XLA Ops:
  1.3 179.3 %layer.1 = (bf16[1024,1024]{1,0:T(8,128)(2,1)S(1)}, bf16[1024,1024]{1,0:T(8,128)(2,1)S(1)}, bf16[1024,1024]{1,0:T(8,128)(2,1)}, f32[64,2048]{1,0:T(8,128)S(1)}, ...) custom-call(s32[1]{0:T(128)S(6)} %copy.21.length_ref, bf16[1024,1024]{1,0:T(8,128)(2,1)} %tokens_hbm.1, ...), custom_call_target="tpu_custom_call" | custom-call | tf_op jit(solution)/shard_map/layer/pallas_call | solution.py:696
  180.6 3.1 %finish.1 = (bf16[1024,1024]{1,0:T(8,128)(2,1)}, bf16[1024,1024]{1,0:T(8,128)(2,1)}, f32[64,512]{1,0:T(8,128)}, f32[64,512]{1,0:T(8,128)}, f32[64,512]{1,0:T(8,1...) custom-call(bf16[1024,1024]{1,0:T(8,128)(2,1)S(1)} %get-tuple-elemen, ...), custom_call_target="tpu_custom_call" | custom-call | tf_op jit(solution)/shard_map/finish/pallas_call | solution.py:734

commit v8 on v7

--- a/solution.py
+++ b/solution.py
@@ -88,7 +88,7 @@
     length_ref, tokens_hbm, wq_hbm, wk_hbm, wv_hbm, wo_hbm, wu_hbm, wd_hbm, gain_ref, bias_ref, cot_hbm,
     result_ref, ingrad_ref, nin_hbm, up_ref, down_ref, attn_ref, norm_ref,
     tokens, wq, wk, wv, wo, wu, wd, cot,
-    nin, q, k, v, att, lse, attn_total, own2, got2, got3, middle, hid, slope, gffn, gattn, gatt, gk, gv,
+    nin, q, k, v, att, lse, attn_total, own2, got2, got3, middle, hid, slope, gffn, gattn, gatt, gk, gv, ahead,
     acc, norm_held, norm_box, norm_peer,
     token_sem, load_sem, wo_sem, save_sem, send_sem, recv_sem, give_sem, take_sem, free_sem,
 ):
@@ -326,22 +326,30 @@
         hat, _ = normalize(tokens[at, :].astype(F32))
         nin[at, :] = (hat * gain(0) + bias(0)).astype(BF16)
 
-    for c in range(rows // PROJECT):
+    spans = rows // PROJECT
+    for c in range(spans // 2):
         token_load(c).wait()
         blocks(c, norm_in, PROJECT)
+        if c == 0:
+            pl.semaphore_wait(barrier, levels + 1)
+            for side in range(2):
+                wo_cross(side).start()
+    for c in range(spans // 2, spans):
+        token_load(c).wait()
     for copy in loads[3:]:
         copy.start()
-    pl.semaphore_wait(barrier, levels + 1)
-    for side in range(2):
-        wo_cross(side).start()
     for copy in loads[:3]:
         copy.wait()
-    query_rows(span_of(0))
-    for c in range(rows // (2 * PROJECT)):
-        at = pl.ds(2 * PROJECT * c, 2 * PROJECT)
+    for h in range(2):
+        at = pl.ds(h * rows // 2, rows // 2)
         normed = nin[at, :]
         k[at, :] = dot(normed, wk[...], NN).astype(BF16)
         v[at, :] = dot(normed, wv[...], NN).astype(BF16)
+        if h == 0:
+            for b in range(rows // 2 // BLOCK):
+                start = rows // 2 + b * BLOCK
+                norm_in(start, pl.ds(start, BLOCK))
+    query_rows(span_of(0))
     save(0, nin, nin_hbm).start()
 
     key_bias = jnp.where(lane_index((1, rows)) < length, 0.0, NEG)
@@ -492,6 +500,11 @@
 
     def attend_back(c, carry):
         at = rows_of(c)
+
+        @pl.when(c == chunks - 1)
+        def _():
+            ahead[...] = dot(q[:CHUNK, :], wq[...], NT)
+
         exchange(2, c, own2, got3).wait_recv()
 
         def norms(start, at):
@@ -559,7 +572,7 @@
         for c in range(first, first + number):
             turn(c)
             exchange(2, c, own2, got3).wait_send()
-        part = dot(q[at, :], wq[...], NT) + dot(k[at, :], wk[...], NT) + dot(v[at, :], wv[...], NT)
+        part = (ahead[...] if first == 0 else dot(q[at, :], wq[...], NT)) + dot(k[at, :], wk[...], NT) + dot(v[at, :], wv[...], NT)
         own2[at, :] = part.astype(BF16)
         for c in range(first, first + number):
             exchange(3, c, own2, got3).start()
@@ -627,6 +640,16 @@
         plan = [("part", 0, 1), "project", "out", ("part", 1, chunks - 1), "norm"] + [x for x in everything if x not in early]
         plan += [("grad", c) for c in range(chunks)]
     assert sorted(x for x in plan if not isinstance(x[0], str)) == sorted(set(everything) - early)
+    def finished(level):
+        for u in range(norm_unit + 1):
+            if level < levels - 1 or u != norm_unit - 1:
+                hop(u, level).wait_send()
+
+    if levels == 4:
+        for level, spot in ((3, ("grad", chunks - 1)), (2, (7, 3)), (1, (7, 2)), (0, ("grad", 3))):
+            plan = plan[: plan.index(spot)] + [("done", level)] + plan[plan.index(spot) :]
+    else:
+        plan = plan + [("done", level) for level in range(levels)]
     for item in plan:
         if item == "project":
             project_grads()
@@ -634,6 +657,8 @@
             out_grad()
         elif item == "norm":
             norm_grads()
+        elif item[0] == "done":
+            finished(item[1])
         elif item[0] == "part":
             input_part(*item[1:])
         elif item[0] == "grad":
@@ -654,9 +679,7 @@
     lax.fori_loop(0, chunks, drain, 0)
     for side in range(2):
         wo_cross(side).wait_send()
-    for unit in range(norm_unit + 1):
-        for level in range(levels):
-            hop(unit, level).wait_send()
+    hop(norm_unit - 1, levels - 1).wait_send()
 
 
 def run_layer(lengths, tokens, wq, wk, wv, wo, wu, wd, gains, biases, cot):
@@ -685,7 +708,7 @@
         pltpu.VMEM(wide, F32), pltpu.VMEM(wide, BF16), pltpu.VMEM(wide, BF16), pltpu.VMEM(wide, BF16),
         pltpu.VMEM(wide, F32), pltpu.VMEM((rows, inner), BF16), pltpu.VMEM((rows, inner), BF16),
         pltpu.VMEM(wide, BF16), pltpu.VMEM(wide, BF16), pltpu.VMEM((CHUNK, local), BF16),
-        pltpu.VMEM((local, rows), F32), pltpu.VMEM((local, rows), F32),
+        pltpu.VMEM((local, rows), F32), pltpu.VMEM((local, rows), F32), pltpu.VMEM((CHUNK, width), F32),
         pltpu.VMEM((8, 8, width), F32),
         pltpu.VMEM((8 * dp_size, LANES), F32), pltpu.VMEM((8 * dp_size, LANES), F32), pltpu.VMEM((8, LANES), F32),
         pltpu.SemaphoreType.DMA((rows // PROJECT,)), pltpu.SemaphoreType.DMA((7,)), pltpu.SemaphoreType.DMA((16,)), pltpu.SemaphoreType.DMA((3,)),

time: 184 us -> 183 us (level)
  no operation moved by 1% of the time
where the time goes in v8:
time: 183 us
  Pallas kernels  181 us (99%)
    pallas_call x1, Pallas kernels, run_layer(): pl.pallas_call(functools.partial(layer_kernel, dp_size), out_shape=outs,...  178 us

profile of v8, /device:TPU:0, one launch (start us, length us, event | category | flops | bytes accessed | tf_op | source)
XLA Modules:
  0.0 182.6 jit_solution(17301605111796059673)
XLA Ops:
  1.3 178.1 %layer.1 = (bf16[1024,1024]{1,0:T(8,128)(2,1)S(1)}, bf16[1024,1024]{1,0:T(8,128)(2,1)S(1)}, bf16[1024,1024]{1,0:T(8,128)(2,1)}, f32[64,2048]{1,0:T(8,128)S(1)}, ...) custom-call(s32[1]{0:T(128)S(6)} %copy.21.length_ref, bf16[1024,1024]{1,0:T(8,128)(2,1)} %tokens_hbm.1, ...), custom_call_target="tpu_custom_call" | custom-call | tf_op jit(solution)/shard_map/layer/pallas_call | solution.py:719
  179.4 3.1 %finish.1 = (bf16[1024,1024]{1,0:T(8,128)(2,1)}, bf16[1024,1024]{1,0:T(8,128)(2,1)}, f32[64,512]{1,0:T(8,128)}, f32[64,512]{1,0:T(8,128)}, f32[64,512]{1,0:T(8,1...) custom-call(bf16[1024,1024]{1,0:T(8,128)(2,1)S(1)} %get-tuple-elemen, ...), custom_call_target="tpu_custom_call" | custom-call | tf_op jit(solution)/shard_map/finish/pallas_call | solution.py:757

commit v9 on v8

--- a/solution.py
+++ b/solution.py
@@ -23,14 +23,14 @@
 ROOT = 0.7978845608028654
 CUBE = 0.044715
 UNROLL = 2
-VMEM_BYTES = 127 * 512 * 1024
+VMEM_BYTES = 255 * 256 * 1024
 WAYS = (0, 0, 1, 0, 0, 0, 0, 0)
-SLOTS = {(2, 0): 1, (3, 0): 1, (0, 1): 4, (2, 1): 5, (0, 2): 7, (1, 1): 7}
+SLOTS = {(2, 0): 1, (3, 0): 2, (0, 1): 4, (2, 1): 5, (1, 1): 7, (0, 2): 7}
 PLAN = [
-    ("part", 0, 1), ("part", 1, 1), (3, 1), "project", (2, 2), ("part", 2, 2), "out", (4, 0), (5, 0), (1, 2), (0, 3),
-    ("part", 4, 2), ("part", 6, 2), "norm", (6, 0), (8, 0), (7, 0), (3, 2), (2, 3), ("grad", 0), ("grad", 1), (4, 1),
-    (1, 3), ("grad", 2), (5, 1), (8, 1), (4, 2), (8, 2), (3, 3), ("grad", 3), (5, 2), (6, 1), (8, 3), (4, 3), ("grad", 4),
-    (5, 3), (7, 1), (6, 2), ("grad", 5), (7, 2), (6, 3), ("grad", 6), (7, 3), ("grad", 7),
+    ("part", 1, 1), "query", (3, 1), ("part", 2, 2), (4, 0), "keyvalue", (2, 2), "out", (5, 0), (1, 2), (0, 3), (6, 0), ("part", 4, 2),
+    (7, 0), ("part", 6, 2), "norm", (3, 2), (8, 0), (2, 3), ("grad", 0), ("grad", 1), (4, 1), ("grad", 2), (1, 3), (8, 1), (5, 1), (4, 2),
+    (3, 3), (8, 2), ("grad", 3), (6, 1), (5, 2), (4, 3), ("grad", 4), (7, 1), (6, 2), (8, 3), (5, 3), ("grad", 5), (7, 2), (6, 3),
+    ("grad", 6), (7, 3), ("grad", 7),
 ]
 
 
@@ -88,7 +88,7 @@
     length_ref, tokens_hbm, wq_hbm, wk_hbm, wv_hbm, wo_hbm, wu_hbm, wd_hbm, gain_ref, bias_ref, cot_hbm,
     result_ref, ingrad_ref, nin_hbm, up_ref, down_ref, attn_ref, norm_ref,
     tokens, wq, wk, wv, wo, wu, wd, cot,
-    nin, q, k, v, att, lse, attn_total, own2, got2, got3, middle, hid, slope, gffn, gattn, gatt, gk, gv, ahead,
+    nin, q, k, v, att, lse, attn_total, own2, got2, got3, middle, hid, slope, gffn, gattn, gk, gv,
     acc, norm_held, norm_box, norm_peer,
     token_sem, load_sem, wo_sem, save_sem, send_sem, recv_sem, give_sem, take_sem, free_sem,
 ):
@@ -192,7 +192,7 @@
         cols = pl.ds(i * local, local)
         table.append((hid.at[:, cols], attn_ref.at[:, cols], cols, WAYS[attn_first + i]))
     norm_unit = len(table)
-    table.append((norm_held, norm_ref, None, 0))
+    table.append((norm_held, norm_ref, None, 1))
 
     def held(unit):
         return table[unit][0]
@@ -498,12 +498,21 @@
 
     tokens_back = pltpu.make_async_copy(tokens_hbm, got2, save_sem.at[2])
 
+    gatt = hid.at[pl.ds(0, CHUNK), pl.ds(0, local)]
+
     def attend_back(c, carry):
         at = rows_of(c)
 
         @pl.when(c == chunks - 1)
         def _():
-            ahead[...] = dot(q[:CHUNK, :], wq[...], NT)
+            attn_total[:CHUNK, :] = dot(q[:CHUNK, :], wq[...], NT)
+
+        for slot, work in agenda.items():
+
+            @pl.when(c == slot)
+            def _(work=work):
+                for unit, level in work:
+                    take(unit, level)
 
         exchange(2, c, own2, got3).wait_recv()
 
@@ -529,33 +538,43 @@
 
         gatt[...] = dot(gattn[at, :], wo[...], NT).astype(BF16)
 
-        def pair(p):
+        def pair(p, first, last, with_queries=True):
             cols = pl.ds(p * LANES, LANES)
-            keys, values, grad = k[:, cols], v[:, cols], gatt[:, cols]
+            span = slice(0, last)
+            keys, values, grad = k[span, cols], v[span, cols], gatt[:, cols]
             query, grads = stack_pair(q[at, cols]), stack_pair(grad)
             through = stack_pair(grad.astype(F32) * att[at, cols].astype(F32))
             shift = jnp.sum(through, axis=1, keepdims=True)
             logs = lse[at, :]
             log = jnp.concatenate([logs[:, 2 * p : 2 * p + 1], logs[:, 2 * p + 1 : 2 * p + 2]], axis=0)
-            weights = jnp.exp(dot(query, keys, NT) + key_bias - log)
+            weights = jnp.exp(dot(query, keys, NT) + key_bias[:, span] - log)
             slopes = (weights * (dot(grads, values, NT) - shift)).astype(BF16)
-            q[at, cols] = (join_pair(dot(slopes, keys, NN)) * 0.125).astype(BF16)
-            gk[cols, :] += dot(query, slopes, TN)
-            gv[cols, :] += dot(grads, weights.astype(BF16), TN)
-
-        for slot, work in agenda.items():
-
-            @pl.when(c == slot)
-            def _(work=work):
-                for unit, level in work:
-                    take(unit, level)
-
-        for p in range(pairs):
-            pair(p)
+            if with_queries:
+                q[at, cols] = (join_pair(dot(slopes, keys, NN)) * 0.125).astype(BF16)
+            gk[cols, first:last] += dot(query, slopes[:, first:], TN)
+            gv[cols, first:last] += dot(grads, weights.astype(BF16)[:, first:], TN)
+
+        @pl.when(c < chunks - 1)
+        def _():
+            for p in range(pairs):
+                pair(p, 0, rows)
+
+        @pl.when(c == chunks - 1)
+        def _():
+            for p in range(pairs):
+                pair(p, 0, CHUNK, False)
+            pl.semaphore_wait(free_sem.at[4 * levels], 1)
+            exchange(2, 0, own2, got3).wait_send()
+            part = attn_total[:CHUNK, :] + dot(gk[:, :CHUNK].astype(BF16).T, wk[...], NT)
+            part = part + dot(gv[:, :CHUNK].astype(BF16).T, wv[...], NT)
+            own2[:CHUNK, :] = part.astype(BF16)
+            exchange(3, 0, own2, got3).start()
+            for p in range(pairs):
+                pair(p, CHUNK, rows)
+
         return carry
 
     lax.fori_loop(0, chunks, attend_back, 0)
-    pl.semaphore_wait(free_sem.at[4 * levels], 1)
     back = got2
 
     turned = set()
@@ -572,18 +591,20 @@
         for c in range(first, first + number):
             turn(c)
             exchange(2, c, own2, got3).wait_send()
-        part = (ahead[...] if first == 0 else dot(q[at, :], wq[...], NT)) + dot(k[at, :], wk[...], NT) + dot(v[at, :], wv[...], NT)
+        part = dot(q[at, :], wq[...], NT) + dot(k[at, :], wk[...], NT) + dot(v[at, :], wv[...], NT)
         own2[at, :] = part.astype(BF16)
         for c in range(first, first + number):
             exchange(3, c, own2, got3).start()
 
-    def project_grads():
+    def project_grads(which):
         for c in range(chunks):
             turn(c)
-        nin_back.wait()
-        weight_grad(nin, [(ref, hid, i * local, WAYS[attn_first + i]) for i, ref in enumerate((q, k, v))])
-        for u in range(attn_first, attn_first + 3):
-            send(u, 0)
+        if 0 in which:
+            nin_back.wait()
+        sources = (q, k, v)
+        weight_grad(nin, [(sources[i], hid, i * local, WAYS[attn_first + i]) for i in which])
+        for i in which:
+            send(attn_first + i, 0)
 
     def out_grad():
         weight_grad(gattn, [(att, hid, 3 * local, WAYS[attn_first + 3])])
@@ -609,7 +630,7 @@
             piece = sums[:, tile * LANES : (tile + 1) * LANES]
             if shift:
                 piece = pltpu.roll(piece, LANES - shift, 1)
-            spot = 8 * fixed_position(index, 0)
+            spot = 8 * fixed_position(index, 1)
             norm_held[spot : spot + 8, :] = piece
         send(norm_unit, 0)
 
@@ -637,7 +658,7 @@
     early = set(SLOTS) | {(u, 0) for u in range(count)}
     plan = PLAN
     if levels != 4:
-        plan = [("part", 0, 1), "project", "out", ("part", 1, chunks - 1), "norm"] + [x for x in everything if x not in early]
+        plan = [("part", 1, chunks - 1), "query", "keyvalue", "out", "norm"] + [x for x in everything if x not in early]
         plan += [("grad", c) for c in range(chunks)]
     assert sorted(x for x in plan if not isinstance(x[0], str)) == sorted(set(everything) - early)
     def finished(level):
@@ -651,8 +672,10 @@
     else:
         plan = plan + [("done", level) for level in range(levels)]
     for item in plan:
-        if item == "project":
-            project_grads()
+        if item == "query":
+            project_grads((0,))
+        elif item == "keyvalue":
+            project_grads((1, 2))
         elif item == "out":
             out_grad()
         elif item == "norm":
@@ -707,8 +730,8 @@
         pltpu.VMEM(thin, BF16), pltpu.VMEM((rows, LANES), F32),
         pltpu.VMEM(wide, F32), pltpu.VMEM(wide, BF16), pltpu.VMEM(wide, BF16), pltpu.VMEM(wide, BF16),
         pltpu.VMEM(wide, F32), pltpu.VMEM((rows, inner), BF16), pltpu.VMEM((rows, inner), BF16),
-        pltpu.VMEM(wide, BF16), pltpu.VMEM(wide, BF16), pltpu.VMEM((CHUNK, local), BF16),
-        pltpu.VMEM((local, rows), F32), pltpu.VMEM((local, rows), F32), pltpu.VMEM((CHUNK, width), F32),
+        pltpu.VMEM(wide, BF16), pltpu.VMEM(wide, BF16),
+        pltpu.VMEM((local, rows), F32), pltpu.VMEM((local, rows), F32),
         pltpu.VMEM((8, 8, width), F32),
         pltpu.VMEM((8 * dp_size, LANES), F32), pltpu.VMEM((8 * dp_size, LANES), F32), pltpu.VMEM((8, LANES), F32),
         pltpu.SemaphoreType.DMA((rows // PROJECT,)), pltpu.SemaphoreType.DMA((7,)), pltpu.SemaphoreType.DMA((16,)), pltpu.SemaphoreType.DMA((3,)),

time: 183 us -> 182 us (level)
  no operation moved by 1% of the time
where the time goes in v9:
time: 182 us
  Pallas kernels  180 us (99%)
    pallas_call x1, Pallas kernels, run_layer(): pl.pallas_call(functools.partial(layer_kernel, dp_size), out_shape=outs,...  177 us

profile of v9, /device:TPU:0, one launch (start us, length us, event | category | flops | bytes accessed | tf_op | source)
XLA Modules:
  0.0 181.9 jit_solution(789944573217398345)
XLA Ops:
  1.3 177.3 %layer.1 = (bf16[1024,1024]{1,0:T(8,128)(2,1)S(1)}, bf16[1024,1024]{1,0:T(8,128)(2,1)S(1)}, bf16[1024,1024]{1,0:T(8,128)(2,1)}, f32[64,2048]{1,0:T(8,128)S(1)}, ...) custom-call(s32[1]{0:T(128)S(6)} %copy.21.length_ref, bf16[1024,1024]{1,0:T(8,128)(2,1)} %tokens_hbm.1, ...), custom_call_target="tpu_custom_call" | custom-call | tf_op jit(solution)/shard_map/layer/pallas_call | solution.py:742
  178.6 3.1 %finish.1 = (bf16[1024,1024]{1,0:T(8,128)(2,1)}, bf16[1024,1024]{1,0:T(8,128)(2,1)}, f32[64,512]{1,0:T(8,128)}, f32[64,512]{1,0:T(8,128)}, f32[64,512]{1,0:T(8,1...) custom-call(bf16[1024,1024]{1,0:T(8,128)(2,1)S(1)} %get-tuple-elemen, ...), custom_call_target="tpu_custom_call" | custom-call | tf_op jit(solution)/shard_map/finish/pallas_call | solution.py:780

commit v10 on v9

--- a/solution.py
+++ b/solution.py
@@ -24,13 +24,13 @@
 CUBE = 0.044715
 UNROLL = 2
 VMEM_BYTES = 255 * 256 * 1024
-WAYS = (0, 0, 1, 0, 0, 0, 0, 0)
+WAYS = (0, 0, 1, 0, 0, 0, 0, 1)
 SLOTS = {(2, 0): 1, (3, 0): 2, (0, 1): 4, (2, 1): 5, (1, 1): 7, (0, 2): 7}
 PLAN = [
-    ("part", 1, 1), "query", (3, 1), ("part", 2, 2), (4, 0), "keyvalue", (2, 2), "out", (5, 0), (1, 2), (0, 3), (6, 0), ("part", 4, 2),
-    (7, 0), ("part", 6, 2), "norm", (3, 2), (8, 0), (2, 3), ("grad", 0), ("grad", 1), (4, 1), ("grad", 2), (1, 3), (8, 1), (5, 1), (4, 2),
-    (3, 3), (8, 2), ("grad", 3), (6, 1), (5, 2), (4, 3), ("grad", 4), (7, 1), (6, 2), (8, 3), (5, 3), ("grad", 5), (7, 2), (6, 3),
-    ("grad", 6), (7, 3), ("grad", 7),
+    ("part", 1, 1), "query", (3, 1), ("part", 2, 2), (4, 0), "keyvalue", (2, 2), "out", (5, 0), (1, 2), (0, 3), (7, 0), ("part", 4, 2),
+    (6, 0), ("part", 6, 2), "norm", (3, 2), (8, 0), (2, 3), ("grad", 0), ("grad", 1), (4, 1), ("grad", 2), (1, 3), (5, 1), (7, 1), (8, 1),
+    ("grad", 3), (6, 1), (4, 2), (3, 3), (8, 2), (5, 2), ("grad", 4), (7, 2), (4, 3), (6, 2), (8, 3), (5, 3), ("grad", 5), (7, 3), (6, 3),
+    ("grad", 6), ("grad", 7),
 ]
 
 

time: 182 us -> 181 us (level)
  no operation moved by 1% of the time
where the time goes in v10:
time: 181 us
  Pallas kernels  179 us (99%)
    pallas_call x1, Pallas kernels, run_layer(): pl.pallas_call(functools.partial(layer_kernel, dp_size), out_shape=outs,...  176 us

profile of v10, /device:TPU:0, one launch (start us, length us, event | category | flops | bytes accessed | tf_op | source)
XLA Modules:
  0.0 180.9 jit_solution(9577256799951665308)
XLA Ops:
  1.3 176.3 %layer.1 = (bf16[1024,1024]{1,0:T(8,128)(2,1)S(1)}, bf16[1024,1024]{1,0:T(8,128)(2,1)S(1)}, bf16[1024,1024]{1,0:T(8,128)(2,1)}, f32[64,2048]{1,0:T(8,128)S(1)}, ...) custom-call(s32[1]{0:T(128)S(6)} %copy.21.length_ref, bf16[1024,1024]{1,0:T(8,128)(2,1)} %tokens_hbm.1, ...), custom_call_target="tpu_custom_call" | custom-call | tf_op jit(solution)/shard_map/layer/pallas_call | solution.py:742
  177.6 3.1 %finish.1 = (bf16[1024,1024]{1,0:T(8,128)(2,1)}, bf16[1024,1024]{1,0:T(8,128)(2,1)}, f32[64,512]{1,0:T(8,128)}, f32[64,512]{1,0:T(8,128)}, f32[64,512]{1,0:T(8,1...) custom-call(bf16[1024,1024]{1,0:T(8,128)(2,1)S(1)} %get-tuple-elemen, ...), custom_call_target="tpu_custom_call" | custom-call | tf_op jit(solution)/shard_map/finish/pallas_call | solution.py:780
